TPU v7x, 32 devices: a whole 2x2x4 slice. The times are simulated.
32 devices in a mesh: dp: 4 (over z), row: 4 (over y, core), col: 2 (over x).
Axes of the slice: x: 2, y: 2, z: 4, core: 2. Of those that a mesh axis runs over, the one named last changes fastest.
Arguments:
- tokens: bfloat16 [4096, 2048], P(('dp', 'col'), 'row'), may hold values from -6 to 6
- ln1_gain: float32 [2048], P('row'), may hold values from 0.5 to 2
- ln1_shift: float32 [2048], P('row'), may hold values from -3 to 3
- qkv_weight: bfloat16 [2048, 16, 3, 128], P('row', 'col'), may hold values from -1 to 1
- qv_bias: float32 [16, 2, 128], P('col'), may hold values from -3 to 3
- out_weight: bfloat16 [16, 128, 2048], P('col', None, 'row'), may hold values from -1.5 to 1.5
- out_bias: float32 [2048], P('row'), may hold values from -3 to 3
- ln2_gain: float32 [2048], P('row'), may hold values from 0.5 to 2
- ln2_shift: float32 [2048], P('row'), may hold values from -3 to 3
- up_weight: bfloat16 [2048, 8192], P('row', 'col'), may hold values from -1 to 1
- up_bias: float32 [8192], P('col'), may hold values from -3 to 3
- down_weight: bfloat16 [8192, 2048], P('col', 'row'), may hold values from -0.125 to 0.125
- down_bias: float32 [2048], P('row'), may hold values from -3 to 3
- span_starts: int32 [4, 2], P('dp'), may hold values from 0 to 768, as said below
- cotangent: bfloat16 [4096, 2048], P(('dp', 'col'), 'row'), may hold values from -6 to 6
Outputs:
- output: bfloat16 [4096, 2048], P(('dp', 'col'), 'row')
- tokens_grad: bfloat16 [4096, 2048], P(('dp', 'col'), 'row')
- ln1_gain_grad: float32 [2048], P('row')
- ln1_shift_grad: float32 [2048], P('row')
- qkv_weight_grad: float32 [2048, 16, 3, 128], P('row', 'col')
- qv_bias_grad: float32 [16, 2, 128], P('col')
- out_weight_grad: float32 [16, 128, 2048], P('col', None, 'row')
- out_bias_grad: float32 [2048], P('row')
- ln2_gain_grad: float32 [2048], P('row')
- ln2_shift_grad: float32 [2048], P('row')
- up_weight_grad: float32 [2048, 8192], P('row', 'col')
- up_bias_grad: float32 [8192], P('col')
- down_weight_grad: float32 [8192, 2048], P('col', 'row')
- down_bias_grad: float32 [2048], P('row')
Inputs may be any that keep to these rules, and one draw needn't show every extreme that they name: `span_starts`: each entry is a multiple of 256; the 2 entries of one sequence are distinct; row s belongs to sequence s.
All inputs are finite; a program needn't handle non-finite values.
Results may differ from a plain program's by a relative error of at most 0.015.
Values may be sent and summed in bfloat16 or wider, within the bound.
A program may use at most 192 MiB of HBM per device.

v0:
```python
import math

import jax
import jax.numpy as jnp
from jax import lax
from jax.sharding import PartitionSpec as P

D = 2048
HEAD = 128
SEQS = 1
SPAN = 256
BLOCK = 512


epsilon = 1e-05
masked_score = -1e30


def gelu_tanh(values):
    return (
        0.5
        * values
        * (1.0 + jnp.tanh(0.7978845608028654 * (values + 0.044715 * values * values * values)))
    )


def gather_columns(block_data):
    return lax.all_gather(block_data, "col", axis=0, tiled=True)


def gather_rows(block_data):
    return lax.all_gather(block_data, "row", axis=0, tiled=True)


def product(left_side, right_side, flipped):
    if flipped:
        return lax.dot_general(
            left_side, right_side, (((1,), (1,)), ((), ())), preferred_element_type=jnp.float32
        )
    return jnp.dot(left_side, right_side, preferred_element_type=jnp.float32)


def outer_sum(left_side, right_side):
    return lax.dot_general(
        left_side, right_side, (((0,), (0,)), ((), ())), preferred_element_type=jnp.float32
    )


def sum_rows(left_side, right_side, flipped):
    wide_left = lax.all_to_all(left_side, "row", split_axis=0, concat_axis=1, tiled=True)
    if flipped:
        wide_right = lax.all_gather(right_side, "row", axis=1, tiled=True)
    else:
        wide_right = lax.all_gather(right_side, "row", axis=0, tiled=True)
    return product(wide_left, wide_right, flipped)


def sum_columns(left_side, right_side, flipped):
    return lax.psum_scatter(
        product(left_side, right_side, flipped), "col", scatter_dimension=0, tiled=True
    )


def row_totals(first_sum, second_sum):
    return lax.psum((first_sum, second_sum), "row")


def norm_forward(values, gain_row, bias_row):
    totals, squares = row_totals(jnp.sum(values, axis=1), jnp.sum(values * values, axis=1))
    center = totals / D
    spread = squares / D - center * center
    inverse = lax.rsqrt(spread + epsilon)
    standard = (values - center[:, None]) * inverse[:, None]
    return (standard, inverse, (standard * gain_row + bias_row).astype(jnp.bfloat16))


def norm_backward(upstream, standard, inverse, gain_row):
    scaled = upstream * gain_row
    first_sum, second_sum = row_totals(jnp.sum(scaled, axis=1), jnp.sum(scaled * standard, axis=1))
    gradient = inverse[:, None] * (
        scaled - first_sum[:, None] / D - standard * (second_sum[:, None] / D)
    )
    return (gradient, jnp.sum(upstream * standard, axis=0), jnp.sum(upstream, axis=0))


def visible(query_pos, query_image, key_pos):
    earlier = key_pos[None, :] <= query_pos[:, None]
    same_span = (key_pos[None, :] // SPAN == query_pos[:, None] // SPAN) & (
        query_image[:, None] > 0
    )
    return earlier | same_span


def attention_forward(queries, key_value, token_image, row_offset, seq_length, block_rows):
    own_rows, head_count, width = queries.shape
    factor = 1.0 / math.sqrt(width)

    def block_forward(block_index):
        local = block_index * block_rows
        start_pos = row_offset + local
        query_block = lax.dynamic_slice_in_dim(queries, local, block_rows, 0)
        query_pos = start_pos + jnp.arange(block_rows, dtype=jnp.int32)
        query_image = lax.dynamic_slice_in_dim(token_image, start_pos, block_rows, 0)
        begin = start_pos // seq_length * seq_length // block_rows
        finish = start_pos // block_rows + 1

        def key_step(key_index, state_in):
            running, weight_sum, gathered = state_in
            key_begin = key_index * block_rows
            key_block = lax.dynamic_slice_in_dim(key_value, key_begin, block_rows, 0)
            key_pos = key_begin + jnp.arange(block_rows, dtype=jnp.int32)
            allowed = visible(query_pos, query_image, key_pos)
            scores = (
                jnp.einsum(
                    "qhd,khd->hqk",
                    query_block,
                    key_block[:, :, 0],
                    preferred_element_type=jnp.float32,
                )
                * factor
            )
            scores = jnp.where(allowed[None], scores, masked_score)
            highest = jnp.maximum(running, jnp.max(scores, axis=2))
            weights = jnp.exp(scores - highest[:, :, None])
            shrink = jnp.exp(running - highest)
            weight_sum = weight_sum * shrink + jnp.sum(weights, axis=2)
            gathered = gathered * shrink.T[:, :, None] + jnp.einsum(
                "hqk,khd->qhd",
                weights.astype(jnp.bfloat16),
                key_block[:, :, 1],
                preferred_element_type=jnp.float32,
            )
            return (highest, weight_sum, gathered)

        initial = (
            jnp.full((head_count, block_rows), masked_score, jnp.float32),
            jnp.zeros((head_count, block_rows), jnp.float32),
            jnp.zeros((block_rows, head_count, width), jnp.float32),
        )
        running, weight_sum, gathered = lax.fori_loop(begin, finish, key_step, initial)
        return (gathered / weight_sum.T[:, :, None], running + jnp.log(weight_sum))

    result, logsum = lax.map(block_forward, jnp.arange(own_rows // block_rows, dtype=jnp.int32))
    return (result.reshape(own_rows, head_count, width), logsum)


def attention_backward(
    queries,
    key_value,
    attended_full,
    logsum,
    d_attended,
    token_image,
    row_offset,
    seq_length,
    block_rows,
):
    own_rows, head_count, width = queries.shape
    factor = 1.0 / math.sqrt(width)
    row_dots = jnp.sum(d_attended.astype(jnp.float32) * attended_full, axis=2)

    def block_backward(block_index, state_out):
        d_queries, d_pairs = state_out
        local = block_index * block_rows
        start_pos = row_offset + local
        query_block = lax.dynamic_slice_in_dim(queries, local, block_rows, 0)
        dout_block = lax.dynamic_slice_in_dim(d_attended, local, block_rows, 0)
        dots_block = lax.dynamic_slice_in_dim(row_dots, local, block_rows, 0).T
        logsum_block = logsum[block_index]
        query_pos = start_pos + jnp.arange(block_rows, dtype=jnp.int32)
        query_image = lax.dynamic_slice_in_dim(token_image, start_pos, block_rows, 0)
        begin = start_pos // seq_length * seq_length // block_rows
        finish = start_pos // block_rows + 1

        def key_step(key_index, state_in):
            d_query, d_keys = state_in
            key_begin = key_index * block_rows
            key_block = lax.dynamic_slice_in_dim(key_value, key_begin, block_rows, 0)
            key_pos = key_begin + jnp.arange(block_rows, dtype=jnp.int32)
            allowed = visible(query_pos, query_image, key_pos)
            scores = (
                jnp.einsum(
                    "qhd,khd->hqk",
                    query_block,
                    key_block[:, :, 0],
                    preferred_element_type=jnp.float32,
                )
                * factor
            )
            scores = jnp.where(allowed[None], scores, masked_score)
            probabilities = jnp.exp(scores - logsum_block[:, :, None])
            d_probs = jnp.einsum(
                "qhd,khd->hqk", dout_block, key_block[:, :, 1], preferred_element_type=jnp.float32
            )
            d_scores = (probabilities * (d_probs - dots_block[:, :, None])).astype(jnp.bfloat16)
            d_query = d_query + jnp.einsum(
                "hqk,khd->qhd", d_scores, key_block[:, :, 0], preferred_element_type=jnp.float32
            )
            d_key = (
                jnp.einsum(
                    "hqk,qhd->khd", d_scores, query_block, preferred_element_type=jnp.float32
                )
                * factor
            )
            d_value = jnp.einsum(
                "hqk,qhd->khd",
                probabilities.astype(jnp.bfloat16),
                dout_block,
                preferred_element_type=jnp.float32,
            )
            previous = lax.dynamic_slice_in_dim(d_keys, key_begin, block_rows, 0)
            d_keys = lax.dynamic_update_slice_in_dim(
                d_keys, previous + jnp.stack([d_key, d_value], axis=2), key_begin, 0
            )
            return (d_query, d_keys)

        d_query, d_pairs = lax.fori_loop(
            begin,
            finish,
            key_step,
            (jnp.zeros((block_rows, head_count, width), jnp.float32), d_pairs),
        )
        d_queries = lax.dynamic_update_slice_in_dim(d_queries, d_query * factor, local, 0)
        return (d_queries, d_pairs)

    initial = (
        jnp.zeros((own_rows, head_count, width), jnp.float32),
        jnp.zeros((key_value.shape[0], head_count, 2, width), jnp.float32),
    )
    return lax.fori_loop(0, own_rows // block_rows, block_backward, initial)


def per_device(
    tokens,
    ln1_gain,
    ln1_shift,
    qkv_weight,
    qv_bias,
    out_weight,
    out_bias,
    ln2_gain,
    ln2_shift,
    up_weight,
    up_bias,
    down_weight,
    down_bias,
    span_starts,
    cotangent,
):
    col_rows, row_width = tokens.shape
    group_rows = col_rows * lax.axis_size("col")
    own_rows = group_rows // lax.axis_size("row")
    head_count = qkv_weight.shape[1]
    seq_length = group_rows // SEQS
    block_rows = BLOCK - own_rows % BLOCK
    row_offset = lax.axis_index("row") * own_rows
    slot_count = seq_length // SPAN
    image_marks = jnp.sum(
        (
            span_starts[:, :, None] // SPAN
            == jnp.arange(slot_count, dtype=jnp.int32)[None, None, :]
        ).astype(jnp.int32),
        axis=1,
    )
    token_image = jnp.broadcast_to(
        image_marks.reshape(-1)[:, None], (group_rows // SPAN, SPAN)
    ).reshape(group_rows)
    qkv_flat = qkv_weight.reshape(row_width, head_count * 3 * HEAD)
    out_flat = out_weight.reshape(head_count * HEAD, row_width)
    inputs = tokens.astype(jnp.float32)
    standard1, inverse1, normed1 = norm_forward(inputs, ln1_gain, ln1_shift)
    normed1_all = gather_columns(normed1)
    mixed_sums = sum_rows(normed1_all, qkv_flat, False).reshape(own_rows, head_count, 3, HEAD)
    queries = (mixed_sums[:, :, 0] + qv_bias[:, 0]).astype(jnp.bfloat16)
    key_value_own = jnp.stack(
        [mixed_sums[:, :, 1], mixed_sums[:, :, 2] + qv_bias[:, 1]], axis=2
    ).astype(jnp.bfloat16)
    key_value = gather_rows(key_value_own)
    attended_full, logsum = attention_forward(
        queries, key_value, token_image, row_offset, seq_length, block_rows
    )
    attended = attended_full.astype(jnp.bfloat16).reshape(own_rows, head_count * HEAD)
    attended_all = gather_rows(attended)
    residual = inputs + (sum_columns(attended_all, out_flat, False) + out_bias)
    standard2, inverse2, normed2 = norm_forward(residual, ln2_gain, ln2_shift)
    normed2_all = gather_columns(normed2)
    up_sums = sum_rows(normed2_all, up_weight, False) + up_bias
    hidden = gelu_tanh(up_sums).astype(jnp.bfloat16)
    hidden_all = gather_rows(hidden)
    output = (residual + (sum_columns(hidden_all, down_weight, False) + down_bias)).astype(
        jnp.bfloat16
    )
    d_output = cotangent.astype(jnp.float32)
    d_output_all = gather_columns(cotangent)
    down_grad = outer_sum(hidden_all, d_output_all)
    down_bias_grad = jnp.sum(d_output_all, axis=0, dtype=jnp.float32)
    d_hidden = sum_rows(d_output_all, down_weight, True)
    d_upper = jax.vjp(gelu_tanh, up_sums)[1](d_hidden)[0].astype(jnp.bfloat16)
    d_upper_all = gather_rows(d_upper)
    normed2_use = gather_columns(normed2)
    up_grad = outer_sum(normed2_use, d_upper_all)
    up_bias_grad = jnp.sum(d_upper_all, axis=0, dtype=jnp.float32)
    d_normed2 = sum_columns(d_upper_all, up_weight, True)
    d_norm2, gain2_grad, shift2_grad = norm_backward(d_normed2, standard2, inverse2, ln2_gain)
    d_residual = d_output + d_norm2
    d_branch = d_residual.astype(jnp.bfloat16)
    d_branch_all = gather_columns(d_branch)
    out_grad = outer_sum(attended_all, d_branch_all)
    out_bias_grad = jnp.sum(d_branch_all, axis=0, dtype=jnp.float32)
    d_attended = (
        sum_rows(d_branch_all, out_flat, True)
        .astype(jnp.bfloat16)
        .reshape(own_rows, head_count, HEAD)
    )
    d_queries, d_pairs = attention_backward(
        queries,
        key_value,
        attended_full,
        logsum,
        d_attended,
        token_image,
        row_offset,
        seq_length,
        block_rows,
    )
    d_pairs_own = lax.psum_scatter(d_pairs, "row", scatter_dimension=0, tiled=True)
    d_mixed = jnp.concatenate([d_queries[:, :, None], d_pairs_own], axis=2).astype(jnp.bfloat16)
    d_mixed_all = gather_rows(d_mixed)
    normed1_use = gather_columns(normed1)
    d_mixed_flat = d_mixed_all.reshape(group_rows, head_count * 3 * HEAD)
    qkv_grad = outer_sum(normed1_use, d_mixed_flat)
    mixed_totals = jnp.sum(d_mixed_all, axis=0, dtype=jnp.float32)
    qv_bias_grad = jnp.stack([mixed_totals[:, 0], mixed_totals[:, 2]], axis=1)
    d_normed1 = sum_columns(d_mixed_flat, qkv_flat, True)
    d_norm1, gain1_grad, shift1_grad = norm_backward(d_normed1, standard1, inverse1, ln1_gain)
    tokens_grad = (d_residual + d_norm1).astype(jnp.bfloat16)
    norm_sums = lax.psum((gain1_grad, shift1_grad, gain2_grad, shift2_grad), ("dp", "col"))
    weight_sums = lax.psum(
        (
            qkv_grad,
            qv_bias_grad,
            out_grad,
            out_bias_grad,
            up_grad,
            up_bias_grad,
            down_grad,
            down_bias_grad,
        ),
        "dp",
    )
    return (
        output,
        tokens_grad,
        norm_sums[0],
        norm_sums[1],
        weight_sums[0].reshape(row_width, head_count, 3, HEAD),
        weight_sums[1],
        weight_sums[2].reshape(head_count, HEAD, row_width),
        weight_sums[3],
        norm_sums[2],
        norm_sums[3],
        weight_sums[4],
        weight_sums[5],
        weight_sums[6],
        weight_sums[7],
    )


def solution(mesh):
    placed = (
        P(("dp", "col"), "row"),
        P("row"),
        P("row"),
        P("row", "col", None, None),
        P("col", None, None),
        P("col", None, "row"),
        P("row"),
        P("row"),
        P("row"),
        P("row", "col"),
        P("col"),
        P("col", "row"),
        P("row"),
        P("dp", None),
        P(("dp", "col"), "row"),
    )
    return jax.shard_map(
        per_device,
        mesh=mesh,
        in_specs=placed,
        out_specs=(
            P(("dp", "col"), "row"),
            P(("dp", "col"), "row"),
            P("row"),
            P("row"),
            P("row", "col", None, None),
            P("col", None, None),
            P("col", None, "row"),
            P("row"),
            P("row"),
            P("row"),
            P("row", "col"),
            P("col"),
            P("col", "row"),
            P("row"),
        ),
        check_vma=False,
    )
```

profile of v0, /device:TPU:0, one launch (start us, length us, event | category | flops | bytes accessed | tf_op | source)
XLA Modules:
  0.0 1871.9 jit_solution(15928005166205797465)
XLA Ops:
  8.5 8.4 all-reduce.4
  16.9 2.1 fusion.43
  19.1 5.0 copy.103
  24.1 16.7 all-gather.14.cloned.1.call-done
  40.8 3.5 all-to-all-start
  44.4 18.3 all-to-all-done
  64.3 63.8 %all-gather.16.cloned.1.call-done = bf16[2048,3072]{0,1:T(8,128)(2,1)} async-done(((bf16[512,3072]{0,1:T(8,128)(2,1)}), bf16[2048,3072]{0,1:T(8,128)(2,1)}) %all-gather.16.cloned.1.call-update) | async-done | bytes 12582928 | tf_op jit(solution)/shard_map/all_gather | solution.py:54
  128.1 7.0 fusion.54
  139.6 32.0 %all-gather.18.cloned.1.call-done = bf16[1024,8,2,128]{3,0,2,1:T(8,128)(2,1)} async-done(((bf16[256,8,2,128]{3,0,2,1:T(8,128)(2,1)}), bf16[1024,8,2,128]{3,0,2,1:T(8,128)(2,1)}) %all-gather.18.cloned.1.call-update) | async-done | bytes 4194320 | tf_op jit(solution)/shard_map/all_gather | solution.py:32
  171.7 4.6 copy.104
  176.4 3.9 while.56
  178.5 1.8 fusion.128
  181.3 34.6 %all-gather.20.cloned.1.call-done = bf16[1024,1024]{0,1:T(8,128)(2,1)} async-done(((bf16[256,1024]{0,1:T(8,128)(2,1)}), bf16[1024,1024]{0,1:T(8,128)(2,1)}) %all-gather.20.cloned.1.call-update) | async-done | bytes 2097168 | tf_op jit(solution)/shard_map/all_gather | solution.py:32
  215.9 4.2 fusion.64
  220.8 31.3 %reduce-scatter.6.cloned.1.call-done = f32[512,512]{1,0:T(8,128)} async-done(((f32[1024,512]{1,0:T(8,128)}), f32[512,512]{1,0:T(8,128)}) %reduce-scatter.6.cloned.1.call-update) | async-done | bytes 1048592 | tf_op jit(solution)/shard_map/reduce_scatter | solution.py:59
  253.6 6.9 all-reduce.3
  263.1 11.9 all-gather.28.cloned.1.call-done
  274.9 18.8 %all_to_all.76 = bf16[4,256,512]{2,1,0:T(8,128)(2,1)} all-to-all(bf16[4,256,512]{2,1,0:T(8,128)(2,1)} %bitcast.189), channel_id=1, replica_groups=mesh['dp'=4,'row'=4,'col'=2] {'row'}, dimensions={0} | all-to-all | bytes 2097152 | tf_op jit(solution)/shard_map/all_to_all | solution.py:50
  293.7 2.3 copy.106
  296.0 2.5 all-gather.22.cloned.1.call-done
  298.5 2.3 copy.105
  300.7 4.2 all-to-all-start.1
  305.3 106.2 %all-gather.30.cloned.1.call-done = bf16[4096,2048]{1,0:T(8,128)(2,1)} async-done(((bf16[4096,512]{1,0:T(8,128)(2,1)}), bf16[4096,2048]{1,0:T(8,128)(2,1)}) %all-gather.30.cloned.1.call-update) | async-done | bytes 16777232 | tf_op jit(solution)/shard_map/all_gather | solution.py:52
  411.5 13.0 fusion.66
  424.5 93.7 %all-gather.24.cloned.1.call-done = bf16[2048,4096]{1,0:T(8,128)(2,1)} async-done(((bf16[512,4096]{1,0:T(8,128)(2,1)}), bf16[2048,4096]{1,0:T(8,128)(2,1)}) %all-gather.24.cloned.1.call-update) | async-done | bytes 16777232 | tf_op jit(solution)/shard_map/all_gather | solution.py:54
  518.2 13.7 fusion.34
  533.1 57.3 %all-gather.32.cloned.1.call-done = bf16[1024,4096]{1,0:T(8,128)(2,1)} async-done(((bf16[256,4096]{1,0:T(8,128)(2,1)}), bf16[1024,4096]{1,0:T(8,128)(2,1)}) %all-gather.32.cloned.1.call-update) | async-done | bytes 8388624 | tf_op jit(solution)/shard_map/all_gather | solution.py:32
  590.3 10.4 fusion.67
  600.8 50.1 %all-gather.26.cloned.1.call-done = bf16[1024,4096]{1,0:T(8,128)(2,1)} async-done(((bf16[256,4096]{1,0:T(8,128)(2,1)}), bf16[1024,4096]{1,0:T(8,128)(2,1)}) %all-gather.26.cloned.1.call-update) | async-done | bytes 8388624 | tf_op jit(solution)/shard_map/all_gather | solution.py:32
  650.9 10.4 fusion.65
  661.3 24.1 %reduce-scatter.10.cloned.1.call-done = f32[512,512]{1,0:T(8,128)} async-done(((f32[1024,512]{1,0:T(8,128)}), f32[512,512]{1,0:T(8,128)}) %reduce-scatter.10.cloned.1.call-update) | async-done | bytes 1048592 | tf_op jit(solution)/shard_map/reduce_scatter | solution.py:59
  685.5 1.7 multiply_reduce_fusion
  687.2 6.9 all-reduce.2
  694.1 26.1 %reduce-scatter.8.cloned.1.call-done = f32[512,512]{1,0:T(8,128)} async-done(((f32[1024,512]{1,0:T(8,128)}), f32[512,512]{1,0:T(8,128)}) %reduce-scatter.8.cloned.1.call-update) | async-done | bytes 1048592 | tf_op jit(solution)/shard_map/reduce_scatter | solution.py:59
  720.2 3.5 fusion.60
  724.3 20.9 %all-gather.34.cloned.1.call-done = bf16[1024,512]{1,0:T(8,128)(2,1)} async-done(((bf16[512,512]{1,0:T(8,128)(2,1)}), bf16[1024,512]{1,0:T(8,128)(2,1)}) %all-gather.34.cloned.1.call-update) | async-done | bytes 1048592 | tf_op jit(solution)/shard_map/all_gather | solution.py:28
  745.2 2.3 copy.107
  747.4 3.5 all-to-all-start.3
  751.0 38.4 %all-gather.36.cloned.1.call-done = bf16[1024,2048]{1,0:T(8,128)(2,1)} async-done(((bf16[1024,512]{1,0:T(8,128)(2,1)}), bf16[1024,2048]{1,0:T(8,128)(2,1)}) %all-gather.36.cloned.1.call-update) | async-done | bytes 4194320 | tf_op jit(solution)/shard_map/all_gather | solution.py:52
  790.4 3.8 convolution_convert_fusion
  796.8 4.3 broadcast_in_dim.100.clone
  801.1 9.1 while.57
  801.3 1.7 fusion.137
  806.9 1.8 constant_dynamic-slice_fusion.2
  810.7 97.5 %reduce-scatter.12.cloned.1.call-done = f32[256,8,2,128]{3,0,2,1:T(8,128)} async-done(((f32[1024,8,2,128]{3,0,2,1:T(8,128)}), f32[256,8,2,128]{3,0,2,1:T(8,128)}) %reduce-scatter.12.cloned.1.call-update) | async-done | bytes 2097168 | tf_op jit(solution)/shard_map/reduce_scatter | solution.py:326
  908.2 1.8 convert.17
  911.4 46.5 %all-gather.38.cloned.1.call-done = bf16[1024,8,3,128]{3,0,2,1:T(8,128)(2,1)} async-done(((bf16[256,8,3,128]{3,0,2,1:T(8,128)(2,1)}), bf16[1024,8,3,128]{3,0,2,1:T(8,128)(2,1)}) %all-gather.38.cloned.1.call-update) | async-done | bytes 6291472 | tf_op jit(solution)/shard_map/all_gather | solution.py:32
  957.9 7.4 convolution_bitcast_fusion.3
  965.5 10.3 fusion.69
  975.8 10.5 fusion.70
  986.3 2.6 fusion.68
  988.9 8.6 copy.114
  997.5 9.2 fusion.71
  1006.9 4.6 convert_reduce_fusion
  1011.7 4.6 convert_reduce_fusion.1
  1016.3 21.9 %all-reduce.5 = (f32[8,2,128]{2,1,0:T(2,128)}, f32[512]{0:T(512)}, f32[4096]{0:T(1024)}, f32[512]{0:T(512)}) all-reduce(f32[8,2,128]{2,1,0:T(2,128)S(1)} %pad_maximum_fusion.2, f32[512]{0:T(512)S(1)} %convert_reduce_fusion.3, f32[4096]{0:T(1024)S(1)} %convert_reduce_fusion, ...), channel_id=1, replica_groups=mesh['dp'=4,'row'=4,'col'=2] {'dp'}, use_global_device_ids=true, to_apply=%region_35.36 | all-reduce | flops 7168 | bytes 57344 | tf_op jit(solution)/shard_map/psum | solution.py:338
  1038.3 1.8 fusion.49
  1040.1 22.1 %all-reduce = (f32[512]{0:T(512)}, f32[512]{0:T(512)}, f32[512]{0:T(512)}, f32[512]{0:T(512)}) all-reduce(f32[512]{0:T(512)S(1)} %get-tuple-element.702, f32[512]{0:T(512)S(1)} %get-tuple-element.707, f32[512]{0:T(512)S(1)} %get-tuple-element.700, f32[512]{0:T(512)S(1)} %get-tuple-element.706), channel_id=1, replica_groups=mesh['dp'=4,'row'=4,'col'=2] {'dp','col'}, use_global_device_ids=true, to_apply=%region_30.31 | all-reduce | flops 2048 | bytes 16384 | tf_op jit(solution)/shard_map/psum | solution.py:337
  1062.1 6.0 all-reduce.1
  1068.2 2.4 fusion.48
  1070.6 774.6 %all-reduce.9.cloned.1.call-done = (f32[512,8,3,128]{0,3,2,1:T(8,128)}, f32[8,128,512]{2,1,0:T(8,128)}, f32[512,4096]{1,0:T(8,128)}, f32[4096,512]{1,0:T(8,128)}) async-done(((f32[512,8,3,128]{0,3,2,1:T(8,128)}, f32[8,128,512]{2,1,0:T(8,128)}, f32[512,4096]{1,0:T(8,128)}, f32[4096,512]{1,0:T(8,128)}), (f32[512,8,3,128]{0,3,2,1:T(8,128)}, f32[8,128,512]{2,1,0:T(8,128)}, f32[512,4096]{1,0:T(8,128)}, ...) | async-done | bytes 25165840 | tf_op jit(solution)/shard_map/psum | solution.py:338
  1845.3 6.7 copy.116
  1853.3 8.5 copy.182
  1861.8 3.4 copy.183
  (150 shorter events, 30.5 us)
Async XLA Ops:
  7.2 33.6 %all-gather.14.cloned.1.call-start = ((), (), s32[]{:S(2)}) async-start(), calls=%async_computation.9 | async-start | bytes 1572864 | tf_op jit(solution)/shard_map/all_gather | solution.py:28
  16.9 7.2 copy-start.9
  16.9 7.2 copy-start.11
  19.0 109.1 %all-gather.16.cloned.1.call-start = ((), (), s32[]{:S(2)}) async-start(), calls=%async_computation.10 | async-start | bytes 15728640 | tf_op jit(solution)/shard_map/all_gather | solution.py:54
  24.1 20.3 %copy-start.15 = (f32[8,2,128]{2,1,0:T(2,128)S(1)}, f32[8,2,128]{2,1,0:T(2,128)}, u32[]{:S(2)}) copy-start(f32[8,2,128]{2,1,0:T(2,128)} %param.23) | copy-start | bytes 24580
  40.8 21.9 %all-to-all-start = ((bf16[4,256,512]{2,1,0:T(8,128)(2,1)}), bf16[4,256,512]{2,1,0:T(8,128)(2,1)S(1)}, u32[]{:S(2)}, u32[]{:S(2)}) async-start(bf16[4,256,512]{2,1,0:T(8,128)(2,1)} %bitcast.199), calls=%async_computation | async-start | bytes 2097152 | tf_op jit(solution)/shard_map/all_to_all | solution.py:50
  44.3 127.4 %all-gather.18.cloned.1.call-start = ((), (), s32[]{:S(2)}) async-start(), calls=%async_computation.11 | async-start | bytes 5242880 | tf_op jit(solution)/shard_map/all_gather | solution.py:32
  135.1 1.7 copy-start.5
  135.1 2.9 copy-start.21
  138.0 77.9 %all-gather.20.cloned.1.call-start = ((), (), s32[]{:S(2)}) async-start(), calls=%async_computation.12 | async-start | bytes 2621440 | tf_op jit(solution)/shard_map/all_gather | solution.py:32
  176.4 39.5 %copy-start.7 = (bf16[8,128,512]{2,1,0:T(8,128)(2,1)S(1)}, bf16[8,128,512]{2,1,0:T(8,128)(2,1)}, u32[]{:S(2)}) copy-start(bf16[8,128,512]{2,1,0:T(8,128)(2,1)} %param.24) | copy-start | bytes 3145732
  181.3 70.9 %reduce-scatter.6.cloned.1.call-start = ((), (), s32[]{:S(2)}) async-start(), calls=%async_computation.13 | async-start | bytes 3145728 | tf_op jit(solution)/shard_map/reduce_scatter | solution.py:59
  215.9 36.3 %copy-start = (bf16[512,512]{1,0:T(8,128)(2,1)S(1)}, bf16[512,512]{1,0:T(8,128)(2,1)}, u32[]{:S(2)}) copy-start(bf16[512,512]{1,0:T(8,128)(2,1)} %param.19) | copy-start | bytes 1572868
  215.9 36.3 %copy-start.18 = (f32[512]{0:T(512)S(1)}, f32[512]{0:T(512)}, u32[]{:S(2)}) copy-start(f32[512]{0:T(512)} %param.25) | copy-start | bytes 6148
  220.1 40.4 %copy-start.13 = (f32[512]{0:T(512)S(1)}, f32[512]{0:T(512)}, u32[]{:S(2)}) copy-start(f32[512]{0:T(512)} %param.26) | copy-start | bytes 6148
  220.1 40.4 %copy-start.17 = (f32[512]{0:T(512)S(1)}, f32[512]{0:T(512)}, u32[]{:S(2)}) copy-start(f32[512]{0:T(512)} %param.27) | copy-start | bytes 6148
  220.2 54.8 %all-gather.28.cloned.1.call-start = ((), (), s32[]{:S(2)}) async-start(), calls=%async_computation.18 | async-start | bytes 1572864 | tf_op jit(solution)/shard_map/all_gather | solution.py:28
  220.7 77.7 %all-gather.22.cloned.1.call-start = ((), (), s32[]{:S(2)}) async-start(), calls=%async_computation.14 | async-start | bytes 1572864 | tf_op jit(solution)/shard_map/all_gather | solution.py:28
  261.6 149.9 %all-gather.30.cloned.1.call-start = ((), (), s32[]{:S(2)}) async-start(), calls=%async_computation.19 | async-start | bytes 20971520 | tf_op jit(solution)/shard_map/all_gather | solution.py:52
  262.3 255.8 %all-gather.24.cloned.1.call-start = ((), (), s32[]{:S(2)}) async-start(), calls=%async_computation.15 | async-start | bytes 20971520 | tf_op jit(solution)/shard_map/all_gather | solution.py:54
  300.7 217.4 %all-to-all-start.1 = ((bf16[4,256,512]{1,2,0:T(8,128)(2,1)}), bf16[4,256,512]{1,2,0:T(8,128)(2,1)}, u32[]{:S(2)}, u32[]{:S(2)}) async-start(bf16[4,256,512]{1,2,0:T(8,128)(2,1)} %copy.105), calls=%async_computation.2 | async-start | bytes 2097152 | tf_op jit(solution)/shard_map/all_to_all | solution.py:50
  305.0 285.3 %all-gather.32.cloned.1.call-start = ((), (), s32[]{:S(2)}) async-start(), calls=%async_computation.20 | async-start | bytes 10485760 | tf_op jit(solution)/shard_map/all_gather | solution.py:32
  411.5 106.7 %copy-start.20 = (f32[4096]{0:T(1024)S(1)}, f32[4096]{0:T(1024)}, u32[]{:S(2)}) copy-start(f32[4096]{0:T(1024)} %param.29) | copy-start | bytes 49156
  531.9 119.0 %all-gather.26.cloned.1.call-start = ((), (), s32[]{:S(2)}) async-start(), calls=%async_computation.16 | async-start | bytes 10485760 | tf_op jit(solution)/shard_map/all_gather | solution.py:32
  532.6 152.9 %reduce-scatter.10.cloned.1.call-start = ((), (), s32[]{:S(2)}) async-start(), calls=%async_computation.21 | async-start | bytes 3145728 | tf_op jit(solution)/shard_map/reduce_scatter | solution.py:59
  600.8 119.4 %reduce-scatter.8.cloned.1.call-start = ((), (), s32[]{:S(2)}) async-start(), calls=%async_computation.17 | async-start | bytes 3145728 | tf_op jit(solution)/shard_map/reduce_scatter | solution.py:59
  661.3 58.9 %copy-start.16 = (f32[512]{0:T(512)S(1)}, f32[512]{0:T(512)}, u32[]{:S(2)}) copy-start(f32[512]{0:T(512)} %param.31) | copy-start | bytes 6148
  661.3 83.9 %all-gather.34.cloned.1.call-start = ((), (), s32[]{:S(2)}) async-start(), calls=%async_computation.22 | async-start | bytes 1572864 | tf_op jit(solution)/shard_map/all_gather | solution.py:28
  723.7 65.8 %all-gather.36.cloned.1.call-start = ((), (), s32[]{:S(2)}) async-start(), calls=%async_computation.23 | async-start | bytes 5242880 | tf_op jit(solution)/shard_map/all_gather | solution.py:52
  747.4 42.0 %all-to-all-start.3 = ((bf16[4,256,512]{1,2,0:T(8,128)(2,1)}), bf16[4,256,512]{1,2,0:T(8,128)(2,1)S(1)}, u32[]{:S(2)}, u32[]{:S(2)}) async-start(bf16[4,256,512]{1,2,0:T(8,128)(2,1)} %copy.107), calls=%async_computation.6 | async-start | bytes 2097152 | tf_op jit(solution)/shard_map/all_to_all | solution.py:50
  751.0 157.3 %reduce-scatter.12.cloned.1.call-start = ((), (), s32[]{:S(2)}) async-start(), calls=%async_computation.24 | async-start | bytes 10485760 | tf_op jit(solution)/shard_map/reduce_scatter | solution.py:326
  789.5 1.0 copy-start.8
  810.2 147.6 %all-gather.38.cloned.1.call-start = ((), (), s32[]{:S(2)}) async-start(), calls=%async_computation.25 | async-start | bytes 7864320 | tf_op jit(solution)/shard_map/all_gather | solution.py:32
  911.3 54.2 %copy-start.1 = (bf16[1024,512]{1,0:T(8,128)(2,1)S(1)}, bf16[1024,512]{1,0:T(8,128)(2,1)}, u32[]{:S(2)}) copy-start(bf16[1024,512]{1,0:T(8,128)(2,1)} %all-gather.22.cloned.1.call-done) | copy-start | bytes 3145732
  911.3 127.0 %reduce-scatter.14.cloned.1.call-start = ((), (), s32[]{:S(2)}) async-start(), calls=%async_computation.26 | async-start | bytes 3145728 | tf_op jit(solution)/shard_map/reduce_scatter | solution.py:59
  965.3 10.5 copy-start.2
  965.3 879.9 %all-reduce.9.cloned.1.call-start = ((), (), s32[]{:S(2)}) async-start(), calls=%async_computation.27 | async-start | bytes 50331648 | tf_op jit(solution)/shard_map/psum | solution.py:338
  975.8 10.5 copy-start.4
  975.8 10.5 copy-start.19
  1011.5 26.8 %copy-start.10 = (f32[512]{0:T(512)S(1)}, f32[512]{0:T(512)}, u32[]{:S(2)}) copy-start(f32[512]{0:T(512)} %copy-done.9) | copy-start | bytes 6148
  1011.5 26.8 %copy-start.12 = (f32[512]{0:T(512)S(1)}, f32[512]{0:T(512)}, u32[]{:S(2)}) copy-start(f32[512]{0:T(512)} %copy-done.11) | copy-start | bytes 6148
  1011.5 26.8 %copy-start.14 = (f32[512]{0:T(512)S(1)}, f32[512]{0:T(512)}, u32[]{:S(2)}) copy-start(f32[512]{0:T(512)} %param.20) | copy-start | bytes 6148
  1011.7 56.5 %copy-start.3 = (f32[512,512]{1,0:T(8,128)S(1)}, f32[512,512]{1,0:T(8,128)}, u32[]{:S(2)}) copy-start(f32[512,512]{1,0:T(8,128)} %get-tuple-element.775) | copy-start | bytes 3145732
  1845.3 6.7 copy-start.6
  1852.0 9.8 slice-start
  1853.3 8.5 slice-start.1
Sparse Core Ops, SparseCore 0:
  19.2 21.5 all-gather.13
  42.4 85.7 all-gather.15
  138.1 33.5 all-gather.17
  181.4 34.4 all-gather.19
  220.3 31.8 reduce-scatter.5
  253.6 21.2 all-gather.27
  277.1 21.2 all-gather.21
  300.1 111.2 all-gather.29
  413.1 105.0 all-gather.23
  532.0 58.2 all-gather.31
  592.6 58.2 all-gather.25
  653.6 31.8 reduce-scatter.9
  688.3 31.8 reduce-scatter.7
  723.8 21.2 all-gather.33
  746.7 42.7 all-gather.35
  810.4 97.8 reduce-scatter.11
  911.4 46.3 all-gather.37
  965.4 31.8 reduce-scatter.13
  1006.8 838.3 all-reduce.8
where the time goes:
time: 1880 us; the launch traced here: 1870 us
  waiting for transfers between devices  1550 us (82%)
  matrix products  111 us (6%)
  blocking collectives  90.9 us (5%)
  local copies, waits for them, and re-layouts  58.2 us (3%)
  other arithmetic  34 us (2%)
    psum x1, waiting for transfers between devices, per_device(): lax.psum((qkv_grad, qv_bias_grad, out_grad, out_bias_grad, up_grad, up_bi...  775 us
    all_gather x5, waiting for transfers between devices, gather_rows(): return lax.all_gather(block_data, 'row', axis=0, tiled=True)  220 us
    all_gather x2, waiting for transfers between devices, sum_rows(): wide_right = lax.all_gather(right_side, 'row', axis=0, tiled=True)  157 us
    all_gather x2, waiting for transfers between devices, sum_rows(): wide_right = lax.all_gather(right_side, 'row', axis=1, tiled=True)  145 us
    reduce_scatter x1, waiting for transfers between devices, per_device(): lax.psum_scatter(d_pairs, 'row', scatter_dimension=0, tiled=True)  97.5 us
    reduce_scatter x4, waiting for transfers between devices, sum_columns(): lax.psum_scatter(product(left_side, right_side, flipped), 'col', scatter_...  81.6 us
    all_gather x4, waiting for transfers between devices, gather_columns(): return lax.all_gather(block_data, 'col', axis=0, tiled=True)  51.9 us
  transfers between devices with their start and end apart: 22, of which 19 were waited for; matrix products, arithmetic and copies ran while one was open for 6% of the time, Pallas kernels for 0%

commit v1 on v0

--- a/solution.py
+++ b/solution.py
@@ -1,9 +1,14 @@
+import functools
 import math
 
 import jax
 import jax.numpy as jnp
 from jax import lax
+from jax.experimental import pallas as pl
+from jax.experimental.pallas import tpu as pltpu
 from jax.sharding import PartitionSpec as P
+
+MESH = pl.DeviceIdType.MESH
 
 D = 2048
 HEAD = 128
@@ -230,7 +235,7 @@
     return lax.fori_loop(0, own_rows // block_rows, block_backward, initial)
 
 
-def per_device(
+def general_plan(
     tokens,
     ln1_gain,
     ln1_shift,
@@ -366,7 +371,349 @@
     )
 
 
+def places():
+    row, col = lax.axis_index("row"), lax.axis_index("col")
+    side, core = row // 2, row % 2
+    return col, side, core
+
+def partners():
+    col, side, core = places()
+    return ({"col": 1 - col}, {"row": (1 - side) * 2 + core}, {"row": side * 2 + 1 - core})
+
+def greet():
+    barrier = pltpu.get_barrier_semaphore()
+    for partner in partners():
+        pl.semaphore_signal(barrier, inc=1, device_id=partner, device_id_type=MESH)
+    pl.semaphore_wait(barrier, 3)
+
+def block(ref, col, side, core, rows, width, part=None):
+    begin, count = col * rows, rows
+    if part is not None:
+        begin, count = begin + part * (rows // 2), rows // 2
+    left = (side * 2 + core) * width
+    return ref.at[pl.ds(pl.multiple_of(begin, count), count), pl.ds(pl.multiple_of(left, width), width)]
+
+def send(ref_from, ref_to, sends, recvs, at, partner):
+    copy = pltpu.make_async_remote_copy(src_ref=ref_from, dst_ref=ref_to, send_sem=sends.at[at], recv_sem=recvs.at[at], device_id=partner, device_id_type=MESH)
+    copy.start()
+    return copy
+
+def spread(out, rows, width, sends, recvs, base):
+    col, side, core = places()
+    to_x, to_y, to_core = partners()
+    def go(at, which, partner, part=None):
+        ref = block(out, *which, rows, width, part)
+        return send(ref, ref, sends, recvs, base + at, partner)
+    own, ox, oy, od = (col, side, core), (1 - col, side, core), (col, 1 - side, core), (1 - col, 1 - side, core)
+    c0 = go(0, own, to_x)
+    c1 = go(1, own, to_y)
+    c2 = go(2, own, to_core)
+    c0.wait_recv()
+    c3 = go(3, ox, to_y, 0)
+    c1.wait_recv()
+    c4 = go(4, oy, to_x, 1)
+    c5 = go(5, ox, to_core)
+    c6 = go(6, oy, to_core)
+    c3.wait_recv()
+    c4.wait_recv()
+    c7 = go(7, od, to_core)
+    for c in (c2, c5, c6, c7):
+        c.wait_recv()
+    for c in (c0, c1, c2, c3, c4, c5, c6, c7):
+        c.wait_send()
+
+def gather_kernel(x_ref, out, sends, recvs):
+    rows, width = x_ref.shape
+    greet()
+    col, side, core = places()
+    block(out, col, side, core, rows, width)[...] = x_ref[...]
+    spread(out, rows, width, sends, recvs, 0)
+
+def gather_plane(x, cid):
+    rows, width = x.shape
+    return pl.pallas_call(gather_kernel, out_shape=jax.ShapeDtypeStruct((2*rows,4*width), x.dtype),
+        in_specs=[pl.BlockSpec(memory_space=pltpu.VMEM)], out_specs=pl.BlockSpec(memory_space=pltpu.VMEM),
+        scratch_shapes=[pltpu.SemaphoreType.DMA((8,)), pltpu.SemaphoreType.DMA((8,))],
+        compiler_params=pltpu.CompilerParams(collective_id=cid, has_side_effects=True, vmem_limit_bytes=50<<20))(x)
+
+def sum_to_owner(part_ref, got, keep, diag, half_x, half_y, to_send, from_xy, sends, recvs, rows, width):
+    col, side, core = places()
+    to_x, to_y, to_core = partners()
+    half = rows // 2
+    spots = ((1-col,1-side),(col,1-side),(1-col,side),(col,side))
+    copies = []
+    for i,(a,b) in enumerate(spots):
+        copies.append(send(block(part_ref, a, b, 1-core, rows, width), got.at[i], sends, recvs, i, to_core))
+    f32 = jnp.float32
+    copies[0].wait_recv()
+    diag[...] = (block(part_ref, 1-col, 1-side, core, rows, width)[...].astype(f32) + got[0].astype(f32)).astype(diag.dtype)
+    dx = send(diag.at[pl.ds(0,half)], half_x, sends, recvs, 4, to_x)
+    dy = send(diag.at[pl.ds(half,half)], half_y, sends, recvs, 5, to_y)
+    copies[1].wait_recv()
+    copies[2].wait_recv()
+    dx.wait_recv()
+    py = block(part_ref, col, 1-side, core, rows, width)
+    px = block(part_ref, 1-col, side, core, rows, width)
+    ty = to_send.at[0]
+    tx = to_send.at[1]
+    ty[pl.ds(0,half)] = (py[pl.ds(0,half)].astype(f32) + got[1,pl.ds(0,half)].astype(f32) + half_x[...].astype(f32)).astype(diag.dtype)
+    ty[pl.ds(half,half)] = (py[pl.ds(half,half)].astype(f32) + got[1,pl.ds(half,half)].astype(f32)).astype(diag.dtype)
+    cy = send(ty, from_xy.at[0], sends, recvs, 6, to_y)
+    dy.wait_recv()
+    tx[pl.ds(0,half)] = (px[pl.ds(0,half)].astype(f32) + got[2,pl.ds(0,half)].astype(f32)).astype(diag.dtype)
+    tx[pl.ds(half,half)] = (px[pl.ds(half,half)].astype(f32) + got[2,pl.ds(half,half)].astype(f32) + half_y[...].astype(f32)).astype(diag.dtype)
+    cx = send(tx, from_xy.at[1], sends, recvs, 7, to_x)
+    copies[3].wait_recv()
+    keep[...] = block(part_ref, col, side, core, rows, width)[...].astype(f32) + got[3].astype(f32)
+    cy.wait_recv()
+    cx.wait_recv()
+    for c in copies + [dx, dy, cy, cx]:
+        c.wait_send()
+    return keep[...] + from_xy[0].astype(f32) + from_xy[1].astype(f32)
+
+def sum_scratch(rows, width, dt):
+    return [pltpu.VMEM((4,rows,width),dt), pltpu.VMEM((rows,width),jnp.float32), pltpu.VMEM((rows,width),dt),
+            pltpu.VMEM((rows//2,width),dt), pltpu.VMEM((rows//2,width),dt), pltpu.VMEM((2,rows,width),dt), pltpu.VMEM((2,rows,width),dt)]
+
+def reduce_kernel(part_ref, out, *scratch):
+    *bufs, sends, recvs = scratch
+    rows, width = out.shape
+    greet()
+    out[...] = sum_to_owner(part_ref, *bufs, sends, recvs, rows, width)
+
+def reduce_plane(part, cid):
+    rows, width = part.shape[0]//2, part.shape[1]//4
+    return pl.pallas_call(reduce_kernel, out_shape=jax.ShapeDtypeStruct((rows,width), jnp.float32),
+        in_specs=[pl.BlockSpec(memory_space=pltpu.VMEM)], out_specs=pl.BlockSpec(memory_space=pltpu.VMEM),
+        scratch_shapes=sum_scratch(rows,width,part.dtype)+[pltpu.SemaphoreType.DMA((8,)), pltpu.SemaphoreType.DMA((8,))],
+        compiler_params=pltpu.CompilerParams(collective_id=cid, has_side_effects=True, vmem_limit_bytes=50<<20))(part)
+
+def total_kernel(part_ref, out, *scratch):
+    *bufs, sends, recvs = scratch
+    rows, width = out.shape[0]//2, out.shape[1]//4
+    greet()
+    own = sum_to_owner(part_ref, *bufs, sends, recvs, rows, width)
+    col, side, core = places()
+    block(out, col, side, core, rows, width)[...] = own.astype(out.dtype)
+    spread(out, rows, width, sends, recvs, 8)
+
+def total_plane(part, cid):
+    rows, width = part.shape[0]//2, part.shape[1]//4
+    return pl.pallas_call(total_kernel, out_shape=jax.ShapeDtypeStruct(part.shape, part.dtype),
+        in_specs=[pl.BlockSpec(memory_space=pltpu.VMEM)], out_specs=pl.BlockSpec(memory_space=pltpu.VMEM),
+        scratch_shapes=sum_scratch(rows,width,part.dtype)+[pltpu.SemaphoreType.DMA((16,)), pltpu.SemaphoreType.DMA((16,))],
+        compiler_params=pltpu.CompilerParams(collective_id=cid, has_side_effects=True, vmem_limit_bytes=50<<20))(part)
+
+
+def shift_rows(pieces):
+    row, count = lax.axis_index("row"), pieces.shape[0]
+    result = pieces
+    for step in range(1, count):
+        pairs = [(k, (k + step) % count) for k in range(count)]
+        sent = lax.dynamic_index_in_dim(pieces, (row + step) % count, 0, keepdims=True)
+        got = lax.ppermute(sent, "row", pairs)
+        result = lax.dynamic_update_slice_in_dim(result, got, (row + count - step) % count, 0)
+    return result
+
+
+def dp_total(share):
+    place = lax.axis_index("dp")
+    f32 = jnp.float32
+    inner = (place == 1) | (place == 2)
+    came = lax.ppermute(share, "dp", [(0, 1), (3, 2)])
+    half = (share.astype(f32) + came.astype(f32)).astype(share.dtype)
+    across = lax.ppermute(half, "dp", [(1, 2), (2, 1)])
+    total = (half.astype(f32) + across.astype(f32)).astype(share.dtype)
+    back = lax.ppermute(total, "dp", [(1, 0), (2, 3)])
+    return jnp.where(inner, total, back)
+
+
+def norm_stats(values):
+    center = jnp.mean(values, axis=1, keepdims=True)
+    spread_of = jnp.mean(values * values, axis=1, keepdims=True) - center * center
+    return center, lax.rsqrt(spread_of + epsilon)
+
+
+def mask_of(span_starts, length):
+    marks = jnp.sum(
+        (span_starts[0][:, None] // SPAN == jnp.arange(length // SPAN, dtype=jnp.int32)[None, :]).astype(jnp.int32),
+        axis=0,
+    )
+    places_of = jnp.arange(length, dtype=jnp.int32)
+    image = jnp.repeat(marks, SPAN)
+    return visible(places_of, image, places_of)
+
+
+def plane_plan(
+    tokens,
+    ln1_gain,
+    ln1_shift,
+    qkv_weight,
+    qv_bias,
+    out_weight,
+    out_bias,
+    ln2_gain,
+    ln2_shift,
+    up_weight,
+    up_bias,
+    down_weight,
+    down_bias,
+    span_starts,
+    cotangent,
+):
+    f32, bf16 = jnp.float32, jnp.bfloat16
+    rows, width = tokens.shape
+    row_count = lax.axis_size("row")
+    col, row = lax.axis_index("col"), lax.axis_index("row")
+    length, full = rows * lax.axis_size("col"), width * row_count
+    heads = qkv_weight.shape[1] // row_count
+    hidden_count = up_weight.shape[1] // row_count
+    factor = 1.0 / math.sqrt(HEAD)
+
+    def own(values):
+        return lax.dynamic_slice(values, (col * rows, row * width), (rows, width))
+
+    def own_width(values):
+        return lax.dynamic_slice_in_dim(values, row * width, width, values.ndim - 1)
+
+    def wide(vector):
+        return lax.all_gather(vector, "row", axis=0, tiled=True)
+
+    qkv_flat = shift_rows(
+        jnp.moveaxis(qkv_weight.reshape(width, row_count, heads * 3 * HEAD), 1, 0)
+    ).reshape(full, heads * 3 * HEAD)
+    out_flat = jnp.moveaxis(
+        shift_rows(out_weight.reshape(row_count, heads * HEAD, width)), 0, 1
+    ).reshape(heads * HEAD, full)
+    up_flat = shift_rows(jnp.moveaxis(up_weight.reshape(width, row_count, hidden_count), 1, 0)).reshape(
+        full, hidden_count
+    )
+    down_flat = jnp.moveaxis(
+        shift_rows(down_weight.reshape(row_count, hidden_count, width)), 0, 1
+    ).reshape(hidden_count, full)
+    vectors = wide(jnp.stack([ln1_gain, ln1_shift, out_bias, ln2_gain, ln2_shift], axis=0).T)
+    gain1, shift1, branch_bias, gain2, shift2 = [vectors[:, k] for k in range(5)]
+    own_qv = lax.dynamic_slice_in_dim(qv_bias, row * heads, heads, 0)
+    own_up_bias = lax.dynamic_slice_in_dim(up_bias, row * hidden_count, hidden_count, 0)
+    allowed = mask_of(span_starts, length)
+
+    tokens_all = gather_plane(tokens, 1)
+    cot_all = gather_plane(cotangent, 2)
+    inputs = tokens_all.astype(f32)
+    center1, inverse1 = norm_stats(inputs)
+    normed1 = ((inputs - center1) * inverse1 * gain1 + shift1).astype(bf16)
+    mixed = product(normed1, qkv_flat, False).reshape(length, heads, 3, HEAD)
+    queries = (mixed[:, :, 0] + own_qv[:, 0]).astype(bf16)
+    key_rows = mixed[:, :, 1].astype(bf16)
+    value_rows = (mixed[:, :, 2] + own_qv[:, 1]).astype(bf16)
+    scores = jnp.einsum("qhd,khd->hqk", queries, key_rows, preferred_element_type=f32) * factor
+    scores = jnp.where(allowed[None], scores, masked_score)
+    weights = jnp.exp(scores - jnp.max(scores, axis=2, keepdims=True))
+    probs = weights / jnp.sum(weights, axis=2, keepdims=True)
+    low_probs = probs.astype(bf16)
+    attended = jnp.einsum("hqk,khd->qhd", low_probs, value_rows, preferred_element_type=f32)
+    attended = attended.astype(bf16).reshape(length, heads * HEAD)
+    branch = total_plane(product(attended, out_flat, False).astype(bf16), 3)
+    residual = inputs + (branch.astype(f32) + branch_bias)
+    center2, inverse2 = norm_stats(residual)
+    standard2 = (residual - center2) * inverse2
+    normed2 = (standard2 * gain2 + shift2).astype(bf16)
+    up_sums = product(normed2, up_flat, False) + own_up_bias
+    hidden = gelu_tanh(up_sums).astype(bf16)
+    d_hidden = product(cot_all, down_flat, True)
+    d_upper = jax.vjp(gelu_tanh, up_sums)[1](d_hidden)[0].astype(bf16)
+
+    parts = 4
+    piece = hidden_count // parts
+    down_grads, up_grads = [], []
+    for part in range(parts):
+        grad = outer_sum(hidden[:, part * piece : (part + 1) * piece], cot_all).astype(bf16)
+        grad = shift_rows(jnp.moveaxis(grad.reshape(piece, row_count, width), 1, 0))
+        down_grads.append(dp_total(grad))
+    for part in range(parts):
+        grad = outer_sum(normed2, d_upper[:, part * piece : (part + 1) * piece]).astype(bf16)
+        up_grads.append(dp_total(shift_rows(grad.reshape(row_count, width, piece))))
+
+    d_normed2 = total_plane(product(d_upper, up_flat, True).astype(bf16), 4).astype(f32)
+    scaled = d_normed2 * gain2
+    d_residual = cot_all.astype(f32) + inverse2 * (
+        scaled
+        - jnp.mean(scaled, axis=1, keepdims=True)
+        - standard2 * jnp.mean(scaled * standard2, axis=1, keepdims=True)
+    )
+    d_branch = d_residual.astype(bf16)
+    out_grad = outer_sum(attended, d_branch).astype(bf16)
+    out_grad = dp_total(shift_rows(jnp.moveaxis(out_grad.reshape(heads * HEAD, row_count, width), 1, 0)))
+    d_attended = product(d_branch, out_flat, True).astype(bf16).reshape(length, heads, HEAD)
+    d_probs = jnp.einsum("qhd,khd->hqk", d_attended, value_rows, preferred_element_type=f32)
+    dots = jnp.sum(probs * d_probs, axis=2, keepdims=True)
+    d_scores = (probs * (d_probs - dots)).astype(bf16)
+    d_query = jnp.einsum("hqk,khd->qhd", d_scores, key_rows, preferred_element_type=f32) * factor
+    d_key = jnp.einsum("hqk,qhd->khd", d_scores, queries, preferred_element_type=f32) * factor
+    d_value = jnp.einsum("hqk,qhd->khd", low_probs, d_attended, preferred_element_type=f32)
+    d_mixed = jnp.stack([d_query, d_key, d_value], axis=2).astype(bf16)
+    d_flat = d_mixed.reshape(length, heads * 3 * HEAD)
+    qkv_grads = []
+    for head in range(heads):
+        grad = outer_sum(normed1, d_flat[:, head * 3 * HEAD : (head + 1) * 3 * HEAD]).astype(bf16)
+        qkv_grads.append(dp_total(shift_rows(grad.reshape(row_count, width, 3 * HEAD))))
+    d_normed1 = reduce_plane(product(d_flat, qkv_flat, True).astype(bf16), 5)
+
+    standard1 = own((inputs - center1) * inverse1)
+    own_inverse1 = lax.dynamic_slice_in_dim(inverse1, col * rows, rows, 0)
+    d_norm1, gain1_grad, shift1_grad = norm_backward(
+        d_normed1, standard1, own_inverse1[:, 0], ln1_gain
+    )
+    tokens_grad = (own(d_residual) + d_norm1).astype(bf16)
+    sums_out = reduce_plane(product(hidden, down_flat, False).astype(bf16), 6)
+    output = (own(residual) + (sums_out + down_bias)).astype(bf16)
+
+    own_n2 = own_width(d_normed2)
+    near = [
+        jnp.sum(own_n2 * own_width(standard2), axis=0),
+        jnp.sum(own_n2, axis=0),
+        jnp.sum(own_width(d_branch), axis=0, dtype=f32),
+        jnp.sum(own_width(cot_all), axis=0, dtype=f32),
+    ]
+    totals = jnp.sum(d_mixed, axis=0, dtype=f32)
+    spread_sums = [
+        jnp.sum(d_upper, axis=0, dtype=f32),
+        jnp.stack([totals[:, 0], totals[:, 2]], axis=1).reshape(heads * 2 * HEAD),
+    ]
+    slots = [lax.dynamic_update_index_in_dim(jnp.zeros((row_count,) + v.shape, f32), v, row, 0) for v in spread_sums]
+    own_slots = [lax.dynamic_update_index_in_dim(jnp.zeros((row_count,) + v.shape, f32), v, row, 0) for v in near]
+    summed = lax.psum(jnp.concatenate(slots + own_slots, axis=1), ("dp", "row"))
+    up_bias_grad = summed[:, :hidden_count].reshape(-1)
+    begin = hidden_count + heads * 2 * HEAD
+    qv_bias_grad = summed[:, hidden_count:begin].reshape(row_count * heads, 2, HEAD)
+    mine = lax.dynamic_index_in_dim(summed[:, begin:], row, 0, keepdims=False).reshape(4, width)
+    norm1_sums = lax.psum((gain1_grad, shift1_grad), ("dp", "col"))
+
+    down_weight_grad = jnp.stack(down_grads, axis=1).reshape(row_count * hidden_count, width).astype(f32)
+    up_weight_grad = jnp.stack(up_grads, axis=1).transpose(2, 0, 1, 3).reshape(width, row_count * hidden_count)
+    qkv_weight_grad = jnp.stack(qkv_grads, axis=1).transpose(2, 0, 1, 3)
+    return (
+        output,
+        tokens_grad,
+        norm1_sums[0],
+        norm1_sums[1],
+        qkv_weight_grad.reshape(width, row_count * heads, 3, HEAD).astype(f32),
+        qv_bias_grad,
+        out_grad.reshape(row_count * heads, HEAD, width).astype(f32),
+        mine[2],
+        mine[0],
+        mine[1],
+        up_weight_grad.astype(f32),
+        up_bias_grad,
+        down_weight_grad,
+        mine[3],
+    )
+
+
 def solution(mesh):
+    sizes = dict(mesh.shape)
+    flat = sizes == {"dp": 4, "row": 4, "col": 2}
+    per_device = plane_plan if flat else general_plan
     placed = (
         P(("dp", "col"), "row"),
         P("row"),

time: 1880 us -> 1250 us (0.66)
  waiting for transfers between devices: 1550 us -> 402 us
  Pallas kernels: 0 us -> 218 us
  starting transfers between devices: 12.8 us -> 137 us
  local copies, waits for them, and re-layouts: 58.2 us -> 172 us
  other arithmetic: 34 us -> 79.9 us
  blocking collectives: 90.9 us -> 121 us
    psum x1 -> x0, waiting for transfers between devices: 775 us -> none  [per_device(): lax.psum((qkv_grad, qv_bias_grad, out_grad, out_bias_grad, up_grad, up_bi...]
    all_gather x13 -> x0, waiting for transfers between devices: 574 us -> none  [the longest x5 220 us: gather_rows(): return lax.all_gather(block_data, 'row', axis=0, tiled=True)]
    ppermute x0 -> x78, waiting for transfers between devices: none -> 402 us  [the longest x11 195 us: dp_total(): back = lax.ppermute(total, 'dp', [(1, 0), (2, 3)])]
    pallas_call x0 -> x6, Pallas kernels: none -> 218 us  [the longest x2 108 us: total_plane(): pl.pallas_call(total_kernel, out_shape=jax.ShapeDtypeStruct(part.shape, p...]
    reduce_scatter x5 -> x0, waiting for transfers between devices: 179 us -> none  [the longest x1 97.5 us: per_device(): lax.psum_scatter(d_pairs, 'row', scatter_dimension=0, tiled=True)]
    ppermute x0 -> x78, starting transfers between devices: none -> 137 us  [the longest x11 74.6 us: dp_total(): came = lax.ppermute(share, 'dp', [(0, 1), (3, 2)])]
    convert_element_type x6 -> x32, other arithmetic: 11.3 us -> 51.4 us  [the longest x11 9.91 us: dp_total(): half = (share.astype(f32) + came.astype(f32)).astype(share.dtype)]
    dynamic_update_slice x0 -> x47, local copies, waits for them, and re-layouts: none -> 36.6 us  [the longest x41 36.4 us: shift_rows(): lax.dynamic_update_slice_in_dim(result, got, (row + count - step) % count...]
  transfers between devices with their start and end apart: 22 -> 78, of which waited for: 19 -> 29; matrix products, arithmetic and copies ran while one was open for 6% -> 27% of each run, Pallas kernels for 0% -> 18%
where the time goes in v1:
time: 1250 us; the launch traced here: 1240 us
  waiting for transfers between devices  402 us (32%)
  Pallas kernels  218 us (17%)
  local copies, waits for them, and re-layouts  172 us (14%)
  starting transfers between devices  137 us (11%)
  blocking collectives  121 us (10%)
  matrix products  104 us (8%)
  other arithmetic  79.9 us (6%)
    ppermute x11, waiting for transfers between devices, dp_total(): back = lax.ppermute(total, 'dp', [(1, 0), (2, 3)])  195 us
    ppermute x11, waiting for transfers between devices, dp_total(): came = lax.ppermute(share, 'dp', [(0, 1), (3, 2)])  115 us
    pallas_call x2, Pallas kernels, total_plane(): pl.pallas_call(total_kernel, out_shape=jax.ShapeDtypeStruct(part.shape, p...  108 us
    ppermute x45, waiting for transfers between devices, shift_rows(): got = lax.ppermute(sent, 'row', pairs)  93.1 us
    ppermute x11, starting transfers between devices, dp_total(): came = lax.ppermute(share, 'dp', [(0, 1), (3, 2)])  74.6 us
    psum x1, blocking collectives, plane_plan(): summed = lax.psum(jnp.concatenate(slots + own_slots, axis=1), ('dp', 'row'))  61.1 us
    pallas_call x2, Pallas kernels, reduce_plane(): pl.pallas_call(reduce_kernel, out_shape=jax.ShapeDtypeStruct((rows, width...  56.8 us
    pallas_call x2, Pallas kernels, gather_plane(): pl.pallas_call(gather_kernel, out_shape=jax.ShapeDtypeStruct((2 * rows, 4...  53.1 us
  transfers between devices with their start and end apart: 78, of which 29 were waited for; matrix products, arithmetic and copies ran while one was open for 27% of the time, Pallas kernels for 18%

profile of v1, /device:TPU:0, one launch (start us, length us, event | category | flops | bytes accessed | tf_op | source)
XLA Modules:
  0.0 1237.0 jit_solution(8531562776525607037)
XLA Ops:
  1.9 4.4 copy.363
  6.8 4.9 copy.238
  19.4 35.8 %all_gather.3 = f32[2048,5]{0,1:T(8,128)S(1)} all-gather(f32[512,5]{0,1:T(8,128)S(1)} %bitcast.285), channel_id=1, replica_groups=mesh['dp'=4,'row'=4,'col'=2] {'row'}, dimensions={0}, use_global_device_ids=true | all-gather | bytes 51200 | tf_op jit(solution)/shard_map/all_gather | solution.py:580
  55.3 25.4 %shard_map.254 = bf16[1024,2048]{1,0:T(8,128)(2,1)} custom-call(bf16[512,512]{1,0:T(8,128)(2,1)S(1)} %copy-done), custom_call_target="tpu_custom_call" | custom-call | tf_op jit(solution)/shard_map/pallas_call | solution.py:434
  84.2 6.5 copy.244
  90.7 7.1 fusion.1
  101.0 3.6 dynamic-slice_bitcast_fusion
  106.6 27.7 %shard_map.257 = bf16[1024,2048]{1,0:T(8,128)(2,1)} custom-call(bf16[512,512]{1,0:T(8,128)(2,1)S(1)} %copy-done.1), custom_call_target="tpu_custom_call" | custom-call | tf_op jit(solution)/shard_map/pallas_call | solution.py:434
  155.7 6.5 fusion.10
  162.2 8.5 fusion.67
  170.7 4.6 fusion.28
  179.5 59.7 %shard_map.255 = bf16[1024,2048]{1,0:T(8,128)(2,1)} custom-call(bf16[1024,2048]{1,0:T(8,128)(2,1)} %convolution_convert_fusion.part_ref), custom_call_target="tpu_custom_call" | custom-call | tf_op jit(solution)/shard_map/pallas_call | solution.py:502
  239.2 3.7 fusion.62
  243.0 5.8 add_convert_fusion
  256.8 6.7 copy.245
  263.5 10.9 multiply_convert_fusion.1
  283.7 4.6 convolution_convert_fusion.9
  289.7 4.6 convolution_convert_fusion.8
  296.6 3.7 constant_dynamic-slice_fusion.35
  328.5 27.8 %collective-permute-done.73 = bf16[1,256,512]{2,1,0:T(8,128)(2,1)S(1)} collective-permute-done((bf16[1,256,512]{2,1,0:T(8,128)(2,1)}, bf16[1,256,512]{2,1,0:T(8,128)(2,1)S(1)}, u32[]{:S(2)}, u32[]{:S(2)}) %collective-permute-start.73) | collective-permute-done | bytes 262176 | tf_op jit(solution)/shard_map/ppermute | solution.py:514
  371.7 4.5 collective-permute-start.63
  387.3 6.3 copy.246
  393.6 9.5 convolution_convert_fusion.3.part_ref
  403.1 7.9 convert_reduce_fusion.1
  411.0 6.5 convolution_convert_fusion.2.part_ref
  426.0 48.5 %shard_map.258 = bf16[1024,2048]{1,0:T(8,128)(2,1)} custom-call(bf16[1024,2048]{1,0:T(8,128)(2,1)} %convolution_convert_fusion.2.part_ref), custom_call_target="tpu_custom_call" | custom-call | tf_op jit(solution)/shard_map/pallas_call | solution.py:502
  474.6 6.7 convert_element_type.378
  482.9 5.0 fusion.63
  492.3 5.1 fusion.23
  510.7 3.6 convolution_convert_fusion.5
  528.9 6.4 convolution_convert_fusion.1.part_ref
  535.4 25.8 %shard_map.259 = f32[512,512]{1,0:T(8,128)S(1)} custom-call(bf16[1024,2048]{1,0:T(8,128)(2,1)} %convolution_convert_fusion.1.part_ref), custom_call_target="tpu_custom_call" | custom-call | tf_op jit(solution)/shard_map/pallas_call | solution.py:486
  566.0 6.2 all-reduce.1
  572.3 31.0 %shard_map.256 = f32[512,512]{1,0:T(8,128)S(1)} custom-call(bf16[1024,2048]{1,0:T(8,128)(2,1)} %convolution_convert_fusion.3.part_ref), custom_call_target="tpu_custom_call" | custom-call | tf_op jit(solution)/shard_map/pallas_call | solution.py:486
  603.3 61.1 %psum.39 = f32[4,3584]{1,0:T(4,128)S(1)} all-reduce(f32[4,3584]{1,0:T(4,128)S(1)} %constant_dynamic-update-slice_fusion.45), channel_id=1, replica_groups=mesh['dp'=4,'row'=4,'col'=2] {'dp','row'}, use_global_device_ids=true, to_apply=%region_24.25 | all-reduce | flops 14336 | bytes 114688 | tf_op jit(solution)/shard_map/psum | solution.py:685
  675.4 18.1 %all-reduce = (f32[512]{0:T(512)}, f32[512]{0:T(512)}) all-reduce(f32[512]{0:T(512)S(1)} %get-tuple-element.126, f32[512]{0:T(512)S(1)} %get-tuple-element.137), channel_id=1, replica_groups=mesh['dp'=4,'row'=4,'col'=2] {'dp','col'}, use_global_device_ids=true, to_apply=%region_15.16 | all-reduce | flops 1024 | bytes 8192 | tf_op jit(solution)/shard_map/psum | solution.py:690
  711.1 4.4 collective-permute-done.25
  721.2 3.9 collective-permute-done.18
  725.7 7.9 collective-permute-done.12
  733.6 4.4 collective-permute-done.19
  738.4 4.9 collective-permute-start.38
  743.3 11.6 collective-permute-done.13
  756.0 7.9 collective-permute-done.43
  764.4 7.5 collective-permute-done.37
  789.2 17.2 %collective-permute-start.15 = (bf16[4,512,384]{1,2,0:T(8,128)(2,1)S(1)}, bf16[4,512,384]{1,2,0:T(8,128)(2,1)S(1)}, u32[]{:S(2)}, u32[]{:S(2)}) collective-permute-start(bf16[4,512,384]{1,2,0:T(8,128)(2,1)S(1)} %constant_dynamic-update-slice_fusion.29), channel_id=1, source_target_pairs={{0,8},{24,16},{1,9},{25,17},{2,10},{26,18},{3,11},{27,19},{4,12},{... | collective-permute-start | bytes 4718600 | tf_op jit(solution)/shard_map/ppermute | solution.py:523
  806.8 22.1 %collective-permute-start.51 = (bf16[4,512,256]{2,1,0:T(8,128)(2,1)S(1)}, bf16[4,512,256]{2,1,0:T(8,128)(2,1)S(1)}, u32[]{:S(2)}, u32[]{:S(2)}) collective-permute-start(bf16[4,512,256]{2,1,0:T(8,128)(2,1)S(1)} %constant_dynamic-update-slice_fusion.11), channel_id=1, source_target_pairs={{0,8},{24,16},{1,9},{25,17},{2,10},{26,18},{3,11},{27,19},{4,12},{... | collective-permute-start | bytes 3145736 | tf_op jit(solution)/shard_map/ppermute | solution.py:523
  829.2 16.7 %collective-permute-start.39 = (bf16[4,512,256]{2,1,0:T(8,128)(2,1)S(1)}, bf16[4,512,256]{2,1,0:T(8,128)(2,1)S(1)}, u32[]{:S(2)}, u32[]{:S(2)}) collective-permute-start(bf16[4,512,256]{2,1,0:T(8,128)(2,1)S(1)} %constant_dynamic-update-slice_fusion.17), channel_id=1, source_target_pairs={{0,8},{24,16},{1,9},{25,17},{2,10},{26,18},{3,11},{27,19},{4,12},{... | collective-permute-start | bytes 3145736 | tf_op jit(solution)/shard_map/ppermute | solution.py:523
  849.6 39.9 %collective-permute-done.51 = bf16[4,512,256]{2,1,0:T(8,128)(2,1)S(1)} collective-permute-done((bf16[4,512,256]{2,1,0:T(8,128)(2,1)S(1)}, bf16[4,512,256]{2,1,0:T(8,128)(2,1)S(1)}, u32[]{:S(2)}, u32[]{:S(2)}) %collective-permute-start.51) | collective-permute-done | bytes 1048608 | tf_op jit(solution)/shard_map/ppermute | solution.py:523
  891.5 20.5 %collective-permute-done.39 = bf16[4,512,256]{2,1,0:T(8,128)(2,1)S(1)} collective-permute-done((bf16[4,512,256]{2,1,0:T(8,128)(2,1)S(1)}, bf16[4,512,256]{2,1,0:T(8,128)(2,1)S(1)}, u32[]{:S(2)}, u32[]{:S(2)}) %collective-permute-start.39) | collective-permute-done | bytes 1048608 | tf_op jit(solution)/shard_map/ppermute | solution.py:523
  913.6 54.1 %collective-permute-done.45 = bf16[4,512,256]{2,1,0:T(8,128)(2,1)S(1)} collective-permute-done((bf16[4,512,256]{2,1,0:T(8,128)(2,1)S(1)}, bf16[4,512,256]{2,1,0:T(8,128)(2,1)S(1)}, u32[]{:S(2)}, u32[]{:S(2)}) %collective-permute-start.45) | collective-permute-done | bytes 1048608 | tf_op jit(solution)/shard_map/ppermute | solution.py:523
  975.7 19.8 %collective-permute-done.77 = bf16[4,256,512]{2,1,0:T(8,128)(2,1)S(1)} collective-permute-done((bf16[4,256,512]{2,1,0:T(8,128)(2,1)S(1)}, bf16[4,256,512]{2,1,0:T(8,128)(2,1)S(1)}, u32[]{:S(2)}, u32[]{:S(2)}) %collective-permute-start.77) | collective-permute-done | bytes 1048608 | tf_op jit(solution)/shard_map/ppermute | solution.py:527
  996.4 20.3 %collective-permute-done.71 = bf16[4,256,512]{2,1,0:T(8,128)(2,1)S(1)} collective-permute-done((bf16[4,256,512]{2,1,0:T(8,128)(2,1)S(1)}, bf16[4,256,512]{2,1,0:T(8,128)(2,1)S(1)}, u32[]{:S(2)}, u32[]{:S(2)}) %collective-permute-start.71) | collective-permute-done | bytes 1048608 | tf_op jit(solution)/shard_map/ppermute | solution.py:527
  1020.3 4.4 copy.290
  1034.3 34.0 %collective-permute-done.29 = bf16[4,256,512]{2,1,0:T(8,128)(2,1)S(1)} collective-permute-done((bf16[4,256,512]{2,1,0:T(8,128)(2,1)S(1)}, bf16[4,256,512]{2,1,0:T(8,128)(2,1)S(1)}, u32[]{:S(2)}, u32[]{:S(2)}) %collective-permute-start.29) | collective-permute-done | bytes 1048608 | tf_op jit(solution)/shard_map/ppermute | solution.py:527
  1074.8 15.9 %collective-permute-done.35 = bf16[4,512,256]{2,1,0:T(8,128)(2,1)S(1)} collective-permute-done((bf16[4,512,256]{2,1,0:T(8,128)(2,1)S(1)}, bf16[4,512,256]{2,1,0:T(8,128)(2,1)S(1)}, u32[]{:S(2)}, u32[]{:S(2)}) %collective-permute-start.35) | collective-permute-done | bytes 1048608 | tf_op jit(solution)/shard_map/ppermute | solution.py:527
  1092.3 24.8 %collective-permute-done.53 = bf16[4,512,256]{2,1,0:T(8,128)(2,1)S(1)} collective-permute-done((bf16[4,512,256]{2,1,0:T(8,128)(2,1)S(1)}, bf16[4,512,256]{2,1,0:T(8,128)(2,1)S(1)}, u32[]{:S(2)}, u32[]{:S(2)}) %collective-permute-start.53) | collective-permute-done | bytes 1048608 | tf_op jit(solution)/shard_map/ppermute | solution.py:527
  1117.2 22.4 %collective-permute-done.41 = bf16[4,512,256]{2,1,0:T(8,128)(2,1)S(1)} collective-permute-done((bf16[4,512,256]{2,1,0:T(8,128)(2,1)S(1)}, bf16[4,512,256]{2,1,0:T(8,128)(2,1)S(1)}, u32[]{:S(2)}, u32[]{:S(2)}) %collective-permute-start.41) | collective-permute-done | bytes 1048608 | tf_op jit(solution)/shard_map/ppermute | solution.py:527
  1139.7 18.5 %collective-permute-done.47 = bf16[4,512,256]{2,1,0:T(8,128)(2,1)S(1)} collective-permute-done((bf16[4,512,256]{2,1,0:T(8,128)(2,1)S(1)}, bf16[4,512,256]{2,1,0:T(8,128)(2,1)S(1)}, u32[]{:S(2)}, u32[]{:S(2)}) %collective-permute-start.47) | collective-permute-done | bytes 1048608 | tf_op jit(solution)/shard_map/ppermute | solution.py:527
  1158.3 3.8 convert_bitcast_fusion
  1162.0 12.1 copy.269
  1174.2 10.7 reshape.461
  1184.9 9.2 collective-permute-done.17
  1195.7 30.0 %collective-permute-done.23 = bf16[4,512,384]{1,2,0:T(8,128)(2,1)} collective-permute-done((bf16[4,512,384]{1,2,0:T(8,128)(2,1)S(1)}, bf16[4,512,384]{1,2,0:T(8,128)(2,1)}, u32[]{:S(2)}, u32[]{:S(2)}) %collective-permute-start.23) | collective-permute-done | bytes 1572896 | tf_op jit(solution)/shard_map/ppermute | solution.py:527
  1230.2 6.6 copy.291
  (431 shorter events, 264.2 us)
Async XLA Ops:
  6.3 93.3 %collective-permute-start.3 = (bf16[1,256,512]{2,1,0:T(8,128)(2,1)S(1)}, bf16[1,256,512]{2,1,0:T(8,128)(2,1)S(1)}, u32[]{:S(2)}, u32[]{:S(2)}) collective-permute-start(bf16[1,256,512]{2,1,0:T(8,128)(2,1)S(1)} %constant_dynamic-slice_fusion.40), channel_id=1, source_target_pairs={{0,2},{2,4},{4,6},{6,0},{1,3},{3,5},{5,7},{7,1},{8,10},{10,12},{12... | collective-permute-start | bytes 786440 | tf_op jit(solution)/shard_map/ppermute | solution.py:514
  14.9 133.6 %collective-permute-start.2 = (bf16[1,512,768]{1,2,0:T(8,128)(2,1)}, bf16[1,512,768]{1,2,0:T(8,128)(2,1)}, u32[]{:S(2)}, u32[]{:S(2)}) collective-permute-start(bf16[1,512,768]{1,2,0:T(8,128)(2,1)} %get-tuple-element.157), channel_id=1, source_target_pairs={{0,6},{2,0},{4,2},{6,4},{1,7},{3,1},{5,3},{7,5},{8,14},{10,8},{12,... | collective-permute-start | bytes 2359304 | tf_op jit(solution)/shard_map/ppermute | solution.py:514
  16.9 129.2 %collective-permute-start.1 = (bf16[1,512,768]{1,2,0:T(8,128)(2,1)}, bf16[1,512,768]{1,2,0:T(8,128)(2,1)}, u32[]{:S(2)}, u32[]{:S(2)}) collective-permute-start(bf16[1,512,768]{1,2,0:T(8,128)(2,1)} %get-tuple-element.158), channel_id=1, source_target_pairs={{0,4},{2,6},{4,0},{6,2},{1,5},{3,7},{5,1},{7,3},{8,12},{10,14},{12... | collective-permute-start | bytes 2359304 | tf_op jit(solution)/shard_map/ppermute | solution.py:514
  19.1 125.8 %collective-permute-start = (bf16[1,512,768]{1,2,0:T(8,128)(2,1)}, bf16[1,512,768]{1,2,0:T(8,128)(2,1)}, u32[]{:S(2)}, u32[]{:S(2)}) collective-permute-start(bf16[1,512,768]{1,2,0:T(8,128)(2,1)} %get-tuple-element.159), channel_id=1, source_target_pairs={{0,2},{2,4},{4,6},{6,0},{1,3},{3,5},{5,7},{7,1},{8,10},{10,12},{12... | collective-permute-start | bytes 2359304 | tf_op jit(solution)/shard_map/ppermute | solution.py:514
  100.5 37.7 %collective-permute-start.4 = (bf16[1,256,512]{2,1,0:T(8,128)(2,1)}, bf16[1,256,512]{2,1,0:T(8,128)(2,1)S(1)}, u32[]{:S(2)}, u32[]{:S(2)}) collective-permute-start(bf16[1,256,512]{2,1,0:T(8,128)(2,1)} %get-tuple-element.194), channel_id=1, source_target_pairs={{0,4},{2,6},{4,0},{6,2},{1,5},{3,7},{5,1},{7,3},{8,12},{10,14},{12... | collective-permute-start | bytes 786440 | tf_op jit(solution)/shard_map/ppermute | solution.py:514
  104.7 35.0 %collective-permute-start.5 = (bf16[1,256,512]{2,1,0:T(8,128)(2,1)}, bf16[1,256,512]{2,1,0:T(8,128)(2,1)}, u32[]{:S(2)}, u32[]{:S(2)}) collective-permute-start(bf16[1,256,512]{2,1,0:T(8,128)(2,1)} %get-tuple-element.193), channel_id=1, source_target_pairs={{0,6},{2,0},{4,2},{6,4},{1,7},{3,1},{5,3},{7,5},{8,14},{10,8},{12,... | collective-permute-start | bytes 786440 | tf_op jit(solution)/shard_map/ppermute | solution.py:514
  138.2 116.4 %collective-permute-start.8 = (bf16[1,512,1024]{1,2,0:T(8,128)(2,1)}, bf16[1,512,1024]{1,2,0:T(8,128)(2,1)}, u32[]{:S(2)}, u32[]{:S(2)}) collective-permute-start(bf16[1,512,1024]{1,2,0:T(8,128)(2,1)} %get-tuple-element.154), channel_id=1, source_target_pairs={{0,6},{2,0},{4,2},{6,4},{1,7},{3,1},{5,3},{7,5},{8,14},{10,8},{12,... | collective-permute-start | bytes 3145736 | tf_op jit(solution)/shard_map/ppermute | solution.py:514
  139.7 112.6 %collective-permute-start.7 = (bf16[1,512,1024]{1,2,0:T(8,128)(2,1)}, bf16[1,512,1024]{1,2,0:T(8,128)(2,1)}, u32[]{:S(2)}, u32[]{:S(2)}) collective-permute-start(bf16[1,512,1024]{1,2,0:T(8,128)(2,1)} %get-tuple-element.155), channel_id=1, source_target_pairs={{0,4},{2,6},{4,0},{6,2},{1,5},{3,7},{5,1},{7,3},{8,12},{10,14},{12... | collective-permute-start | bytes 3145736 | tf_op jit(solution)/shard_map/ppermute | solution.py:514
  144.9 105.1 %collective-permute-start.6 = (bf16[1,512,1024]{1,2,0:T(8,128)(2,1)}, bf16[1,512,1024]{1,2,0:T(8,128)(2,1)}, u32[]{:S(2)}, u32[]{:S(2)}) collective-permute-start(bf16[1,512,1024]{1,2,0:T(8,128)(2,1)} %get-tuple-element.156), channel_id=1, source_target_pairs={{0,2},{2,4},{4,6},{6,0},{1,3},{3,5},{5,7},{7,1},{8,10},{10,12},{12... | collective-permute-start | bytes 3145736 | tf_op jit(solution)/shard_map/ppermute | solution.py:514
  146.1 150.5 %collective-permute-start.9 = (bf16[1,1024,512]{2,1,0:T(8,128)(2,1)}, bf16[1,1024,512]{2,1,0:T(8,128)(2,1)}, u32[]{:S(2)}, u32[]{:S(2)}) collective-permute-start(bf16[1,1024,512]{2,1,0:T(8,128)(2,1)} %constant_dynamic-slice_fusion.37), channel_id=1, source_target_pairs={{0,2},{2,4},{4,6},{6,0},{1,3},{3,5},{5,7},{7,1},{8,10},{10,12},{12... | collective-permute-start | bytes 3145736 | tf_op jit(solution)/shard_map/ppermute | solution.py:514
  281.5 42.3 %collective-permute-start.67 = (bf16[1,256,512]{2,1,0:T(8,128)(2,1)}, bf16[1,256,512]{2,1,0:T(8,128)(2,1)}, u32[]{:S(2)}, u32[]{:S(2)}) collective-permute-start(bf16[1,256,512]{2,1,0:T(8,128)(2,1)} %bitcast.97), channel_id=1, source_target_pairs={{0,4},{2,6},{4,0},{6,2},{1,5},{3,7},{5,1},{7,3},{8,12},{10,14},{12... | collective-permute-start | bytes 786440 | tf_op jit(solution)/shard_map/ppermute | solution.py:514
  282.2 39.1 %collective-permute-start.66 = (bf16[1,256,512]{2,1,0:T(8,128)(2,1)}, bf16[1,256,512]{2,1,0:T(8,128)(2,1)}, u32[]{:S(2)}, u32[]{:S(2)}) collective-permute-start(bf16[1,256,512]{2,1,0:T(8,128)(2,1)} %bitcast.96), channel_id=1, source_target_pairs={{0,2},{2,4},{4,6},{6,0},{1,3},{3,5},{5,7},{7,1},{8,10},{10,12},{12... | collective-permute-start | bytes 786440 | tf_op jit(solution)/shard_map/ppermute | solution.py:514
  282.2 43.3 %collective-permute-start.72 = (bf16[1,256,512]{2,1,0:T(8,128)(2,1)}, bf16[1,256,512]{2,1,0:T(8,128)(2,1)}, u32[]{:S(2)}, u32[]{:S(2)}) collective-permute-start(bf16[1,256,512]{2,1,0:T(8,128)(2,1)} %bitcast.102), channel_id=1, source_target_pairs={{0,2},{2,4},{4,6},{6,0},{1,3},{3,5},{5,7},{7,1},{8,10},{10,12},{12... | collective-permute-start | bytes 786440 | tf_op jit(solution)/shard_map/ppermute | solution.py:514
  307.9 78.4 %collective-permute-start.11 = (bf16[1,1024,512]{2,1,0:T(8,128)(2,1)}, bf16[1,1024,512]{2,1,0:T(8,128)(2,1)S(1)}, u32[]{:S(2)}, u32[]{:S(2)}) collective-permute-start(bf16[1,1024,512]{2,1,0:T(8,128)(2,1)} %get-tuple-element.151), channel_id=1, source_target_pairs={{0,6},{2,0},{4,2},{6,4},{1,7},{3,1},{5,3},{7,5},{8,14},{10,8},{12,... | collective-permute-start | bytes 3145736 | tf_op jit(solution)/shard_map/ppermute | solution.py:514
  308.3 74.6 %collective-permute-start.10 = (bf16[1,1024,512]{2,1,0:T(8,128)(2,1)}, bf16[1,1024,512]{2,1,0:T(8,128)(2,1)S(1)}, u32[]{:S(2)}, u32[]{:S(2)}) collective-permute-start(bf16[1,1024,512]{2,1,0:T(8,128)(2,1)} %get-tuple-element.152), channel_id=1, source_target_pairs={{0,4},{2,6},{4,0},{6,2},{1,5},{3,7},{5,1},{7,3},{8,12},{10,14},{12... | collective-permute-start | bytes 3145736 | tf_op jit(solution)/shard_map/ppermute | solution.py:514
  321.3 34.9 %collective-permute-start.73 = (bf16[1,256,512]{2,1,0:T(8,128)(2,1)}, bf16[1,256,512]{2,1,0:T(8,128)(2,1)S(1)}, u32[]{:S(2)}, u32[]{:S(2)}) collective-permute-start(bf16[1,256,512]{2,1,0:T(8,128)(2,1)} %bitcast.280), channel_id=1, source_target_pairs={{0,4},{2,6},{4,0},{6,2},{1,5},{3,7},{5,1},{7,3},{8,12},{10,14},{12... | collective-permute-start | bytes 786440 | tf_op jit(solution)/shard_map/ppermute | solution.py:514
  323.8 33.2 %collective-permute-start.54 = (bf16[1,256,512]{2,1,0:T(8,128)(2,1)}, bf16[1,256,512]{2,1,0:T(8,128)(2,1)S(1)}, u32[]{:S(2)}, u32[]{:S(2)}) collective-permute-start(bf16[1,256,512]{2,1,0:T(8,128)(2,1)} %bitcast.281), channel_id=1, source_target_pairs={{0,2},{2,4},{4,6},{6,0},{1,3},{3,5},{5,7},{7,1},{8,10},{10,12},{12... | collective-permute-start | bytes 786440 | tf_op jit(solution)/shard_map/ppermute | solution.py:514
  325.5 33.6 %collective-permute-start.55 = (bf16[1,256,512]{2,1,0:T(8,128)(2,1)}, bf16[1,256,512]{2,1,0:T(8,128)(2,1)S(1)}, u32[]{:S(2)}, u32[]{:S(2)}) collective-permute-start(bf16[1,256,512]{2,1,0:T(8,128)(2,1)} %bitcast.279), channel_id=1, source_target_pairs={{0,4},{2,6},{4,0},{6,2},{1,5},{3,7},{5,1},{7,3},{8,12},{10,14},{12... | collective-permute-start | bytes 786440 | tf_op jit(solution)/shard_map/ppermute | solution.py:514
  371.7 324.5 %collective-permute-start.63 = (bf16[4,256,512]{2,1,0:T(8,128)(2,1)}, bf16[4,256,512]{2,1,0:T(8,128)(2,1)}, u32[]{:S(2)}, u32[]{:S(2)}) collective-permute-start(bf16[4,256,512]{2,1,0:T(8,128)(2,1)} %constant_dynamic-update-slice_fusion.5), channel_id=1, source_target_pairs={{0,8},{24,16},{1,9},{25,17},{2,10},{26,18},{3,11},{27,19},{4,12},{... | collective-permute-start | bytes 3145736 | tf_op jit(solution)/shard_map/ppermute | solution.py:523
  376.9 321.3 %collective-permute-start.57 = (bf16[4,256,512]{2,1,0:T(8,128)(2,1)}, bf16[4,256,512]{2,1,0:T(8,128)(2,1)}, u32[]{:S(2)}, u32[]{:S(2)}) collective-permute-start(bf16[4,256,512]{2,1,0:T(8,128)(2,1)} %constant_dynamic-update-slice_fusion.8), channel_id=1, source_target_pairs={{0,8},{24,16},{1,9},{25,17},{2,10},{26,18},{3,11},{27,19},{4,12},{... | collective-permute-start | bytes 3145736 | tf_op jit(solution)/shard_map/ppermute | solution.py:523
  379.9 320.3 %collective-permute-start.75 = (bf16[4,256,512]{2,1,0:T(8,128)(2,1)}, bf16[4,256,512]{2,1,0:T(8,128)(2,1)}, u32[]{:S(2)}, u32[]{:S(2)}) collective-permute-start(bf16[4,256,512]{2,1,0:T(8,128)(2,1)} %constant_dynamic-update-slice_fusion.32), channel_id=1, source_target_pairs={{0,8},{24,16},{1,9},{25,17},{2,10},{26,18},{3,11},{27,19},{4,12},{... | collective-permute-start | bytes 3145736 | tf_op jit(solution)/shard_map/ppermute | solution.py:523
  382.9 319.4 %collective-permute-start.69 = (bf16[4,256,512]{2,1,0:T(8,128)(2,1)}, bf16[4,256,512]{2,1,0:T(8,128)(2,1)}, u32[]{:S(2)}, u32[]{:S(2)}) collective-permute-start(bf16[4,256,512]{2,1,0:T(8,128)(2,1)} %constant_dynamic-update-slice_fusion.2), channel_id=1, source_target_pairs={{0,8},{24,16},{1,9},{25,17},{2,10},{26,18},{3,11},{27,19},{4,12},{... | collective-permute-start | bytes 3145736 | tf_op jit(solution)/shard_map/ppermute | solution.py:523
  668.7 37.6 %collective-permute-start.42 = (bf16[1,512,256]{2,1,0:T(8,128)(2,1)}, bf16[1,512,256]{2,1,0:T(8,128)(2,1)}, u32[]{:S(2)}, u32[]{:S(2)}) collective-permute-start(bf16[1,512,256]{2,1,0:T(8,128)(2,1)} %constant_dynamic-slice_fusion.19), channel_id=1, source_target_pairs={{0,2},{2,4},{4,6},{6,0},{1,3},{3,5},{5,7},{7,1},{8,10},{10,12},{12... | collective-permute-start | bytes 786440 | tf_op jit(solution)/shard_map/ppermute | solution.py:514
  696.2 11.6 collective-permute-start.36
  709.3 29.1 %collective-permute-start.20 = (bf16[1,512,384]{1,2,0:T(8,128)(2,1)S(1)}, bf16[1,512,384]{1,2,0:T(8,128)(2,1)S(1)}, u32[]{:S(2)}, u32[]{:S(2)}) collective-permute-start(bf16[1,512,384]{1,2,0:T(8,128)(2,1)S(1)} %copy-done.31), channel_id=1, source_target_pairs={{0,6},{2,0},{4,2},{6,4},{1,7},{3,1},{5,3},{7,5},{8,14},{10,8},{12,... | collective-permute-start | bytes 1179656 | tf_op jit(solution)/shard_map/ppermute | solution.py:514
  709.8 15.4 %collective-permute-start.18 = (bf16[1,512,384]{1,2,0:T(8,128)(2,1)S(1)}, bf16[1,512,384]{1,2,0:T(8,128)(2,1)S(1)}, u32[]{:S(2)}, u32[]{:S(2)}) collective-permute-start(bf16[1,512,384]{1,2,0:T(8,128)(2,1)S(1)} %copy-done.33), channel_id=1, source_target_pairs={{0,2},{2,4},{4,6},{6,0},{1,3},{3,5},{5,7},{7,1},{8,10},{10,12},{12... | collective-permute-start | bytes 1179656 | tf_op jit(solution)/shard_map/ppermute | solution.py:514
  711.1 22.5 %collective-permute-start.12 = (bf16[1,512,384]{1,2,0:T(8,128)(2,1)S(1)}, bf16[1,512,384]{1,2,0:T(8,128)(2,1)S(1)}, u32[]{:S(2)}, u32[]{:S(2)}) collective-permute-start(bf16[1,512,384]{1,2,0:T(8,128)(2,1)S(1)} %get-tuple-element.162), channel_id=1, source_target_pairs={{0,2},{2,4},{4,6},{6,0},{1,3},{3,5},{5,7},{7,1},{8,10},{10,12},{12... | collective-permute-start | bytes 1179656 | tf_op jit(solution)/shard_map/ppermute | solution.py:514
  715.6 22.5 %collective-permute-start.19 = (bf16[1,512,384]{1,2,0:T(8,128)(2,1)S(1)}, bf16[1,512,384]{1,2,0:T(8,128)(2,1)S(1)}, u32[]{:S(2)}, u32[]{:S(2)}) collective-permute-start(bf16[1,512,384]{1,2,0:T(8,128)(2,1)S(1)} %copy-done.32), channel_id=1, source_target_pairs={{0,4},{2,6},{4,0},{6,2},{1,5},{3,7},{5,1},{7,3},{8,12},{10,14},{12... | collective-permute-start | bytes 1179656 | tf_op jit(solution)/shard_map/ppermute | solution.py:514
  719.0 36.2 %collective-permute-start.14 = (bf16[1,512,384]{1,2,0:T(8,128)(2,1)S(1)}, bf16[1,512,384]{1,2,0:T(8,128)(2,1)S(1)}, u32[]{:S(2)}, u32[]{:S(2)}) collective-permute-start(bf16[1,512,384]{1,2,0:T(8,128)(2,1)S(1)} %get-tuple-element.160), channel_id=1, source_target_pairs={{0,6},{2,0},{4,2},{6,4},{1,7},{3,1},{5,3},{7,5},{8,14},{10,8},{12,... | collective-permute-start | bytes 1179656 | tf_op jit(solution)/shard_map/ppermute | solution.py:514
  725.2 29.7 %collective-permute-start.13 = (bf16[1,512,384]{1,2,0:T(8,128)(2,1)S(1)}, bf16[1,512,384]{1,2,0:T(8,128)(2,1)S(1)}, u32[]{:S(2)}, u32[]{:S(2)}) collective-permute-start(bf16[1,512,384]{1,2,0:T(8,128)(2,1)S(1)} %get-tuple-element.161), channel_id=1, source_target_pairs={{0,4},{2,6},{4,0},{6,2},{1,5},{3,7},{5,1},{7,3},{8,12},{10,14},{12... | collective-permute-start | bytes 1179656 | tf_op jit(solution)/shard_map/ppermute | solution.py:514
  733.6 30.3 %collective-permute-start.44 = (bf16[1,512,256]{2,1,0:T(8,128)(2,1)S(1)}, bf16[1,512,256]{2,1,0:T(8,128)(2,1)S(1)}, u32[]{:S(2)}, u32[]{:S(2)}) collective-permute-start(bf16[1,512,256]{2,1,0:T(8,128)(2,1)S(1)} %get-tuple-element.184), channel_id=1, source_target_pairs={{0,6},{2,0},{4,2},{6,4},{1,7},{3,1},{5,3},{7,5},{8,14},{10,8},{12,... | collective-permute-start | bytes 786440 | tf_op jit(solution)/shard_map/ppermute | solution.py:514
  738.0 25.9 %collective-permute-start.43 = (bf16[1,512,256]{2,1,0:T(8,128)(2,1)S(1)}, bf16[1,512,256]{2,1,0:T(8,128)(2,1)S(1)}, u32[]{:S(2)}, u32[]{:S(2)}) collective-permute-start(bf16[1,512,256]{2,1,0:T(8,128)(2,1)S(1)} %get-tuple-element.185), channel_id=1, source_target_pairs={{0,4},{2,6},{4,0},{6,2},{1,5},{3,7},{5,1},{7,3},{8,12},{10,14},{12... | collective-permute-start | bytes 786440 | tf_op jit(solution)/shard_map/ppermute | solution.py:514
  738.4 34.3 %collective-permute-start.38 = (bf16[1,512,256]{2,1,0:T(8,128)(2,1)S(1)}, bf16[1,512,256]{2,1,0:T(8,128)(2,1)S(1)}, u32[]{:S(2)}, u32[]{:S(2)}) collective-permute-start(bf16[1,512,256]{2,1,0:T(8,128)(2,1)S(1)} %get-tuple-element.181), channel_id=1, source_target_pairs={{0,6},{2,0},{4,2},{6,4},{1,7},{3,1},{5,3},{7,5},{8,14},{10,8},{12,... | collective-permute-start | bytes 786440 | tf_op jit(solution)/shard_map/ppermute | solution.py:514
  754.9 17.0 %collective-permute-start.37 = (bf16[1,512,256]{2,1,0:T(8,128)(2,1)S(1)}, bf16[1,512,256]{2,1,0:T(8,128)(2,1)S(1)}, u32[]{:S(2)}, u32[]{:S(2)}) collective-permute-start(bf16[1,512,256]{2,1,0:T(8,128)(2,1)S(1)} %get-tuple-element.182), channel_id=1, source_target_pairs={{0,4},{2,6},{4,0},{6,2},{1,5},{3,7},{5,1},{7,3},{8,12},{10,14},{12... | collective-permute-start | bytes 786440 | tf_op jit(solution)/shard_map/ppermute | solution.py:514
  755.2 32.3 %collective-permute-start.64 = (bf16[4,256,512]{2,1,0:T(8,128)(2,1)S(1)}, bf16[4,256,512]{2,1,0:T(8,128)(2,1)S(1)}, u32[]{:S(2)}, u32[]{:S(2)}) collective-permute-start(bf16[4,256,512]{2,1,0:T(8,128)(2,1)S(1)} %add_convert_fusion.11), channel_id=1, source_target_pairs={{8,16},{16,8},{9,17},{17,9},{10,18},{18,10},{11,19},{19,11},{12,20... | collective-permute-start | bytes 3145736 | tf_op jit(solution)/shard_map/ppermute | solution.py:525
  763.9 16.8 %collective-permute-start.49 = (bf16[1,512,256]{2,1,0:T(8,128)(2,1)S(1)}, bf16[1,512,256]{2,1,0:T(8,128)(2,1)S(1)}, u32[]{:S(2)}, u32[]{:S(2)}) collective-permute-start(bf16[1,512,256]{2,1,0:T(8,128)(2,1)S(1)} %get-tuple-element.188), channel_id=1, source_target_pairs={{0,4},{2,6},{4,0},{6,2},{1,5},{3,7},{5,1},{7,3},{8,12},{10,14},{12... | collective-permute-start | bytes 786440 | tf_op jit(solution)/shard_map/ppermute | solution.py:514
  771.9 17.3 %collective-permute-start.58 = (bf16[4,256,512]{2,1,0:T(8,128)(2,1)S(1)}, bf16[4,256,512]{2,1,0:T(8,128)(2,1)S(1)}, u32[]{:S(2)}, u32[]{:S(2)}) collective-permute-start(bf16[4,256,512]{2,1,0:T(8,128)(2,1)S(1)} %add_convert_fusion.13), channel_id=1, source_target_pairs={{8,16},{16,8},{9,17},{17,9},{10,18},{18,10},{11,19},{19,11},{12,20... | collective-permute-start | bytes 3145736 | tf_op jit(solution)/shard_map/ppermute | solution.py:525
  780.7 26.0 %collective-permute-start.76 = (bf16[4,256,512]{2,1,0:T(8,128)(2,1)S(1)}, bf16[4,256,512]{2,1,0:T(8,128)(2,1)S(1)}, u32[]{:S(2)}, u32[]{:S(2)}) collective-permute-start(bf16[4,256,512]{2,1,0:T(8,128)(2,1)S(1)} %add_convert_fusion.7), channel_id=1, source_target_pairs={{8,16},{16,8},{9,17},{17,9},{10,18},{18,10},{11,19},{19,11},{12,20... | collective-permute-start | bytes 3145736 | tf_op jit(solution)/shard_map/ppermute | solution.py:525
  783.6 45.6 %collective-permute-start.70 = (bf16[4,256,512]{2,1,0:T(8,128)(2,1)S(1)}, bf16[4,256,512]{2,1,0:T(8,128)(2,1)S(1)}, u32[]{:S(2)}, u32[]{:S(2)}) collective-permute-start(bf16[4,256,512]{2,1,0:T(8,128)(2,1)S(1)} %add_convert_fusion.9), channel_id=1, source_target_pairs={{8,16},{16,8},{9,17},{17,9},{10,18},{18,10},{11,19},{19,11},{12,20... | collective-permute-start | bytes 3145736 | tf_op jit(solution)/shard_map/ppermute | solution.py:525
  784.3 61.9 %collective-permute-start.27 = (bf16[4,256,512]{2,1,0:T(8,128)(2,1)S(1)}, bf16[4,256,512]{2,1,0:T(8,128)(2,1)S(1)}, u32[]{:S(2)}, u32[]{:S(2)}) collective-permute-start(bf16[4,256,512]{2,1,0:T(8,128)(2,1)S(1)} %constant_dynamic-update-slice_fusion.23), channel_id=1, source_target_pairs={{0,8},{24,16},{1,9},{25,17},{2,10},{26,18},{3,11},{27,19},{4,12},{... | collective-permute-start | bytes 3145736 | tf_op jit(solution)/shard_map/ppermute | solution.py:523
  787.5 60.1 %collective-permute-start.33 = (bf16[4,512,256]{2,1,0:T(8,128)(2,1)S(1)}, bf16[4,512,256]{2,1,0:T(8,128)(2,1)S(1)}, u32[]{:S(2)}, u32[]{:S(2)}) collective-permute-start(bf16[4,512,256]{2,1,0:T(8,128)(2,1)S(1)} %constant_dynamic-update-slice_fusion.20), channel_id=1, source_target_pairs={{0,8},{24,16},{1,9},{25,17},{2,10},{26,18},{3,11},{27,19},{4,12},{... | collective-permute-start | bytes 3145736 | tf_op jit(solution)/shard_map/ppermute | solution.py:523
  789.2 180.0 %collective-permute-start.15 = (bf16[4,512,384]{1,2,0:T(8,128)(2,1)S(1)}, bf16[4,512,384]{1,2,0:T(8,128)(2,1)S(1)}, u32[]{:S(2)}, u32[]{:S(2)}) collective-permute-start(bf16[4,512,384]{1,2,0:T(8,128)(2,1)S(1)} %constant_dynamic-update-slice_fusion.29), channel_id=1, source_target_pairs={{0,8},{24,16},{1,9},{25,17},{2,10},{26,18},{3,11},{27,19},{4,12},{... | collective-permute-start | bytes 4718600 | tf_op jit(solution)/shard_map/ppermute | solution.py:523
  806.8 82.7 %collective-permute-start.51 = (bf16[4,512,256]{2,1,0:T(8,128)(2,1)S(1)}, bf16[4,512,256]{2,1,0:T(8,128)(2,1)S(1)}, u32[]{:S(2)}, u32[]{:S(2)}) collective-permute-start(bf16[4,512,256]{2,1,0:T(8,128)(2,1)S(1)} %constant_dynamic-update-slice_fusion.11), channel_id=1, source_target_pairs={{0,8},{24,16},{1,9},{25,17},{2,10},{26,18},{3,11},{27,19},{4,12},{... | collective-permute-start | bytes 3145736 | tf_op jit(solution)/shard_map/ppermute | solution.py:523
  829.2 82.8 %collective-permute-start.39 = (bf16[4,512,256]{2,1,0:T(8,128)(2,1)S(1)}, bf16[4,512,256]{2,1,0:T(8,128)(2,1)S(1)}, u32[]{:S(2)}, u32[]{:S(2)}) collective-permute-start(bf16[4,512,256]{2,1,0:T(8,128)(2,1)S(1)} %constant_dynamic-update-slice_fusion.17), channel_id=1, source_target_pairs={{0,8},{24,16},{1,9},{25,17},{2,10},{26,18},{3,11},{27,19},{4,12},{... | collective-permute-start | bytes 3145736 | tf_op jit(solution)/shard_map/ppermute | solution.py:523
  846.2 124.8 %collective-permute-start.21 = (bf16[4,512,384]{1,2,0:T(8,128)(2,1)S(1)}, bf16[4,512,384]{1,2,0:T(8,128)(2,1)S(1)}, u32[]{:S(2)}, u32[]{:S(2)}) collective-permute-start(bf16[4,512,384]{1,2,0:T(8,128)(2,1)S(1)} %constant_dynamic-update-slice_fusion.26), channel_id=1, source_target_pairs={{0,8},{24,16},{1,9},{25,17},{2,10},{26,18},{3,11},{27,19},{4,12},{... | collective-permute-start | bytes 4718600 | tf_op jit(solution)/shard_map/ppermute | solution.py:523
  847.6 120.0 %collective-permute-start.45 = (bf16[4,512,256]{2,1,0:T(8,128)(2,1)S(1)}, bf16[4,512,256]{2,1,0:T(8,128)(2,1)S(1)}, u32[]{:S(2)}, u32[]{:S(2)}) collective-permute-start(bf16[4,512,256]{2,1,0:T(8,128)(2,1)S(1)} %constant_dynamic-update-slice_fusion.14), channel_id=1, source_target_pairs={{0,8},{24,16},{1,9},{25,17},{2,10},{26,18},{3,11},{27,19},{4,12},{... | collective-permute-start | bytes 3145736 | tf_op jit(solution)/shard_map/ppermute | solution.py:523
  889.5 82.7 %collective-permute-start.65 = (bf16[4,256,512]{2,1,0:T(8,128)(2,1)S(1)}, bf16[4,256,512]{2,1,0:T(8,128)(2,1)S(1)}, u32[]{:S(2)}, u32[]{:S(2)}) collective-permute-start(bf16[4,256,512]{2,1,0:T(8,128)(2,1)S(1)} %add_convert_fusion.10), channel_id=1, source_target_pairs={{8,0},{16,24},{9,1},{17,25},{10,2},{18,26},{11,3},{19,27},{12,4},{... | collective-permute-start | bytes 3145736 | tf_op jit(solution)/shard_map/ppermute | solution.py:527
  912.0 62.0 %collective-permute-start.59 = (bf16[4,256,512]{2,1,0:T(8,128)(2,1)S(1)}, bf16[4,256,512]{2,1,0:T(8,128)(2,1)S(1)}, u32[]{:S(2)}, u32[]{:S(2)}) collective-permute-start(bf16[4,256,512]{2,1,0:T(8,128)(2,1)S(1)} %add_convert_fusion.12), channel_id=1, source_target_pairs={{8,0},{16,24},{9,1},{17,25},{10,2},{18,26},{11,3},{19,27},{12,4},{... | collective-permute-start | bytes 3145736 | tf_op jit(solution)/shard_map/ppermute | solution.py:527
  967.6 28.0 %collective-permute-start.77 = (bf16[4,256,512]{2,1,0:T(8,128)(2,1)S(1)}, bf16[4,256,512]{2,1,0:T(8,128)(2,1)S(1)}, u32[]{:S(2)}, u32[]{:S(2)}) collective-permute-start(bf16[4,256,512]{2,1,0:T(8,128)(2,1)S(1)} %add_convert_fusion.6), channel_id=1, source_target_pairs={{8,0},{16,24},{9,1},{17,25},{10,2},{18,26},{11,3},{19,27},{12,4},{... | collective-permute-start | bytes 3145736 | tf_op jit(solution)/shard_map/ppermute | solution.py:527
  969.2 47.5 %collective-permute-start.71 = (bf16[4,256,512]{2,1,0:T(8,128)(2,1)S(1)}, bf16[4,256,512]{2,1,0:T(8,128)(2,1)S(1)}, u32[]{:S(2)}, u32[]{:S(2)}) collective-permute-start(bf16[4,256,512]{2,1,0:T(8,128)(2,1)S(1)} %add_convert_fusion.8), channel_id=1, source_target_pairs={{8,0},{16,24},{9,1},{17,25},{10,2},{18,26},{11,3},{19,27},{12,4},{... | collective-permute-start | bytes 3145736 | tf_op jit(solution)/shard_map/ppermute | solution.py:527
  971.0 48.2 %collective-permute-start.28 = (bf16[4,256,512]{2,1,0:T(8,128)(2,1)S(1)}, bf16[4,256,512]{2,1,0:T(8,128)(2,1)S(1)}, u32[]{:S(2)}, u32[]{:S(2)}) collective-permute-start(bf16[4,256,512]{2,1,0:T(8,128)(2,1)S(1)} %add_convert_fusion.23), channel_id=1, source_target_pairs={{8,16},{16,8},{9,17},{17,9},{10,18},{18,10},{11,19},{19,11},{12,20... | collective-permute-start | bytes 3145736 | tf_op jit(solution)/shard_map/ppermute | solution.py:525
  972.2 52.5 %collective-permute-start.34 = (bf16[4,512,256]{2,1,0:T(8,128)(2,1)S(1)}, bf16[4,512,256]{2,1,0:T(8,128)(2,1)}, u32[]{:S(2)}, u32[]{:S(2)}) collective-permute-start(bf16[4,512,256]{2,1,0:T(8,128)(2,1)S(1)} %add_convert_fusion.21), channel_id=1, source_target_pairs={{8,16},{16,8},{9,17},{17,9},{10,18},{18,10},{11,19},{19,11},{12,20... | collective-permute-start | bytes 3145736 | tf_op jit(solution)/shard_map/ppermute | solution.py:525
  974.0 51.5 %collective-permute-start.52 = (bf16[4,512,256]{2,1,0:T(8,128)(2,1)S(1)}, bf16[4,512,256]{2,1,0:T(8,128)(2,1)}, u32[]{:S(2)}, u32[]{:S(2)}) collective-permute-start(bf16[4,512,256]{2,1,0:T(8,128)(2,1)S(1)} %add_convert_fusion.15), channel_id=1, source_target_pairs={{8,16},{16,8},{9,17},{17,9},{10,18},{18,10},{11,19},{19,11},{12,20... | collective-permute-start | bytes 3145736 | tf_op jit(solution)/shard_map/ppermute | solution.py:525
  995.6 34.3 %collective-permute-start.40 = (bf16[4,512,256]{2,1,0:T(8,128)(2,1)S(1)}, bf16[4,512,256]{2,1,0:T(8,128)(2,1)S(1)}, u32[]{:S(2)}, u32[]{:S(2)}) collective-permute-start(bf16[4,512,256]{2,1,0:T(8,128)(2,1)S(1)} %add_convert_fusion.19), channel_id=1, source_target_pairs={{8,16},{16,8},{9,17},{17,9},{10,18},{18,10},{11,19},{19,11},{12,20... | collective-permute-start | bytes 3145736 | tf_op jit(solution)/shard_map/ppermute | solution.py:525
  1016.7 14.7 %collective-permute-start.46 = (bf16[4,512,256]{2,1,0:T(8,128)(2,1)S(1)}, bf16[4,512,256]{2,1,0:T(8,128)(2,1)}, u32[]{:S(2)}, u32[]{:S(2)}) collective-permute-start(bf16[4,512,256]{2,1,0:T(8,128)(2,1)S(1)} %add_convert_fusion.17), channel_id=1, source_target_pairs={{8,16},{16,8},{9,17},{17,9},{10,18},{18,10},{11,19},{19,11},{12,20... | collective-permute-start | bytes 3145736 | tf_op jit(solution)/shard_map/ppermute | solution.py:525
  1019.2 52.1 %collective-permute-start.16 = (bf16[4,512,384]{1,2,0:T(8,128)(2,1)S(1)}, bf16[4,512,384]{1,2,0:T(8,128)(2,1)S(1)}, u32[]{:S(2)}, u32[]{:S(2)}) collective-permute-start(bf16[4,512,384]{1,2,0:T(8,128)(2,1)S(1)} %add_convert_fusion.5), channel_id=1, source_target_pairs={{8,16},{16,8},{9,17},{17,9},{10,18},{18,10},{11,19},{19,11},{12,20... | collective-permute-start | bytes 4718600 | tf_op jit(solution)/shard_map/ppermute | solution.py:525
  1024.7 48.3 %collective-permute-start.22 = (bf16[4,512,384]{1,2,0:T(8,128)(2,1)S(1)}, bf16[4,512,384]{1,2,0:T(8,128)(2,1)S(1)}, u32[]{:S(2)}, u32[]{:S(2)}) collective-permute-start(bf16[4,512,384]{1,2,0:T(8,128)(2,1)S(1)} %add_convert_fusion.3), channel_id=1, source_target_pairs={{8,16},{16,8},{9,17},{17,9},{10,18},{18,10},{11,19},{19,11},{12,20... | collective-permute-start | bytes 4718600 | tf_op jit(solution)/shard_map/ppermute | solution.py:525
  1025.5 42.8 %collective-permute-start.29 = (bf16[4,256,512]{2,1,0:T(8,128)(2,1)S(1)}, bf16[4,256,512]{2,1,0:T(8,128)(2,1)S(1)}, u32[]{:S(2)}, u32[]{:S(2)}) collective-permute-start(bf16[4,256,512]{2,1,0:T(8,128)(2,1)S(1)} %add_convert_fusion.22), channel_id=1, source_target_pairs={{8,0},{16,24},{9,1},{17,25},{10,2},{18,26},{11,3},{19,27},{12,4},{... | collective-permute-start | bytes 3145736 | tf_op jit(solution)/shard_map/ppermute | solution.py:527
  1029.9 60.9 %collective-permute-start.35 = (bf16[4,512,256]{2,1,0:T(8,128)(2,1)S(1)}, bf16[4,512,256]{2,1,0:T(8,128)(2,1)S(1)}, u32[]{:S(2)}, u32[]{:S(2)}) collective-permute-start(bf16[4,512,256]{2,1,0:T(8,128)(2,1)S(1)} %add_convert_fusion.20), channel_id=1, source_target_pairs={{8,0},{16,24},{9,1},{17,25},{10,2},{18,26},{11,3},{19,27},{12,4},{... | collective-permute-start | bytes 3145736 | tf_op jit(solution)/shard_map/ppermute | solution.py:527
  1031.5 85.6 %collective-permute-start.53 = (bf16[4,512,256]{2,1,0:T(8,128)(2,1)S(1)}, bf16[4,512,256]{2,1,0:T(8,128)(2,1)S(1)}, u32[]{:S(2)}, u32[]{:S(2)}) collective-permute-start(bf16[4,512,256]{2,1,0:T(8,128)(2,1)S(1)} %add_convert_fusion.14), channel_id=1, source_target_pairs={{8,0},{16,24},{9,1},{17,25},{10,2},{18,26},{11,3},{19,27},{12,4},{... | collective-permute-start | bytes 3145736 | tf_op jit(solution)/shard_map/ppermute | solution.py:527
  1068.3 71.3 %collective-permute-start.41 = (bf16[4,512,256]{2,1,0:T(8,128)(2,1)S(1)}, bf16[4,512,256]{2,1,0:T(8,128)(2,1)S(1)}, u32[]{:S(2)}, u32[]{:S(2)}) collective-permute-start(bf16[4,512,256]{2,1,0:T(8,128)(2,1)S(1)} %add_convert_fusion.18), channel_id=1, source_target_pairs={{8,0},{16,24},{9,1},{17,25},{10,2},{18,26},{11,3},{19,27},{12,4},{... | collective-permute-start | bytes 3145736 | tf_op jit(solution)/shard_map/ppermute | solution.py:527
  1071.3 86.9 %collective-permute-start.47 = (bf16[4,512,256]{2,1,0:T(8,128)(2,1)S(1)}, bf16[4,512,256]{2,1,0:T(8,128)(2,1)S(1)}, u32[]{:S(2)}, u32[]{:S(2)}) collective-permute-start(bf16[4,512,256]{2,1,0:T(8,128)(2,1)S(1)} %add_convert_fusion.16), channel_id=1, source_target_pairs={{8,0},{16,24},{9,1},{17,25},{10,2},{18,26},{11,3},{19,27},{12,4},{... | collective-permute-start | bytes 3145736 | tf_op jit(solution)/shard_map/ppermute | solution.py:527
  1073.1 121.0 %collective-permute-start.17 = (bf16[4,512,384]{1,2,0:T(8,128)(2,1)S(1)}, bf16[4,512,384]{1,2,0:T(8,128)(2,1)}, u32[]{:S(2)}, u32[]{:S(2)}) collective-permute-start(bf16[4,512,384]{1,2,0:T(8,128)(2,1)S(1)} %add_convert_fusion.4), channel_id=1, source_target_pairs={{8,0},{16,24},{9,1},{17,25},{10,2},{18,26},{11,3},{19,27},{12,4},{... | collective-permute-start | bytes 4718600 | tf_op jit(solution)/shard_map/ppermute | solution.py:527
  1090.7 134.9 %collective-permute-start.23 = (bf16[4,512,384]{1,2,0:T(8,128)(2,1)S(1)}, bf16[4,512,384]{1,2,0:T(8,128)(2,1)}, u32[]{:S(2)}, u32[]{:S(2)}) collective-permute-start(bf16[4,512,384]{1,2,0:T(8,128)(2,1)S(1)} %add_convert_fusion.2), channel_id=1, source_target_pairs={{8,0},{16,24},{9,1},{17,25},{10,2},{18,26},{11,3},{19,27},{12,4},{... | collective-permute-start | bytes 4718600 | tf_op jit(solution)/shard_map/ppermute | solution.py:527
  (68 other events, 1019.0 us)

commit v2 on v1

--- a/solution.py
+++ b/solution.py
@@ -505,6 +505,611 @@
         compiler_params=pltpu.CompilerParams(collective_id=cid, has_side_effects=True, vmem_limit_bytes=50<<20))(part)
 
 
+def put(ref_from, ref_to, sends, recvs, at, partner):
+    return pltpu.make_async_remote_copy(
+        src_ref=ref_from,
+        dst_ref=ref_to,
+        send_sem=sends.at[at],
+        recv_sem=recvs.at[at],
+        device_id=partner,
+        device_id_type=MESH,
+    )
+
+
+def strip(begin, count):
+    return pl.ds(pl.multiple_of(begin, count), count)
+
+
+def dot_nt(left, right):
+    return lax.dot_general(left, right, (((1,), (1,)), ((), ())), preferred_element_type=jnp.float32)
+
+
+def dot_tn(left, right):
+    return lax.dot_general(left, right, (((0,), (0,)), ((), ())), preferred_element_type=jnp.float32)
+
+
+def tiled_nt(left, right, target, inner, tile_rows, tile_cols):
+    rows, cols = target.shape
+    across = cols // tile_cols
+
+    def step(at, none):
+        down, side = at // across, at % across
+        value = dot_nt(left[strip(down * tile_rows, tile_rows), :inner], right[strip(side * tile_cols, tile_cols), :inner])
+        target[strip(down * tile_rows, tile_rows), strip(side * tile_cols, tile_cols)] = value.astype(target.dtype)
+        return none
+
+    lax.fori_loop(0, (rows // tile_rows) * across, step, 0)
+
+
+def tiled_nn(left, right, target, tile_rows, tile_cols):
+    rows, cols = target.shape
+    across = cols // tile_cols
+
+    def step(at, none):
+        down, side = at // across, at % across
+        value = jnp.dot(
+            left[strip(down * tile_rows, tile_rows), :],
+            right[:, strip(side * tile_cols, tile_cols)],
+            preferred_element_type=jnp.float32,
+        )
+        target[strip(down * tile_rows, tile_rows), strip(side * tile_cols, tile_cols)] = value.astype(target.dtype)
+        return none
+
+    lax.fori_loop(0, (rows // tile_rows) * across, step, 0)
+
+
+def reduce_steps(part, result, got, keep, diag, half_x, half_y, to_send, from_xy, sends, recvs, base):
+    f32 = jnp.float32
+    rows, width = result.shape
+    half = rows // 2
+    low, high = pl.ds(0, half), pl.ds(half, half)
+    col, side, core = places()
+    to_x, to_y, to_core = partners()
+    spots = ((1 - col, 1 - side), (col, 1 - side), (1 - col, side), (col, side))
+    copies = [
+        put(block(part, a, b, 1 - core, rows, width), got.at[k], sends, recvs, base + k, to_core)
+        for k, (a, b) in enumerate(spots)
+    ]
+    for copy in copies:
+        copy.start()
+    mine = [block(part, a, b, core, rows, width) for a, b in spots]
+    dx = put(diag.at[low], half_x, sends, recvs, base + 4, to_x)
+    dy = put(diag.at[high], half_y, sends, recvs, base + 5, to_y)
+    cy = put(to_send.at[0], from_xy.at[0], sends, recvs, base + 6, to_y)
+    cx = put(to_send.at[1], from_xy.at[1], sends, recvs, base + 7, to_x)
+    yield
+    copies[0].wait_recv()
+    diag[...] = (mine[0][...].astype(f32) + got[0].astype(f32)).astype(diag.dtype)
+    dx.start()
+    dy.start()
+    copies[1].wait_recv()
+    copies[2].wait_recv()
+    to_send[0, high] = (mine[1][high].astype(f32) + got[1, high].astype(f32)).astype(diag.dtype)
+    to_send[1, low] = (mine[2][low].astype(f32) + got[2, low].astype(f32)).astype(diag.dtype)
+    copies[3].wait_recv()
+    keep[...] = mine[3][...].astype(f32) + got[3].astype(f32)
+    yield
+    dx.wait_recv()
+    to_send[0, low] = (mine[1][low].astype(f32) + got[1, low].astype(f32) + half_x[...].astype(f32)).astype(diag.dtype)
+    cy.start()
+    dy.wait_recv()
+    to_send[1, high] = (mine[2][high].astype(f32) + got[2, high].astype(f32) + half_y[...].astype(f32)).astype(
+        diag.dtype
+    )
+    cx.start()
+    yield
+    cy.wait_recv()
+    cx.wait_recv()
+    result[...] = keep[...] + from_xy[0].astype(f32) + from_xy[1].astype(f32)
+    for copy in copies + [dx, dy, cy, cx]:
+        copy.wait_send()
+
+
+def spread_steps(out, rows, width, sends, recvs, base):
+    col, side, core = places()
+    to_x, to_y, to_core = partners()
+
+    def copy_of(at, which, partner, part=None):
+        ref = block(out, *which, rows, width, part)
+        return put(ref, ref, sends, recvs, base + at, partner)
+
+    own, ox, oy, od = (col, side, core), (1 - col, side, core), (col, 1 - side, core), (1 - col, 1 - side, core)
+    plan = [
+        copy_of(0, own, to_x),
+        copy_of(1, own, to_y),
+        copy_of(2, own, to_core),
+        copy_of(3, ox, to_y, 0),
+        copy_of(4, oy, to_x, 1),
+        copy_of(5, ox, to_core),
+        copy_of(6, oy, to_core),
+        copy_of(7, od, to_core),
+    ]
+    for at in (0, 1, 2):
+        plan[at].start()
+    yield
+    plan[0].wait_recv()
+    plan[3].start()
+    plan[1].wait_recv()
+    plan[4].start()
+    plan[5].start()
+    plan[6].start()
+    yield
+    plan[3].wait_recv()
+    plan[4].wait_recv()
+    plan[7].start()
+    yield
+    for at in (2, 5, 6, 7):
+        plan[at].wait_recv()
+    for copy in plan:
+        copy.wait_send()
+
+
+CHUNK = 256
+
+
+def backward_kernel(
+    counts,
+    hid_h,
+    cot_h,
+    dup_h,
+    n2_h,
+    upw_h,
+    std_h,
+    n1_h,
+    qkvw_h,
+    downw_h,
+    attended,
+    outw,
+    mixed,
+    lse,
+    bias,
+    inv2,
+    gain2,
+    down_out,
+    up_out,
+    out_out,
+    qkv_out,
+    r_land,
+    m_land,
+    b_land,
+    dres_own,
+    dn1_own,
+    outp_own,
+    sums,
+    mixed_sums,
+    cot,
+    n2,
+    std,
+    part,
+    tot,
+    upw,
+    hid,
+    dup,
+    d_att,
+    d_mix,
+    dk_acc,
+    dv_acc,
+    g,
+    s,
+    ld,
+    t,
+    got_a,
+    diag_a,
+    hx_a,
+    hy_a,
+    ts_a,
+    fx_a,
+    got_b,
+    diag_b,
+    hx_b,
+    hy_b,
+    ts_b,
+    fx_b,
+    keep,
+    load_sem,
+    ld_sem,
+    own_sem,
+    z_send,
+    z_recv,
+    a_send,
+    a_recv,
+    p_send,
+    p_recv,
+):
+    f32, bf16 = jnp.float32, jnp.bfloat16
+    n_down, n_up, n_out, n_qkv = counts
+    total = sum(counts)
+    plane, row, col = lax.axis_index("dp"), lax.axis_index("row"), lax.axis_index("col")
+    length, full = cot.shape
+    rows, width = dres_own.shape
+    row_count = full // width
+    inner = (plane == 1) | (plane == 2)
+    outer = jnp.logical_not(inner)
+    to_inner = {"dp": plane // 3 + 1}
+    to_middle = {"dp": 3 - plane}
+    to_outer = {"dp": (plane - 1) * 3}
+    side, core = row // 2, row % 2
+
+    loads = [
+        (hid_h, hid),
+        (cot_h, cot),
+        (dup_h, dup),
+        (upw_h, upw),
+        (n2_h, n2),
+        (std_h, std),
+        (qkvw_h, upw.at[:, : qkvw_h.shape[1]]),
+        (n1_h, std),
+        (downw_h, n2),
+    ]
+    loads = [pltpu.make_async_copy(a, b, load_sem.at[k]) for k, (a, b) in enumerate(loads)]
+    for k in range(6):
+        loads[k].start()
+
+    barrier = pltpu.get_barrier_semaphore()
+    for partner in partners() + ({"row": (1 - side) * 2 + 1 - core},):
+        pl.semaphore_signal(barrier, inc=1, device_id=partner, device_id_type=MESH)
+
+    @pl.when(outer)
+    def _():
+        pl.semaphore_signal(barrier, inc=1, device_id=to_inner, device_id_type=MESH)
+        pl.semaphore_wait(barrier, 5)
+
+    @pl.when(inner)
+    def _():
+        pl.semaphore_signal(barrier, inc=1, device_id=to_middle, device_id_type=MESH)
+        pl.semaphore_signal(barrier, inc=1, device_id=to_outer, device_id_type=MESH)
+        pl.semaphore_wait(barrier, 6)
+
+    def place(i, source):
+        if i < n_down:
+            return down_out.at[:, strip(source * n_down * CHUNK + i * CHUNK, CHUNK), :]
+        i -= n_down
+        if i < n_up:
+            return up_out.at[:, :, strip(source * n_up * CHUNK + i * CHUNK, CHUNK)]
+        i -= n_up
+        if i < n_out:
+            return out_out.at[:, strip(source * n_out * CHUNK + i * CHUNK, CHUNK), :]
+        i -= n_out
+        return qkv_out.at[:, :, strip(source * n_qkv * CHUNK + i * CHUNK, CHUNK)]
+
+    g_slots, s_slots = g.shape[0], s.shape[0]
+
+    def inward(i):
+        return put(g.at[i % g_slots], r_land.at[i], z_send, z_recv, i, to_inner)
+
+    def across(i):
+        return put(s.at[i % s_slots], m_land.at[i], z_send, z_recv, total + i, to_middle)
+
+    def outward(i):
+        return put(t.at[i % s_slots], b_land.at[i], z_send, z_recv, 2 * total + i, to_outer)
+
+    def home(i, step, source):
+        target = (row + step) % row_count
+        return put(source.at[target], place(i, row), a_send, a_recv, 3 * i + step - 1, {"row": target})
+
+    def home_own(i, source):
+        return pltpu.make_async_copy(source.at[row], place(i, row), own_sem.at[i])
+
+    def send_home(i, source):
+        for step in range(1, row_count):
+            home(i, step, source).start()
+        home_own(i, source).start()
+
+    def sent_home(i, source):
+        for step in range(1, row_count):
+            home(i, step, source).wait_send()
+        home_own(i, source).wait()
+
+    def produce(i):
+        if i >= g_slots:
+
+            @pl.when(outer)
+            def _():
+                inward(i - g_slots).wait_send()
+
+        slot = g.at[i % g_slots]
+        if i < n_down or n_down + n_up <= i < n_down + n_up + n_out:
+            if i < n_down:
+                left, begin, right = hid, i * CHUNK, cot
+            else:
+                left, begin, right = attended, (i - n_down - n_up) * CHUNK, part
+
+            def step(k, none):
+                value = dot_tn(left[:, begin : begin + CHUNK], right[:, strip(k * width, width)]).astype(bf16)
+                slot[k, 0] = value[:, :CHUNK]
+                slot[k, 1] = value[:, CHUNK:]
+                return none
+        else:
+            if i < n_down + n_up:
+                left, right, begin = n2, dup, (i - n_down) * CHUNK
+            else:
+                left, right, begin = std, d_mix, (i - n_down - n_up - n_out) * CHUNK
+
+            def step(k, none):
+                value = dot_tn(left[:, strip(k * width, width)], right[:, begin : begin + CHUNK]).astype(bf16)
+                slot[k, 0] = value[:CHUNK]
+                slot[k, 1] = value[CHUNK:]
+                return none
+
+        lax.fori_loop(0, row_count, step, 0)
+
+        @pl.when(outer)
+        def _():
+            inward(i).start()
+
+    def add(first, target):
+        def step(k, none):
+            for half in range(2):
+                target[k, half] = (first[k, half].astype(f32) + ld[k, half].astype(f32)).astype(bf16)
+            return none
+
+        lax.fori_loop(0, row_count, step, 0)
+
+    def fetch(source):
+        copy = pltpu.make_async_copy(source, ld, ld_sem)
+        copy.start()
+        copy.wait()
+
+    def middle(i):
+        @pl.when(inner)
+        def _():
+            inward(i).wait_recv()
+            fetch(r_land.at[i])
+            add(g.at[i % g_slots], s.at[i % s_slots])
+            across(i).start()
+
+    def finish_inner(i):
+        @pl.when(inner)
+        def _():
+            if i >= s_slots:
+                outward(i - s_slots).wait_send()
+                sent_home(i - s_slots, t.at[i % s_slots])
+            across(i).wait_recv()
+            fetch(m_land.at[i])
+            add(s.at[i % s_slots], t.at[i % s_slots])
+            outward(i).start()
+            send_home(i, t.at[i % s_slots])
+            across(i).wait_send()
+
+    def finish_outer(i):
+        @pl.when(outer)
+        def _():
+            outward(i).wait_recv()
+            send_home(i, b_land.at[i])
+
+    def finish(i):
+        finish_inner(i)
+        if i >= 1:
+            finish_outer(i - 1)
+
+    set_a = (got_a, keep, diag_a, hx_a, hy_a, ts_a, fx_a)
+    set_b = (got_b, keep, diag_b, hx_b, hy_b, ts_b, fx_b)
+
+    loads[0].wait()
+    loads[1].wait()
+    produce(0)
+    produce(1)
+    loads[2].wait()
+    loads[3].wait()
+    tiled_nt(dup, upw, part, dup.shape[1], 1024, 256)
+    loads[6].start()
+    first = reduce_steps(part, outp_own, *set_a, p_send, p_recv, 0)
+    next(first)
+    next(first)
+    next(first)
+    loads[4].wait()
+    loads[5].wait()
+    middle(0)
+    produce(2)
+    next(first, None)
+    block(tot, col, side, core, rows, width)[...] = outp_own[...].astype(bf16)
+    second = spread_steps(tot, rows, width, p_send, p_recv, 8)
+    next(second)
+    next(second)
+    next(second)
+    middle(1)
+    produce(3)
+    finish(0)
+    next(second, None)
+
+    tile = 64
+    sums[...] = jnp.zeros_like(sums)
+
+    def norm_step(k, none):
+        at = strip(k * tile, tile)
+        grad, standard, inverse = tot[at, :].astype(f32), std[at, :].astype(f32), inv2[at, :]
+        scaled = grad * gain2[...]
+        mean_one = jnp.sum(scaled, axis=1, keepdims=True) / full
+        mean_two = jnp.sum(scaled * standard, axis=1, keepdims=True) / full
+        d_res = cot[at, :].astype(f32) + inverse * (scaled - mean_one - standard * mean_two)
+        low = d_res.astype(bf16)
+        part[at, :] = low
+        sums[0:1, :] += jnp.sum(grad * standard, axis=0, keepdims=True)
+        sums[1:2, :] += jnp.sum(grad, axis=0, keepdims=True)
+        sums[2:3, :] += jnp.sum(low.astype(f32), axis=0, keepdims=True)
+
+        @pl.when(k // (rows // tile) == col)
+        def _():
+            here = strip(row * width, width)
+            own = tot[at, here].astype(f32) * gain2[:, here]
+            dres_own[strip(k % (rows // tile) * tile, tile), :] = cot[at, here].astype(f32) + inverse * (
+                own - mean_one - std[at, here].astype(f32) * mean_two
+            )
+
+        return none
+
+    lax.fori_loop(0, length // tile, norm_step, 0)
+    loads[7].start()
+    tiled_nt(part, outw, d_att, full, 512, 256)
+    produce(4)
+    middle(2)
+    finish(1)
+
+    heads = mixed.shape[1] // (3 * HEAD)
+    factor = 1.0 / math.sqrt(HEAD)
+    blocks = length // SPAN
+
+    def head_step(head, none):
+        base = head * 3 * HEAD
+        at_q, at_k, at_v = strip(base, HEAD), strip(base + HEAD, HEAD), strip(base + 2 * HEAD, HEAD)
+        at_o = strip(head * HEAD, HEAD)
+        dk_acc[...] = jnp.zeros_like(dk_acc)
+        dv_acc[...] = jnp.zeros_like(dv_acc)
+        for k in range(blocks):
+            here = pl.ds(k * SPAN, SPAN)
+            seen = (k + 1) * SPAN
+            query, dout = mixed[here, at_q], d_att[here, at_o]
+            keys, values = mixed[:seen, at_k], mixed[:seen, at_v]
+            scores = dot_nt(query, keys) * factor
+            last = scores[:, seen - SPAN :] + bias[k]
+            scores = last if k == 0 else jnp.concatenate([scores[:, : seen - SPAN], last], axis=1)
+            probs = jnp.exp(scores - lse[head, here])
+            d_probs = dot_nt(dout, values)
+            dots = jnp.sum(probs * d_probs, axis=1, keepdims=True)
+            d_scores = (probs * (d_probs - dots)).astype(bf16)
+            d_mix[here, at_q] = (jnp.dot(d_scores, keys, preferred_element_type=f32) * factor).astype(bf16)
+            dk_acc[:seen] += dot_tn(d_scores, query)
+            dv_acc[:seen] += dot_tn(probs.astype(bf16), dout)
+        d_mix[:, at_k] = (dk_acc[...] * factor).astype(bf16)
+        d_mix[:, at_v] = dv_acc[...].astype(bf16)
+        return none
+
+    lax.fori_loop(0, heads, head_step, 0)
+    mixed_sums[...] = jnp.sum(d_mix[...].astype(f32), axis=0, keepdims=True)
+    produce(5)
+    middle(3)
+    finish(2)
+    loads[6].wait()
+    tiled_nt(d_mix, upw, cot, d_mix.shape[1], 1024, 256)
+    third = reduce_steps(cot, dn1_own, *set_b, p_send, p_recv, 16)
+    next(third)
+    next(third)
+    produce(6)
+    middle(4)
+    finish(3)
+    next(third)
+    next(third, None)
+    produce(7)
+    loads[8].start()
+    middle(5)
+    finish(4)
+    loads[8].wait()
+    tiled_nn(hid, n2, tot, 1024, 256)
+    fourth = reduce_steps(tot, outp_own, *set_a, p_send, p_recv, 24)
+    next(fourth)
+    next(fourth)
+    produce(8)
+    middle(6)
+    finish(5)
+    next(fourth)
+    next(fourth, None)
+    loads[7].wait()
+    for k in range(9, total):
+        produce(k)
+        middle(k - 2)
+        finish(k - 3)
+    middle(total - 2)
+    finish(total - 3)
+    middle(total - 1)
+    finish(total - 2)
+    finish(total - 1)
+    finish_outer(total - 1)
+
+    @pl.when(outer)
+    def _():
+        for k in range(total - g_slots, total):
+            inward(k).wait_send()
+        for k in range(total):
+            sent_home(k, b_land.at[k])
+
+    @pl.when(inner)
+    def _():
+        for k in range(total - s_slots, total):
+            outward(k).wait_send()
+            sent_home(k, t.at[k % s_slots])
+
+    for k in range(total):
+        for step in range(1, row_count):
+            source = (row + row_count - step) % row_count
+            put(t.at[0, source], place(k, source), a_send, a_recv, 3 * k + step - 1, {"row": source}).wait_recv()
+
+
+def backward_plane(cid, hid, cot, dup, n2, upw, std, n1, qkvw, downw, attended, outw, mixed, lse, bias, inv2, gain2):
+    f32, bf16 = jnp.float32, jnp.bfloat16
+    length, full = cot.shape
+    rows, width = length // lax.axis_size("col"), full // lax.axis_size("row")
+    row_count = full // width
+    counts = (dup.shape[1] // CHUNK, dup.shape[1] // CHUNK, attended.shape[1] // CHUNK, mixed.shape[1] // CHUNK)
+    total = sum(counts)
+    one = (row_count, width // CHUNK, CHUNK, CHUNK)
+    shape = jax.ShapeDtypeStruct
+    away, near = pl.BlockSpec(memory_space=pl.ANY), pl.BlockSpec(memory_space=pltpu.VMEM)
+    vmem, dma = pltpu.VMEM, pltpu.SemaphoreType.DMA
+    sets = [
+        vmem((4, rows, width), bf16),
+        vmem((rows, width), bf16),
+        vmem((rows // 2, width), bf16),
+        vmem((rows // 2, width), bf16),
+        vmem((2, rows, width), bf16),
+        vmem((2, rows, width), bf16),
+    ]
+    return pl.pallas_call(
+        functools.partial(backward_kernel, counts),
+        out_shape=[
+            shape((2, row_count * counts[0] * CHUNK, CHUNK), bf16),
+            shape((2, CHUNK, row_count * counts[1] * CHUNK), bf16),
+            shape((2, row_count * counts[2] * CHUNK, CHUNK), bf16),
+            shape((2, CHUNK, row_count * counts[3] * CHUNK), bf16),
+            shape((total,) + one, bf16),
+            shape((total,) + one, bf16),
+            shape((total,) + one, bf16),
+            shape((rows, width), f32),
+            shape((rows, width), f32),
+            shape((rows, width), f32),
+            shape((8, full), f32),
+            shape((1, mixed.shape[1]), f32),
+        ],
+        in_specs=[away] * 9 + [near] * 7,
+        out_specs=[away] * 7 + [near] * 5,
+        scratch_shapes=[
+            vmem((length, full), bf16),
+            vmem((length, full), bf16),
+            vmem((length, full), bf16),
+            vmem((length, full), bf16),
+            vmem((length, full), bf16),
+            vmem(upw.shape, bf16),
+            vmem(hid.shape, bf16),
+            vmem(dup.shape, bf16),
+            vmem(attended.shape, bf16),
+            vmem(mixed.shape, bf16),
+            vmem((length, HEAD), f32),
+            vmem((length, HEAD), f32),
+            vmem((3,) + one, bf16),
+            vmem((2,) + one, bf16),
+            vmem(one, bf16),
+            vmem((2,) + one, bf16),
+        ]
+        + sets
+        + sets
+        + [
+            vmem((rows, width), f32),
+            dma((9,)),
+            dma,
+            dma((total,)),
+            dma((3 * total,)),
+            dma((3 * total,)),
+            dma((3 * total,)),
+            dma((3 * total,)),
+            dma((32,)),
+            dma((32,)),
+        ],
+        compiler_params=pltpu.CompilerParams(
+            collective_id=cid, has_side_effects=True, vmem_limit_bytes=64 * 1024 * 1024 - 65536
+        ),
+        cost_estimate=pl.CostEstimate(flops=40_000_000_000, bytes_accessed=100_000_000, transcendentals=4_000_000),
+    )(hid, cot, dup, n2, upw, std, n1, qkvw, downw, attended, outw, mixed, lse, bias, inv2, gain2)
+
+
 def shift_rows(pieces):
     row, count = lax.axis_index("row"), pieces.shape[0]
     result = pieces
@@ -514,18 +1119,6 @@
         got = lax.ppermute(sent, "row", pairs)
         result = lax.dynamic_update_slice_in_dim(result, got, (row + count - step) % count, 0)
     return result
-
-
-def dp_total(share):
-    place = lax.axis_index("dp")
-    f32 = jnp.float32
-    inner = (place == 1) | (place == 2)
-    came = lax.ppermute(share, "dp", [(0, 1), (3, 2)])
-    half = (share.astype(f32) + came.astype(f32)).astype(share.dtype)
-    across = lax.ppermute(half, "dp", [(1, 2), (2, 1)])
-    total = (half.astype(f32) + across.astype(f32)).astype(share.dtype)
-    back = lax.ppermute(total, "dp", [(1, 0), (2, 3)])
-    return jnp.where(inner, total, back)
 
 
 def norm_stats(values):
@@ -608,10 +1201,11 @@
     value_rows = (mixed[:, :, 2] + own_qv[:, 1]).astype(bf16)
     scores = jnp.einsum("qhd,khd->hqk", queries, key_rows, preferred_element_type=f32) * factor
     scores = jnp.where(allowed[None], scores, masked_score)
-    weights = jnp.exp(scores - jnp.max(scores, axis=2, keepdims=True))
-    probs = weights / jnp.sum(weights, axis=2, keepdims=True)
-    low_probs = probs.astype(bf16)
-    attended = jnp.einsum("hqk,khd->qhd", low_probs, value_rows, preferred_element_type=f32)
+    highest = jnp.max(scores, axis=2, keepdims=True)
+    weights = jnp.exp(scores - highest)
+    weight_sum = jnp.sum(weights, axis=2, keepdims=True)
+    logsum = highest + jnp.log(weight_sum)
+    attended = jnp.einsum("hqk,khd->qhd", (weights / weight_sum).astype(bf16), value_rows, preferred_element_type=f32)
     attended = attended.astype(bf16).reshape(length, heads * HEAD)
     branch = total_plane(product(attended, out_flat, False).astype(bf16), 3)
     residual = inputs + (branch.astype(f32) + branch_bias)
@@ -623,59 +1217,46 @@
     d_hidden = product(cot_all, down_flat, True)
     d_upper = jax.vjp(gelu_tanh, up_sums)[1](d_hidden)[0].astype(bf16)
 
-    parts = 4
-    piece = hidden_count // parts
-    down_grads, up_grads = [], []
-    for part in range(parts):
-        grad = outer_sum(hidden[:, part * piece : (part + 1) * piece], cot_all).astype(bf16)
-        grad = shift_rows(jnp.moveaxis(grad.reshape(piece, row_count, width), 1, 0))
-        down_grads.append(dp_total(grad))
-    for part in range(parts):
-        grad = outer_sum(normed2, d_upper[:, part * piece : (part + 1) * piece]).astype(bf16)
-        up_grads.append(dp_total(shift_rows(grad.reshape(row_count, width, piece))))
-
-    d_normed2 = total_plane(product(d_upper, up_flat, True).astype(bf16), 4).astype(f32)
-    scaled = d_normed2 * gain2
-    d_residual = cot_all.astype(f32) + inverse2 * (
-        scaled
-        - jnp.mean(scaled, axis=1, keepdims=True)
-        - standard2 * jnp.mean(scaled * standard2, axis=1, keepdims=True)
-    )
-    d_branch = d_residual.astype(bf16)
-    out_grad = outer_sum(attended, d_branch).astype(bf16)
-    out_grad = dp_total(shift_rows(jnp.moveaxis(out_grad.reshape(heads * HEAD, row_count, width), 1, 0)))
-    d_attended = product(d_branch, out_flat, True).astype(bf16).reshape(length, heads, HEAD)
-    d_probs = jnp.einsum("qhd,khd->hqk", d_attended, value_rows, preferred_element_type=f32)
-    dots = jnp.sum(probs * d_probs, axis=2, keepdims=True)
-    d_scores = (probs * (d_probs - dots)).astype(bf16)
-    d_query = jnp.einsum("hqk,khd->qhd", d_scores, key_rows, preferred_element_type=f32) * factor
-    d_key = jnp.einsum("hqk,qhd->khd", d_scores, queries, preferred_element_type=f32) * factor
-    d_value = jnp.einsum("hqk,qhd->khd", low_probs, d_attended, preferred_element_type=f32)
-    d_mixed = jnp.stack([d_query, d_key, d_value], axis=2).astype(bf16)
-    d_flat = d_mixed.reshape(length, heads * 3 * HEAD)
-    qkv_grads = []
-    for head in range(heads):
-        grad = outer_sum(normed1, d_flat[:, head * 3 * HEAD : (head + 1) * 3 * HEAD]).astype(bf16)
-        qkv_grads.append(dp_total(shift_rows(grad.reshape(row_count, width, 3 * HEAD))))
-    d_normed1 = reduce_plane(product(d_flat, qkv_flat, True).astype(bf16), 5)
-
+    blocks = length // SPAN
+    places_of = jnp.arange(SPAN, dtype=jnp.int32)
+    marked = jnp.any(span_starts[0][:, None] // SPAN == jnp.arange(blocks, dtype=jnp.int32)[None, :], axis=0)
+    open_pairs = (places_of[None, :] <= places_of[:, None])[None] | marked[:, None, None]
+    bias = jnp.where(open_pairs, 0.0, masked_score).astype(f32)
+    mixed_rows = jnp.stack([queries, key_rows, value_rows], axis=2).reshape(length, heads * 3 * HEAD)
+    down_grad, up_grad, out_grad, qkv_grad, _, _, _, d_residual, d_normed1, sums_out, sums2, mixed_sums = backward_plane(
+        4,
+        hidden,
+        cot_all,
+        d_upper,
+        normed2,
+        up_flat,
+        standard2.astype(bf16),
+        normed1,
+        qkv_flat,
+        down_flat,
+        attended,
+        out_flat,
+        mixed_rows,
+        logsum,
+        bias,
+        inverse2,
+        gain2[None],
+    )
     standard1 = own((inputs - center1) * inverse1)
     own_inverse1 = lax.dynamic_slice_in_dim(inverse1, col * rows, rows, 0)
     d_norm1, gain1_grad, shift1_grad = norm_backward(
         d_normed1, standard1, own_inverse1[:, 0], ln1_gain
     )
-    tokens_grad = (own(d_residual) + d_norm1).astype(bf16)
-    sums_out = reduce_plane(product(hidden, down_flat, False).astype(bf16), 6)
+    tokens_grad = (d_residual + d_norm1).astype(bf16)
     output = (own(residual) + (sums_out + down_bias)).astype(bf16)
 
-    own_n2 = own_width(d_normed2)
     near = [
-        jnp.sum(own_n2 * own_width(standard2), axis=0),
-        jnp.sum(own_n2, axis=0),
-        jnp.sum(own_width(d_branch), axis=0, dtype=f32),
+        own_width(sums2[0]),
+        own_width(sums2[1]),
+        own_width(sums2[2]),
         jnp.sum(own_width(cot_all), axis=0, dtype=f32),
     ]
-    totals = jnp.sum(d_mixed, axis=0, dtype=f32)
+    totals = mixed_sums.reshape(heads, 3, HEAD)
     spread_sums = [
         jnp.sum(d_upper, axis=0, dtype=f32),
         jnp.stack([totals[:, 0], totals[:, 2]], axis=1).reshape(heads * 2 * HEAD),
@@ -689,23 +1270,20 @@
     mine = lax.dynamic_index_in_dim(summed[:, begin:], row, 0, keepdims=False).reshape(4, width)
     norm1_sums = lax.psum((gain1_grad, shift1_grad), ("dp", "col"))
 
-    down_weight_grad = jnp.stack(down_grads, axis=1).reshape(row_count * hidden_count, width).astype(f32)
-    up_weight_grad = jnp.stack(up_grads, axis=1).transpose(2, 0, 1, 3).reshape(width, row_count * hidden_count)
-    qkv_weight_grad = jnp.stack(qkv_grads, axis=1).transpose(2, 0, 1, 3)
     return (
         output,
         tokens_grad,
         norm1_sums[0],
         norm1_sums[1],
-        qkv_weight_grad.reshape(width, row_count * heads, 3, HEAD).astype(f32),
+        qkv_grad.astype(f32).reshape(width, row_count * heads, 3, HEAD),
         qv_bias_grad,
-        out_grad.reshape(row_count * heads, HEAD, width).astype(f32),
+        jnp.moveaxis(out_grad, 0, 1).astype(f32).reshape(row_count * heads, HEAD, width),
         mine[2],
         mine[0],
         mine[1],
-        up_weight_grad.astype(f32),
+        up_grad.astype(f32).reshape(width, row_count * hidden_count),
         up_bias_grad,
-        down_weight_grad,
+        jnp.moveaxis(down_grad, 0, 1).astype(f32).reshape(row_count * hidden_count, width),
         mine[3],
     )
 

time: 1250 us -> 862 us (0.69)
  waiting for transfers between devices: 402 us -> 24.2 us
  Pallas kernels: 218 us -> 503 us
  starting transfers between devices: 137 us -> 9.76 us
  matrix products: 104 us -> 32.1 us
  other arithmetic: 79.9 us -> 48.6 us
  blocking collectives: 121 us -> 89.9 us
  local copies, waits for them, and re-layouts: 172 us -> 141 us
    ppermute x33 -> x0, waiting for transfers between devices: 309 us -> none  [the longest x11 195 us: dp_total(): back = lax.ppermute(total, 'dp', [(1, 0), (2, 3)])]
    pallas_call x2 -> x1, Pallas kernels: 56.8 us -> 360 us  [backward_plane(): pl.pallas_call(functools.partial(backward_kernel, counts), out_shape=[sha...]
    ppermute x33 -> x0, starting transfers between devices: 100 us -> none  [the longest x11 74.6 us: dp_total(): came = lax.ppermute(share, 'dp', [(0, 1), (3, 2)])]
    ppermute x45 -> x12, waiting for transfers between devices: 93.1 us -> 24.2 us  [shift_rows(): got = lax.ppermute(sent, 'row', pairs)]
    pallas_call x2 -> x1, Pallas kernels: 108 us -> 49.5 us  [total_plane(): pl.pallas_call(total_kernel, out_shape=jax.ShapeDtypeStruct(part.shape, p...]
    pallas_call x2, Pallas kernels: 53.1 us -> 93.7 us  [gather_plane(): pl.pallas_call(gather_kernel, out_shape=jax.ShapeDtypeStruct((2 * rows, 4...]
    convert_element_type x31 -> x3, other arithmetic: 49.1 us -> 8.89 us  [the longest x1 6.4 us: plane_plan(): standard2.astype(bf16)]
    dot_general x16 -> x2, matrix products: 43.1 us -> 4.96 us  [the longest x1 2.87 us: plane_plan(): jnp.einsum('hqk,khd->qhd', (weights / weight_sum).astype(bf16), value_row...]
  transfers between devices with their start and end apart: 78 -> 12, of which waited for: 29 -> 2; matrix products, arithmetic and copies ran while one was open for 27% -> 16% of each run, Pallas kernels for 18% -> 17%
where the time goes in v2:
time: 862 us; the launch traced here: 850 us
  Pallas kernels  503 us (58%)
  local copies, waits for them, and re-layouts  141 us (16%)
  blocking collectives  89.9 us (10%)
  other arithmetic  48.6 us (6%)
  matrix products  32.1 us (4%)
  waiting for transfers between devices  24.2 us (3%)
  starting transfers between devices  9.76 us (1%)
    pallas_call x1, Pallas kernels, backward_plane(): pl.pallas_call(functools.partial(backward_kernel, counts), out_shape=[sha...  360 us
    pallas_call x2, Pallas kernels, gather_plane(): pl.pallas_call(gather_kernel, out_shape=jax.ShapeDtypeStruct((2 * rows, 4...  93.7 us
    psum x1, blocking collectives, plane_plan(): summed = lax.psum(jnp.concatenate(slots + own_slots, axis=1), ('dp', 'row'))  59.5 us
    dynamic_update_slice x13, local copies, waits for them, and re-layouts, shift_rows(): lax.dynamic_update_slice_in_dim(result, got, (row + count - step) % count...  50.9 us
    pallas_call x1, Pallas kernels, total_plane(): pl.pallas_call(total_kernel, out_shape=jax.ShapeDtypeStruct(part.shape, p...  49.5 us
    unnamed x74, local copies, waits for them, and re-layouts  42.6 us
    ppermute x12, waiting for transfers between devices, shift_rows(): got = lax.ppermute(sent, 'row', pairs)  24.2 us
    psum x1, blocking collectives, plane_plan(): norm1_sums = lax.psum((gain1_grad, shift1_grad), ('dp', 'col'))  19.4 us
  transfers between devices with their start and end apart: 12, of which 2 were waited for; matrix products, arithmetic and copies ran while one was open for 16% of the time, Pallas kernels for 17%

profile of v2, /device:TPU:0, one launch (start us, length us, event | category | flops | bytes accessed | tf_op | source)
XLA Modules:
  0.0 850.2 jit_solution(18332552622217062950)
XLA Ops:
  0.7 4.6 copy.200
  5.2 3.2 copy.130
  8.4 3.2 dynamic-slice_bitcast_fusion.3
  12.1 2.5 collective-permute-start.1
  14.7 1.4 collective-permute-start.2
  17.9 2.6 constant_dynamic-slice_fusion.8
  20.9 68.3 %shard_map.254 = bf16[1024,2048]{1,0:T(8,128)(2,1)} custom-call(bf16[512,512]{1,0:T(8,128)(2,1)S(1)} %copy-done), custom_call_target="tpu_custom_call" | custom-call | tf_op jit(solution)/shard_map/pallas_call | solution.py:434
  89.2 3.4 convert_reduce_fusion
  92.7 5.2 all_gather.3
  98.8 2.3 constant_dynamic-slice_fusion.7
  101.1 1.8 fusion.16
  103.0 7.1 fusion
  110.9 6.6 copy.141
  117.5 25.4 %shard_map.256.cot_h = bf16[1024,2048]{1,0:T(8,128)(2,1)} custom-call(bf16[512,512]{1,0:T(8,128)(2,1)S(1)} %copy-done.1), custom_call_target="tpu_custom_call" | custom-call | tf_op jit(solution)/shard_map/pallas_call | solution.py:434
  142.9 3.7 dynamic-slice_bitcast_fusion
  147.1 1.7 convert_reduce_fusion.2
  150.2 1.1 or_select_fusion.bias
  151.4 10.3 %dynamic_update_slice.59 = bf16[4,256,512]{2,0,1:T(4,128)(2,1)} dynamic-update-slice(bf16[4,256,512]{2,0,1:T(4,128)(2,1)} %copy-done.5, bf16[1,256,512]{2,0,1:T(2,128)(2,1)} %collective-permute-done.3, s32[]{:T(128)S(6)} %select_n.162, s32[]{:T(128)} %constant.201.clone.1, s32[]{:T(128)} %constant.201.clone.1) | dynamic-update-slice | bytes 524292 | tf_op jit(solution)/shard_map/dynamic_update_slice | solution.py:1120
  161.6 10.3 %dynamic_update_slice.60 = bf16[4,256,512]{2,0,1:T(4,128)(2,1)} dynamic-update-slice(bf16[4,256,512]{2,0,1:T(4,128)(2,1)} %dynamic_update_slice.59, bf16[1,256,512]{2,0,1:T(2,128)(2,1)} %collective-permute-done.4, s32[]{:T(128)S(6)} %select_n.164, s32[]{:T(128)} %constant.201.clone.1, s32[]{:T(128)} %constant.201.clone.1) | dynamic-update-slice | bytes 524292 | tf_op jit(solution)/shard_map/dynamic_update_slice | solution.py:1120
  171.9 1.2 collective-permute-start.7
  173.1 10.3 %dynamic_update_slice.61 = bf16[4,256,512]{2,0,1:T(4,128)(2,1)} dynamic-update-slice(bf16[4,256,512]{2,0,1:T(4,128)(2,1)} %dynamic_update_slice.60, bf16[1,256,512]{2,0,1:T(2,128)(2,1)} %collective-permute-done.5, s32[]{:T(128)S(6)} %select_n.160, s32[]{:T(128)} %constant.201.clone.1, s32[]{:T(128)} %constant.201.clone.1) | dynamic-update-slice | bytes 524292 | tf_op jit(solution)/shard_map/dynamic_update_slice | solution.py:1120
  183.4 2.5 copy.172
  185.9 1.4 collective-permute-start.8
  187.3 1.2 constant_dynamic-update-slice_fusion.14
  188.6 1.2 constant_dynamic-update-slice_fusion.13
  189.8 1.2 constant_dynamic-update-slice_fusion.12
  191.0 3.0 copy.131
  194.0 3.2 copy.132
  197.2 5.3 fusion.11
  202.6 2.1 fusion.2
  204.9 2.0 fusion.4
  206.9 2.9 fusion.18
  209.8 3.3 convolution_convert_fusion.part_ref
  213.1 49.5 %shard_map.255 = bf16[1024,2048]{1,0:T(8,128)(2,1)} custom-call(bf16[1024,2048]{1,0:T(8,128)(2,1)} %convolution_convert_fusion.part_ref), custom_call_target="tpu_custom_call" | custom-call | tf_op jit(solution)/shard_map/pallas_call | solution.py:502
  262.6 5.9 fusion.33
  269.8 1.8 copy.150.mixed
  271.5 1.4 copy.151.lse
  272.9 1.0 copy.152.inv2
  273.9 6.4 fusion.3
  280.3 2.3 constant_dynamic-update-slice_fusion.11
  282.7 2.3 constant_dynamic-update-slice_fusion.10
  285.0 2.3 constant_dynamic-update-slice_fusion.9
  287.3 6.3 copy.148
  293.6 3.3 constant_dynamic-slice_fusion.5
  298.5 9.0 %multiply_convert_fusion = (bf16[1024,1024]{1,0:T(8,128)(2,1)}, f32[1024,1024]{1,0:T(8,128)S(1)}) fusion(f32[1024]{0:T(1024)S(1)} %dynamic_slice.82, bf16[1024,2048]{1,0:T(8,128)(2,1)S(1)} %copy-done.9, bf16[2048,1024]{1,0:T(8,128)(2,1)} %bitcast.133), kind=kOutput, calls=%fused_computation.36 | convolution fusion | flops 4305453056 | bytes 14684160 | tf_op jit(solution)/shard_map/dot_general | solution.py:45
  307.5 14.7 %collective-permute-done.10 = bf16[1,1024,512]{2,1,0:T(8,128)(2,1)S(1)} collective-permute-done((bf16[1,1024,512]{2,1,0:T(8,128)(2,1)S(1)}, bf16[1,1024,512]{2,1,0:T(8,128)(2,1)S(1)}, u32[]{:S(2)}, u32[]{:S(2)}) %collective-permute-start.10) | collective-permute-done | bytes 1048608 | tf_op jit(solution)/shard_map/ppermute | solution.py:1119
  322.4 9.4 %collective-permute-done.11 = bf16[1,1024,512]{2,1,0:T(8,128)(2,1)S(1)} collective-permute-done((bf16[1,1024,512]{2,1,0:T(8,128)(2,1)S(1)}, bf16[1,1024,512]{2,1,0:T(8,128)(2,1)S(1)}, u32[]{:S(2)}, u32[]{:S(2)}) %collective-permute-start.11) | collective-permute-done | bytes 1048608 | tf_op jit(solution)/shard_map/ppermute | solution.py:1119
  332.6 3.0 copy-done.7
  335.6 9.5 %convert_reduce_fusion.1 = (f32[1024]{0:T(1024)}, bf16[1024,1024]{1,0:T(8,128)(2,1)}) fusion(bf16[1024,2048]{1,0:T(8,128)(2,1)S(1)} %bitcast.135, bf16[1024,2048]{1,0:T(8,128)(2,1)S(1)} %copy-done.7, f32[1024,1024]{1,0:T(8,128)S(1)} %get-tuple-element.157, f32[1024]{0:T(1024)S(1)} %dynamic_slice.82), kind=kOutput, calls=%fused_computation.35 | convolution fusion | flops 4323277824 | bytes 14688256 | tf_op jit(solution)/shard_map/dot_general | solution.py:42
  345.0 360.3 %shard_map.257 = (bf16[2,4096,256]{2,1,0:T(8,128)(2,1)}, bf16[2,256,4096]{2,1,0:T(8,128)(2,1)}, bf16[2,1024,256]{2,1,0:T(8,128)(2,1)}, bf16[2,256,3072]{2,1,0:T(...) custom-call(bf16[1024,1024]{1,0:T(8,128)(2,1)} %get-tuple-element.15, ...), custom_call_target="tpu_custom_call" | custom-call | flops 40000000000 | bytes 100000000 | tf_op jit(solution)/shard_map/pallas_call | solution.py:1056
  708.9 59.5 %psum.39 = f32[4,3584]{1,0:T(4,128)S(1)} all-reduce(f32[4,3584]{1,0:T(4,128)S(1)} %constant_dynamic-update-slice_fusion), channel_id=1, replica_groups=mesh['dp'=4,'row'=4,'col'=2] {'dp','row'}, use_global_device_ids=true, to_apply=%region_18.19 | all-reduce | flops 14336 | bytes 114688 | tf_op jit(solution)/shard_map/psum | solution.py:1266
  768.5 6.3 convert_bitcast_fusion
  774.7 8.9 %copy.155 = f32[4096,2,256]{0,2,1:T(8,128)} copy(f32[4096,2,256]{2,0,1:T(8,128)} %convert_bitcast_fusion) | data formatting | bytes 16777216 | tf_op jit(solution)/shard_map/reshape | solution.py:1286
  783.6 9.1 %copy.158 = f32[4096,512]{1,0:T(8,128)} copy(f32[4096,512]{0,1:T(8,128)} %bitcast.123) | data formatting | bytes 16777216
  794.0 7.4 reshape.480
  801.3 7.0 copy.156
  808.3 4.8 bitcast_convert_fusion
  813.3 1.6 copy.169
  814.9 2.7 reshape.481
  817.6 1.7 multiply_reduce_fusion.1
  819.3 19.4 %all-reduce = (f32[512]{0:T(512)}, f32[512]{0:T(512)}) all-reduce(f32[512]{0:T(512)S(1)} %get-tuple-element.102, f32[512]{0:T(512)S(1)} %get-tuple-element.109), channel_id=1, replica_groups=mesh['dp'=4,'row'=4,'col'=2] {'dp','col'}, use_global_device_ids=true, to_apply=%region_13.14 | all-reduce | flops 1024 | bytes 8192 | tf_op jit(solution)/shard_map/psum | solution.py:1271
  838.7 5.7 all-reduce.1
  844.4 2.6 add_convert_fusion.3
  847.7 2.3 add_convert_fusion.2
  (134 shorter events, 15.9 us)
Async XLA Ops:
  0.6 4.6 copy-start.13
  8.4 7.7 copy-start.16
  8.4 12.4 %copy-start = (bf16[512,512]{1,0:T(8,128)(2,1)S(1)}, bf16[512,512]{1,0:T(8,128)(2,1)}, u32[]{:S(2)}) copy-start(bf16[512,512]{1,0:T(8,128)(2,1)} %x_ref.2) | copy-start | bytes 1572868
  11.6 174.2 %collective-permute-start = (bf16[1,512,768]{1,2,0:T(8,128)(2,1)}, bf16[1,512,768]{1,2,0:T(8,128)(2,1)}, u32[]{:S(2)}, u32[]{:S(2)}) collective-permute-start(bf16[1,512,768]{1,2,0:T(8,128)(2,1)} %get-tuple-element.129), channel_id=1, source_target_pairs={{0,2},{2,4},{4,6},{6,0},{1,3},{3,5},{5,7},{7,1},{8,10},{10,12},{12... | collective-permute-start | bytes 2359304 | tf_op jit(solution)/shard_map/ppermute | solution.py:1119
  12.1 176.4 %collective-permute-start.1 = (bf16[1,512,768]{1,2,0:T(8,128)(2,1)}, bf16[1,512,768]{1,2,0:T(8,128)(2,1)}, u32[]{:S(2)}, u32[]{:S(2)}) collective-permute-start(bf16[1,512,768]{1,2,0:T(8,128)(2,1)} %get-tuple-element.128), channel_id=1, source_target_pairs={{0,4},{2,6},{4,0},{6,2},{1,5},{3,7},{5,1},{7,3},{8,12},{10,14},{12... | collective-permute-start | bytes 2359304 | tf_op jit(solution)/shard_map/ppermute | solution.py:1119
  14.7 175.2 %collective-permute-start.2 = (bf16[1,512,768]{1,2,0:T(8,128)(2,1)}, bf16[1,512,768]{1,2,0:T(8,128)(2,1)}, u32[]{:S(2)}, u32[]{:S(2)}) collective-permute-start(bf16[1,512,768]{1,2,0:T(8,128)(2,1)} %get-tuple-element.127), channel_id=1, source_target_pairs={{0,6},{2,0},{4,2},{6,4},{1,7},{3,1},{5,3},{7,5},{8,14},{10,8},{12,... | collective-permute-start | bytes 2359304 | tf_op jit(solution)/shard_map/ppermute | solution.py:1119
  16.9 1.0 copy-start.5
  20.4 126.2 %collective-permute-start.3 = (bf16[1,256,512]{2,0,1:T(2,128)(2,1)}, bf16[1,256,512]{2,0,1:T(2,128)(2,1)}, u32[]{:S(2)}, u32[]{:S(2)}) collective-permute-start(bf16[1,256,512]{2,0,1:T(2,128)(2,1)} %get-tuple-element.132), channel_id=1, source_target_pairs={{0,2},{2,4},{4,6},{6,0},{1,3},{3,5},{5,7},{7,1},{8,10},{10,12},{12... | collective-permute-start | bytes 786440 | tf_op jit(solution)/shard_map/ppermute | solution.py:1119
  20.4 141.2 %collective-permute-start.4 = (bf16[1,256,512]{2,0,1:T(2,128)(2,1)}, bf16[1,256,512]{2,0,1:T(2,128)(2,1)}, u32[]{:S(2)}, u32[]{:S(2)}) collective-permute-start(bf16[1,256,512]{2,0,1:T(2,128)(2,1)} %get-tuple-element.131), channel_id=1, source_target_pairs={{0,4},{2,6},{4,0},{6,2},{1,5},{3,7},{5,1},{7,3},{8,12},{10,14},{12... | collective-permute-start | bytes 786440 | tf_op jit(solution)/shard_map/ppermute | solution.py:1119
  20.9 71.8 %copy-start.20 = (f32[512]{0:T(512)S(1)}, f32[512]{0:T(512)}, u32[]{:S(2)}) copy-start(f32[512]{0:T(512)} %param.16) | copy-start | bytes 6148
  20.9 71.8 %copy-start.23 = (f32[512]{0:T(512)S(1)}, f32[512]{0:T(512)}, u32[]{:S(2)}) copy-start(f32[512]{0:T(512)} %param.17) | copy-start | bytes 6148
  20.9 71.8 %copy-start.24 = (f32[512]{0:T(512)S(1)}, f32[512]{0:T(512)}, u32[]{:S(2)}) copy-start(f32[512]{0:T(512)} %param.21) | copy-start | bytes 6148
  20.9 71.8 %copy-start.25 = (f32[512]{0:T(512)S(1)}, f32[512]{0:T(512)}, u32[]{:S(2)}) copy-start(f32[512]{0:T(512)} %param.22) | copy-start | bytes 6148
  20.9 71.8 %copy-start.26 = (f32[512]{0:T(512)S(1)}, f32[512]{0:T(512)}, u32[]{:S(2)}) copy-start(f32[512]{0:T(512)} %param.23) | copy-start | bytes 6148
  20.9 77.7 %copy-start.28 = (s32[1,2]{1,0:T(1,128)S(1)}, s32[1,2]{1,0:T(1,128)}, u32[]{:S(2)}) copy-start(s32[1,2]{1,0:T(1,128)} %param.28) | copy-start | bytes 28
  110.9 6.6 copy-start.1
  146.6 40.7 %copy-start.4 = (bf16[512,8,3,128]{0,3,2,1:T(8,128)(2,1)S(1)}, bf16[512,8,3,128]{0,3,2,1:T(8,128)(2,1)}, u32[]{:S(2)}) copy-start(bf16[512,8,3,128]{0,3,2,1:T(8,128)(2,1)} %copy.130) | copy-start | bytes 9437188
  146.6 25.3 %collective-permute-start.5 = (bf16[1,256,512]{2,0,1:T(2,128)(2,1)}, bf16[1,256,512]{2,0,1:T(2,128)(2,1)}, u32[]{:S(2)}, u32[]{:S(2)}) collective-permute-start(bf16[1,256,512]{2,0,1:T(2,128)(2,1)} %get-tuple-element.130), channel_id=1, source_target_pairs={{0,6},{2,0},{4,2},{6,4},{1,7},{3,1},{5,3},{7,5},{8,14},{10,8},{12,... | collective-permute-start | bytes 786440 | tf_op jit(solution)/shard_map/ppermute | solution.py:1119
  150.2 39.6 %copy-start.19 = (f32[4,512]{1,0:T(4,128)}, f32[4,512]{1,0:T(4,128)S(1)}, u32[]{:S(2)}) copy-start(f32[4,512]{1,0:T(4,128)S(1)} %dynamic_update_slice.73) | copy-start | bytes 24580
  161.6 118.7 %collective-permute-start.6 = (bf16[1,512,1024]{1,2,0:T(8,128)(2,1)}, bf16[1,512,1024]{1,2,0:T(8,128)(2,1)}, u32[]{:S(2)}, u32[]{:S(2)}) collective-permute-start(bf16[1,512,1024]{1,2,0:T(8,128)(2,1)} %get-tuple-element.124), channel_id=1, source_target_pairs={{0,2},{2,4},{4,6},{6,0},{1,3},{3,5},{5,7},{7,1},{8,10},{10,12},{12... | collective-permute-start | bytes 3145736 | tf_op jit(solution)/shard_map/ppermute | solution.py:1119
  171.9 110.8 %collective-permute-start.7 = (bf16[1,512,1024]{1,2,0:T(8,128)(2,1)}, bf16[1,512,1024]{1,2,0:T(8,128)(2,1)}, u32[]{:S(2)}, u32[]{:S(2)}) collective-permute-start(bf16[1,512,1024]{1,2,0:T(8,128)(2,1)} %get-tuple-element.123), channel_id=1, source_target_pairs={{0,4},{2,6},{4,0},{6,2},{1,5},{3,7},{5,1},{7,3},{8,12},{10,14},{12... | collective-permute-start | bytes 3145736 | tf_op jit(solution)/shard_map/ppermute | solution.py:1119
  185.9 99.1 %collective-permute-start.8 = (bf16[1,512,1024]{1,2,0:T(8,128)(2,1)}, bf16[1,512,1024]{1,2,0:T(8,128)(2,1)}, u32[]{:S(2)}, u32[]{:S(2)}) collective-permute-start(bf16[1,512,1024]{1,2,0:T(8,128)(2,1)} %get-tuple-element.122), channel_id=1, source_target_pairs={{0,6},{2,0},{4,2},{6,4},{1,7},{3,1},{5,3},{7,5},{8,14},{10,8},{12,... | collective-permute-start | bytes 3145736 | tf_op jit(solution)/shard_map/ppermute | solution.py:1119
  188.5 105.1 %collective-permute-start.9 = (bf16[1,1024,512]{2,1,0:T(8,128)(2,1)}, bf16[1,1024,512]{2,1,0:T(8,128)(2,1)}, u32[]{:S(2)}, u32[]{:S(2)}) collective-permute-start(bf16[1,1024,512]{2,1,0:T(8,128)(2,1)} %constant_dynamic-slice_fusion.7), channel_id=1, source_target_pairs={{0,2},{2,4},{4,6},{6,0},{1,3},{3,5},{5,7},{7,1},{8,10},{10,12},{12... | collective-permute-start | bytes 3145736 | tf_op jit(solution)/shard_map/ppermute | solution.py:1119
  197.2 5.4 copy-start.6
  206.9 2.9 copy-start.12
  213.1 49.5 %copy-start.2 = (bf16[1024,2048]{1,0:T(8,128)(2,1)S(1)}, bf16[1024,2048]{1,0:T(8,128)(2,1)}, u32[]{:S(2)}) copy-start(bf16[1024,2048]{1,0:T(8,128)(2,1)} %shard_map.254) | copy-start | bytes 12582916
  293.6 5.0 copy-start.9
  296.9 25.4 %collective-permute-start.10 = (bf16[1,1024,512]{2,1,0:T(8,128)(2,1)S(1)}, bf16[1,1024,512]{2,1,0:T(8,128)(2,1)S(1)}, u32[]{:S(2)}, u32[]{:S(2)}) collective-permute-start(bf16[1,1024,512]{2,1,0:T(8,128)(2,1)S(1)} %get-tuple-element.120), channel_id=1, source_target_pairs={{0,4},{2,6},{4,0},{6,2},{1,5},{3,7},{5,1},{7,3},{8,12},{10,14},{12... | collective-permute-start | bytes 3145736 | tf_op jit(solution)/shard_map/ppermute | solution.py:1119
  297.7 34.1 %collective-permute-start.11 = (bf16[1,1024,512]{2,1,0:T(8,128)(2,1)S(1)}, bf16[1,1024,512]{2,1,0:T(8,128)(2,1)S(1)}, u32[]{:S(2)}, u32[]{:S(2)}) collective-permute-start(bf16[1,1024,512]{2,1,0:T(8,128)(2,1)S(1)} %get-tuple-element.119), channel_id=1, source_target_pairs={{0,6},{2,0},{4,2},{6,4},{1,7},{3,1},{5,3},{7,5},{8,14},{10,8},{12,... | collective-permute-start | bytes 3145736 | tf_op jit(solution)/shard_map/ppermute | solution.py:1119
  298.5 23.7 %copy-start.3 = (bf16[4,1024,512]{2,1,0:T(8,128)(2,1)S(1)}, bf16[4,1024,512]{2,1,0:T(8,128)(2,1)}, u32[]{:S(2)}) copy-start(bf16[4,1024,512]{2,1,0:T(8,128)(2,1)} %get-tuple-element.121) | copy-start | bytes 12582916
  331.9 3.7 copy-start.7
  332.5 12.5 %copy-start.10 = (bf16[4,128,8,512]{3,2,0,1:T(8,128)(2,1)}, bf16[4,128,8,512]{3,2,0,1:T(8,128)(2,1)S(1)}, u32[]{:S(2)}) copy-start(bf16[4,128,8,512]{3,2,0,1:T(8,128)(2,1)S(1)} %copy.171) | copy-start | bytes 12582916
  768.5 6.3 copy-start.18
  783.6 9.7 %slice-start.1 = ((f32[4,3584]{1,0:T(4,128)}), f32[4,512]{1,0:T(4,128)S(1)}, s32[]{:S(2)}) async-start(f32[4,3584]{1,0:T(4,128)} %copy-done.18), calls=%async_computation.1 | async-start | bytes 16384 | tf_op jit(solution)/shard_map/slice | solution.py:1269
  783.6 10.3 %copy-start.14 = (bf16[2,256,3072]{2,1,0:T(8,128)(2,1)S(1)}, bf16[2,256,3072]{2,1,0:T(8,128)(2,1)}, u32[]{:S(2)}) copy-start(bf16[2,256,3072]{2,1,0:T(8,128)(2,1)} %get-tuple-element.26) | copy-start | bytes 9437188
  801.3 7.0 copy-start.8
  808.3 4.8 copy-start.15
  813.3 4.4 copy-start.11
  813.3 4.4 copy-start.21
  814.9 29.5 %copy-start.27 = (f32[512]{0:T(512)S(1)}, f32[512]{0:T(512)}, u32[]{:S(2)}) copy-start(f32[512]{0:T(512)} %param.27) | copy-start | bytes 6148
  814.9 32.1 %slice-start = ((f32[4,3584]{1,0:T(4,128)}), f32[4,2048]{1,0:T(4,128)S(1)}, s32[]{:S(2)}) async-start(f32[4,3584]{1,0:T(4,128)} %copy-done.18), calls=%async_computation | async-start | bytes 65536 | tf_op jit(solution)/shard_map/slice | solution.py:1270
  814.9 32.8 %copy-start.22 = (f32[512]{0:T(512)S(1)}, f32[512]{0:T(512)}, u32[]{:S(2)}) copy-start(f32[512]{0:T(512)} %dynamic-slice.27) | copy-start | bytes 6148
  817.6 30.1 %copy-start.17 = (f32[512,512]{1,0:T(8,128)S(1)}, f32[512,512]{1,0:T(8,128)}, u32[]{:S(2)}) copy-start(f32[512,512]{1,0:T(8,128)} %get-tuple-element.24) | copy-start | bytes 3145732

commit v3 on v2

--- a/solution.py
+++ b/solution.py
@@ -373,136 +373,19 @@
 
 def places():
     row, col = lax.axis_index("row"), lax.axis_index("col")
-    side, core = row // 2, row % 2
-    return col, side, core
+    return col, row // 2, row % 2
+
 
 def partners():
     col, side, core = places()
     return ({"col": 1 - col}, {"row": (1 - side) * 2 + core}, {"row": side * 2 + 1 - core})
 
-def greet():
-    barrier = pltpu.get_barrier_semaphore()
-    for partner in partners():
-        pl.semaphore_signal(barrier, inc=1, device_id=partner, device_id_type=MESH)
-    pl.semaphore_wait(barrier, 3)
 
 def block(ref, col, side, core, rows, width, part=None):
     begin, count = col * rows, rows
     if part is not None:
         begin, count = begin + part * (rows // 2), rows // 2
-    left = (side * 2 + core) * width
-    return ref.at[pl.ds(pl.multiple_of(begin, count), count), pl.ds(pl.multiple_of(left, width), width)]
-
-def send(ref_from, ref_to, sends, recvs, at, partner):
-    copy = pltpu.make_async_remote_copy(src_ref=ref_from, dst_ref=ref_to, send_sem=sends.at[at], recv_sem=recvs.at[at], device_id=partner, device_id_type=MESH)
-    copy.start()
-    return copy
-
-def spread(out, rows, width, sends, recvs, base):
-    col, side, core = places()
-    to_x, to_y, to_core = partners()
-    def go(at, which, partner, part=None):
-        ref = block(out, *which, rows, width, part)
-        return send(ref, ref, sends, recvs, base + at, partner)
-    own, ox, oy, od = (col, side, core), (1 - col, side, core), (col, 1 - side, core), (1 - col, 1 - side, core)
-    c0 = go(0, own, to_x)
-    c1 = go(1, own, to_y)
-    c2 = go(2, own, to_core)
-    c0.wait_recv()
-    c3 = go(3, ox, to_y, 0)
-    c1.wait_recv()
-    c4 = go(4, oy, to_x, 1)
-    c5 = go(5, ox, to_core)
-    c6 = go(6, oy, to_core)
-    c3.wait_recv()
-    c4.wait_recv()
-    c7 = go(7, od, to_core)
-    for c in (c2, c5, c6, c7):
-        c.wait_recv()
-    for c in (c0, c1, c2, c3, c4, c5, c6, c7):
-        c.wait_send()
-
-def gather_kernel(x_ref, out, sends, recvs):
-    rows, width = x_ref.shape
-    greet()
-    col, side, core = places()
-    block(out, col, side, core, rows, width)[...] = x_ref[...]
-    spread(out, rows, width, sends, recvs, 0)
-
-def gather_plane(x, cid):
-    rows, width = x.shape
-    return pl.pallas_call(gather_kernel, out_shape=jax.ShapeDtypeStruct((2*rows,4*width), x.dtype),
-        in_specs=[pl.BlockSpec(memory_space=pltpu.VMEM)], out_specs=pl.BlockSpec(memory_space=pltpu.VMEM),
-        scratch_shapes=[pltpu.SemaphoreType.DMA((8,)), pltpu.SemaphoreType.DMA((8,))],
-        compiler_params=pltpu.CompilerParams(collective_id=cid, has_side_effects=True, vmem_limit_bytes=50<<20))(x)
-
-def sum_to_owner(part_ref, got, keep, diag, half_x, half_y, to_send, from_xy, sends, recvs, rows, width):
-    col, side, core = places()
-    to_x, to_y, to_core = partners()
-    half = rows // 2
-    spots = ((1-col,1-side),(col,1-side),(1-col,side),(col,side))
-    copies = []
-    for i,(a,b) in enumerate(spots):
-        copies.append(send(block(part_ref, a, b, 1-core, rows, width), got.at[i], sends, recvs, i, to_core))
-    f32 = jnp.float32
-    copies[0].wait_recv()
-    diag[...] = (block(part_ref, 1-col, 1-side, core, rows, width)[...].astype(f32) + got[0].astype(f32)).astype(diag.dtype)
-    dx = send(diag.at[pl.ds(0,half)], half_x, sends, recvs, 4, to_x)
-    dy = send(diag.at[pl.ds(half,half)], half_y, sends, recvs, 5, to_y)
-    copies[1].wait_recv()
-    copies[2].wait_recv()
-    dx.wait_recv()
-    py = block(part_ref, col, 1-side, core, rows, width)
-    px = block(part_ref, 1-col, side, core, rows, width)
-    ty = to_send.at[0]
-    tx = to_send.at[1]
-    ty[pl.ds(0,half)] = (py[pl.ds(0,half)].astype(f32) + got[1,pl.ds(0,half)].astype(f32) + half_x[...].astype(f32)).astype(diag.dtype)
-    ty[pl.ds(half,half)] = (py[pl.ds(half,half)].astype(f32) + got[1,pl.ds(half,half)].astype(f32)).astype(diag.dtype)
-    cy = send(ty, from_xy.at[0], sends, recvs, 6, to_y)
-    dy.wait_recv()
-    tx[pl.ds(0,half)] = (px[pl.ds(0,half)].astype(f32) + got[2,pl.ds(0,half)].astype(f32)).astype(diag.dtype)
-    tx[pl.ds(half,half)] = (px[pl.ds(half,half)].astype(f32) + got[2,pl.ds(half,half)].astype(f32) + half_y[...].astype(f32)).astype(diag.dtype)
-    cx = send(tx, from_xy.at[1], sends, recvs, 7, to_x)
-    copies[3].wait_recv()
-    keep[...] = block(part_ref, col, side, core, rows, width)[...].astype(f32) + got[3].astype(f32)
-    cy.wait_recv()
-    cx.wait_recv()
-    for c in copies + [dx, dy, cy, cx]:
-        c.wait_send()
-    return keep[...] + from_xy[0].astype(f32) + from_xy[1].astype(f32)
-
-def sum_scratch(rows, width, dt):
-    return [pltpu.VMEM((4,rows,width),dt), pltpu.VMEM((rows,width),jnp.float32), pltpu.VMEM((rows,width),dt),
-            pltpu.VMEM((rows//2,width),dt), pltpu.VMEM((rows//2,width),dt), pltpu.VMEM((2,rows,width),dt), pltpu.VMEM((2,rows,width),dt)]
-
-def reduce_kernel(part_ref, out, *scratch):
-    *bufs, sends, recvs = scratch
-    rows, width = out.shape
-    greet()
-    out[...] = sum_to_owner(part_ref, *bufs, sends, recvs, rows, width)
-
-def reduce_plane(part, cid):
-    rows, width = part.shape[0]//2, part.shape[1]//4
-    return pl.pallas_call(reduce_kernel, out_shape=jax.ShapeDtypeStruct((rows,width), jnp.float32),
-        in_specs=[pl.BlockSpec(memory_space=pltpu.VMEM)], out_specs=pl.BlockSpec(memory_space=pltpu.VMEM),
-        scratch_shapes=sum_scratch(rows,width,part.dtype)+[pltpu.SemaphoreType.DMA((8,)), pltpu.SemaphoreType.DMA((8,))],
-        compiler_params=pltpu.CompilerParams(collective_id=cid, has_side_effects=True, vmem_limit_bytes=50<<20))(part)
-
-def total_kernel(part_ref, out, *scratch):
-    *bufs, sends, recvs = scratch
-    rows, width = out.shape[0]//2, out.shape[1]//4
-    greet()
-    own = sum_to_owner(part_ref, *bufs, sends, recvs, rows, width)
-    col, side, core = places()
-    block(out, col, side, core, rows, width)[...] = own.astype(out.dtype)
-    spread(out, rows, width, sends, recvs, 8)
-
-def total_plane(part, cid):
-    rows, width = part.shape[0]//2, part.shape[1]//4
-    return pl.pallas_call(total_kernel, out_shape=jax.ShapeDtypeStruct(part.shape, part.dtype),
-        in_specs=[pl.BlockSpec(memory_space=pltpu.VMEM)], out_specs=pl.BlockSpec(memory_space=pltpu.VMEM),
-        scratch_shapes=sum_scratch(rows,width,part.dtype)+[pltpu.SemaphoreType.DMA((16,)), pltpu.SemaphoreType.DMA((16,))],
-        compiler_params=pltpu.CompilerParams(collective_id=cid, has_side_effects=True, vmem_limit_bytes=50<<20))(part)
+    return ref.at[strip(begin, count), strip((side * 2 + core) * width, width)]
 
 
 def put(ref_from, ref_to, sends, recvs, at, partner):
@@ -558,7 +441,7 @@
     lax.fori_loop(0, (rows // tile_rows) * across, step, 0)
 
 
-def reduce_steps(part, result, got, keep, diag, half_x, half_y, to_send, from_xy, sends, recvs, base):
+def reduce_steps(part, result, got, diag, half_x, half_y, to_send, from_xy, sends, recvs, base):
     f32 = jnp.float32
     rows, width = result.shape
     half = rows // 2
@@ -587,7 +470,7 @@
     to_send[0, high] = (mine[1][high].astype(f32) + got[1, high].astype(f32)).astype(diag.dtype)
     to_send[1, low] = (mine[2][low].astype(f32) + got[2, low].astype(f32)).astype(diag.dtype)
     copies[3].wait_recv()
-    keep[...] = mine[3][...].astype(f32) + got[3].astype(f32)
+    result[...] = mine[3][...].astype(f32) + got[3].astype(f32)
     yield
     dx.wait_recv()
     to_send[0, low] = (mine[1][low].astype(f32) + got[1, low].astype(f32) + half_x[...].astype(f32)).astype(diag.dtype)
@@ -600,7 +483,7 @@
     yield
     cy.wait_recv()
     cx.wait_recv()
-    result[...] = keep[...] + from_xy[0].astype(f32) + from_xy[1].astype(f32)
+    result[...] = result[...] + from_xy[0].astype(f32) + from_xy[1].astype(f32)
     for copy in copies + [dx, dy, cy, cx]:
         copy.wait_send()
 
@@ -651,20 +534,24 @@
     counts,
     hid_h,
     cot_h,
-    dup_h,
+    slope_h,
     n2_h,
     upw_h,
     std_h,
     n1_h,
     qkvw_h,
-    downw_h,
+    down_nat,
+    resid_h,
     attended,
     outw,
     mixed,
     lse,
     bias,
     inv2,
-    gain2,
+    vec_all,
+    std1_own,
+    inv1_own,
+    down_bias,
     down_out,
     up_out,
     out_out,
@@ -672,11 +559,10 @@
     r_land,
     m_land,
     b_land,
-    dres_own,
-    dn1_own,
-    outp_own,
-    sums,
-    mixed_sums,
+    downw_land,
+    out_block,
+    tokens_block,
+    small_out,
     cot,
     n2,
     std,
@@ -705,7 +591,13 @@
     hy_b,
     ts_b,
     fx_b,
-    keep,
+    dres_own,
+    own_sum,
+    sums,
+    small,
+    x_land,
+    dp_land,
+    stat_land,
     load_sem,
     ld_sem,
     own_sem,
@@ -733,36 +625,44 @@
     loads = [
         (hid_h, hid),
         (cot_h, cot),
-        (dup_h, dup),
+        (slope_h, dup),
         (upw_h, upw),
         (n2_h, n2),
         (std_h, std),
         (qkvw_h, upw.at[:, : qkvw_h.shape[1]]),
         (n1_h, std),
-        (downw_h, n2),
+        (downw_land, n2),
+        (downw_land, tot),
+        (resid_h, dres_own),
     ]
     loads = [pltpu.make_async_copy(a, b, load_sem.at[k]) for k, (a, b) in enumerate(loads)]
     for k in range(6):
         loads[k].start()
 
+    dp_count = dp_land.shape[0]
     barrier = pltpu.get_barrier_semaphore()
-    for partner in partners() + ({"row": (1 - side) * 2 + 1 - core},):
+    others = [{"row": (1 - side) * 2 + 1 - core}] + [{"dp": (plane + k) % dp_count} for k in range(1, dp_count)]
+    for partner in partners() + tuple(others):
         pl.semaphore_signal(barrier, inc=1, device_id=partner, device_id_type=MESH)
-
-    @pl.when(outer)
-    def _():
-        pl.semaphore_signal(barrier, inc=1, device_id=to_inner, device_id_type=MESH)
-        pl.semaphore_wait(barrier, 5)
-
-    @pl.when(inner)
-    def _():
-        pl.semaphore_signal(barrier, inc=1, device_id=to_middle, device_id_type=MESH)
-        pl.semaphore_signal(barrier, inc=1, device_id=to_outer, device_id_type=MESH)
-        pl.semaphore_wait(barrier, 6)
+    pl.semaphore_wait(barrier, 3 + len(others))
+
+    units = hid.shape[1]
+    down_sends, down_recvs = [], []
+    for step in range(1, row_count):
+        target, source = (row + step) % row_count, (row + row_count - step) % row_count
+        here, there = downw_land.at[:, strip(row * width, width)], downw_land.at[:, strip(source * width, width)]
+        piece = down_nat.at[strip(target * units, units), :]
+        down_sends.append(put(piece, here, p_send, p_recv, 32 + step - 1, {"row": target}))
+        down_recvs.append(put(piece, there, p_send, p_recv, 32 + step - 1, {"row": source}))
+        down_sends[-1].start()
+    down_own = pltpu.make_async_copy(
+        down_nat.at[strip(row * units, units), :], downw_land.at[:, strip(row * width, width)], own_sem.at[total]
+    )
+    down_own.start()
 
     def place(i, source):
         if i < n_down:
-            return down_out.at[:, strip(source * n_down * CHUNK + i * CHUNK, CHUNK), :]
+            return down_out.at[strip(source * n_down + i // 2 * 2, 2), :, pl.ds(i % 2 * CHUNK, CHUNK)]
         i -= n_down
         if i < n_up:
             return up_out.at[:, :, strip(source * n_up * CHUNK + i * CHUNK, CHUNK)]
@@ -808,11 +708,16 @@
                 inward(i - g_slots).wait_send()
 
         slot = g.at[i % g_slots]
-        if i < n_down or n_down + n_up <= i < n_down + n_up + n_out:
-            if i < n_down:
-                left, begin, right = hid, i * CHUNK, cot
-            else:
-                left, begin, right = attended, (i - n_down - n_up) * CHUNK, part
+        if i < n_down:
+            begin, lane = i // 2 * 2 * CHUNK, i % 2 * CHUNK
+
+            def step(k, none):
+                value = dot_tn(hid[:, begin : begin + 2 * CHUNK], cot[:, strip(k * width + lane, CHUNK)]).astype(bf16)
+                slot[k, 0] = value[:CHUNK]
+                slot[k, 1] = value[CHUNK:]
+                return none
+        elif n_down + n_up <= i < n_down + n_up + n_out:
+            left, begin, right = attended, (i - n_down - n_up) * CHUNK, part
 
             def step(k, none):
                 value = dot_tn(left[:, begin : begin + CHUNK], right[:, strip(k * width, width)]).astype(bf16)
@@ -882,56 +787,76 @@
         if i >= 1:
             finish_outer(i - 1)
 
-    set_a = (got_a, keep, diag_a, hx_a, hy_a, ts_a, fx_a)
-    set_b = (got_b, keep, diag_b, hx_b, hy_b, ts_b, fx_b)
+    set_a = (got_a, diag_a, hx_a, hy_a, ts_a, fx_a)
+    set_b = (got_b, diag_b, hx_b, hy_b, ts_b, fx_b)
+    gain2 = vec_all[3:4, :]
 
     loads[0].wait()
     loads[1].wait()
     produce(0)
     produce(1)
+    sums[...] = jnp.zeros_like(sums)
+    middle(0)
+    produce(2)
+    down_own.wait()
+    for copy in down_recvs:
+        copy.wait_recv()
+    loads[9].start()
     loads[2].wait()
+    middle(1)
+    produce(3)
+    finish(0)
+    loads[9].wait()
+
+    def upper_step(k, none):
+        down, across_ = k // (units // CHUNK), k % (units // CHUNK)
+        at, lanes = strip(down * rows, rows), strip(across_ * CHUNK, CHUNK)
+        dup[at, lanes] = (dot_nt(cot[at, :], tot[lanes, :]) * dup[at, lanes].astype(f32)).astype(bf16)
+        return none
+
+    lax.fori_loop(0, (length // rows) * (units // CHUNK), upper_step, 0)
     loads[3].wait()
     tiled_nt(dup, upw, part, dup.shape[1], 1024, 256)
     loads[6].start()
-    first = reduce_steps(part, outp_own, *set_a, p_send, p_recv, 0)
-    next(first)
+    first = reduce_steps(part, own_sum, *set_a, p_send, p_recv, 0)
     next(first)
     next(first)
     loads[4].wait()
     loads[5].wait()
-    middle(0)
-    produce(2)
+    next(first)
+    middle(2)
+    produce(4)
     next(first, None)
-    block(tot, col, side, core, rows, width)[...] = outp_own[...].astype(bf16)
+    block(tot, col, side, core, rows, width)[...] = own_sum[...].astype(bf16)
     second = spread_steps(tot, rows, width, p_send, p_recv, 8)
     next(second)
+    finish(1)
     next(second)
     next(second)
-    middle(1)
-    produce(3)
-    finish(0)
+    middle(3)
+    produce(5)
     next(second, None)
 
     tile = 64
-    sums[...] = jnp.zeros_like(sums)
 
     def norm_step(k, none):
         at = strip(k * tile, tile)
         grad, standard, inverse = tot[at, :].astype(f32), std[at, :].astype(f32), inv2[at, :]
-        scaled = grad * gain2[...]
+        scaled = grad * gain2
         mean_one = jnp.sum(scaled, axis=1, keepdims=True) / full
         mean_two = jnp.sum(scaled * standard, axis=1, keepdims=True) / full
-        d_res = cot[at, :].astype(f32) + inverse * (scaled - mean_one - standard * mean_two)
-        low = d_res.astype(bf16)
+        top = cot[at, :].astype(f32)
+        low = (top + inverse * (scaled - mean_one - standard * mean_two)).astype(bf16)
         part[at, :] = low
         sums[0:1, :] += jnp.sum(grad * standard, axis=0, keepdims=True)
         sums[1:2, :] += jnp.sum(grad, axis=0, keepdims=True)
         sums[2:3, :] += jnp.sum(low.astype(f32), axis=0, keepdims=True)
+        sums[3:4, :] += jnp.sum(top, axis=0, keepdims=True)
 
         @pl.when(k // (rows // tile) == col)
         def _():
             here = strip(row * width, width)
-            own = tot[at, here].astype(f32) * gain2[:, here]
+            own = tot[at, here].astype(f32) * vec_all[3:4, here]
             dres_own[strip(k % (rows // tile) * tile, tile), :] = cot[at, here].astype(f32) + inverse * (
                 own - mean_one - std[at, here].astype(f32) * mean_two
             )
@@ -940,10 +865,8 @@
 
     lax.fori_loop(0, length // tile, norm_step, 0)
     loads[7].start()
+    finish(2)
     tiled_nt(part, outw, d_att, full, 512, 256)
-    produce(4)
-    middle(2)
-    finish(1)
 
     heads = mixed.shape[1] // (3 * HEAD)
     factor = 1.0 / math.sqrt(HEAD)
@@ -961,7 +884,7 @@
             query, dout = mixed[here, at_q], d_att[here, at_o]
             keys, values = mixed[:seen, at_k], mixed[:seen, at_v]
             scores = dot_nt(query, keys) * factor
-            last = scores[:, seen - SPAN :] + bias[k]
+            last = scores[:, seen - SPAN :] + bias[k].astype(f32)
             scores = last if k == 0 else jnp.concatenate([scores[:, : seen - SPAN], last], axis=1)
             probs = jnp.exp(scores - lse[head, here])
             d_probs = dot_nt(dout, values)
@@ -975,38 +898,105 @@
         return none
 
     lax.fori_loop(0, heads, head_step, 0)
-    mixed_sums[...] = jnp.sum(d_mix[...].astype(f32), axis=0, keepdims=True)
-    produce(5)
-    middle(3)
-    finish(2)
+    middle(4)
+    produce(6)
+    finish(3)
     loads[6].wait()
     tiled_nt(d_mix, upw, cot, d_mix.shape[1], 1024, 256)
-    third = reduce_steps(cot, dn1_own, *set_b, p_send, p_recv, 16)
+    third = reduce_steps(cot, own_sum, *set_b, p_send, p_recv, 16)
     next(third)
     next(third)
-    produce(6)
-    middle(4)
-    finish(3)
+    middle(5)
+    produce(7)
+    loads[8].start()
+    finish(4)
     next(third)
     next(third, None)
-    produce(7)
-    loads[8].start()
-    middle(5)
-    finish(4)
+
+    grad1, gain1 = own_sum, vec_all[0:1, strip(row * width, width)]
+    scaled1 = grad1[...] * gain1
+    first_sum = jnp.sum(scaled1, axis=1, keepdims=True)
+    second_sum = jnp.sum(scaled1 * std1_own[...].astype(f32), axis=1, keepdims=True)
+    lane = lax.broadcasted_iota(jnp.int32, (rows, 128), 1)
+    pair = jnp.where(lane == 0, first_sum, jnp.where(lane == 1, second_sum, 0.0))
+    stat_land[row] = pair.T[:8]
+    stat_sends, stat_recvs = [], []
+    for step in range(1, row_count):
+        target, source = (row + step) % row_count, (row + row_count - step) % row_count
+        stat_sends.append(put(stat_land.at[row], stat_land.at[row], p_send, p_recv, 35 + step - 1, {"row": target}))
+        stat_recvs.append(
+            put(stat_land.at[source], stat_land.at[source], p_send, p_recv, 35 + step - 1, {"row": source})
+        )
+        stat_sends[-1].start()
+    small[...] = jnp.zeros_like(small)
+    here = strip(row * width, width)
+    small[0:1, :] = jnp.sum(grad1[...] * std1_own[...].astype(f32), axis=0, keepdims=True)
+    small[1:2, :] = jnp.sum(grad1[...], axis=0, keepdims=True)
+    small[2:6, :] = sums[0:4, here]
+    uppers = jnp.sum(dup[...].astype(f32), axis=0, keepdims=True)
+    for k in range(units // width):
+        small[8 + k : 9 + k, :] = uppers[:, k * width : (k + 1) * width]
+    mixes = jnp.sum(d_mix[...].astype(f32), axis=0, keepdims=True)
+    spot = 8 + units // width
+    picked = [mixes[:, (head * 3 + kind) * HEAD : (head * 3 + kind + 1) * HEAD] for head in range(heads) for kind in (0, 2)]
+    small[spot : spot + 1, : 2 * heads * HEAD] = jnp.concatenate(picked, axis=1)
+    to_x = partners()[0]
+    x_copy = put(small.at[pl.ds(0, 8)], x_land, p_send, p_recv, 38, to_x)
+    x_copy.start()
+    middle(6)
+    produce(8)
+    finish(5)
+    x_copy.wait_recv()
+    x_copy.wait_send()
+    small[0:2, :] += x_land[0:2, :]
+    dp_sends, dp_recvs = [], []
+    dp_land[plane] = small[...]
+    for step in range(1, dp_count):
+        target, source = (plane + step) % dp_count, (plane + dp_count - step) % dp_count
+        dp_sends.append(put(dp_land.at[plane], dp_land.at[plane], p_send, p_recv, 39 + step - 1, {"dp": target}))
+        dp_recvs.append(put(dp_land.at[source], dp_land.at[source], p_send, p_recv, 39 + step - 1, {"dp": source}))
+        dp_sends[-1].start()
+    for copy in stat_recvs:
+        copy.wait_recv()
+    both = stat_land[0]
+    for k in range(1, row_count):
+        both = both + stat_land[k]
+    both = jnp.concatenate([both, jnp.zeros((120, rows), f32)], axis=0).T
+    d_norm1 = inv1_own[...] * (
+        scaled1 - both[:, 0:1] / full - std1_own[...].astype(f32) * (both[:, 1:2] / full)
+    )
+    tokens_block[...] = (dres_own[...] + d_norm1).astype(bf16)
+    loads[10].start()
     loads[8].wait()
     tiled_nn(hid, n2, tot, 1024, 256)
-    fourth = reduce_steps(tot, outp_own, *set_a, p_send, p_recv, 24)
+    fourth = reduce_steps(tot, own_sum, *set_a, p_send, p_recv, 24)
     next(fourth)
     next(fourth)
-    produce(8)
-    middle(6)
-    finish(5)
+    middle(7)
+    loads[7].wait()
+    produce(9)
+    finish(6)
     next(fourth)
     next(fourth, None)
-    loads[7].wait()
-    for k in range(9, total):
+    loads[10].wait()
+    out_block[...] = (dres_own[...] + (own_sum[...] + down_bias[...])).astype(bf16)
+    for copy in dp_recvs:
+        copy.wait_recv()
+    together = dp_land[0]
+    for k in range(1, dp_count):
+        together = together + dp_land[k]
+    small_out[row] = together
+    row_sends, row_recvs = [], []
+    for step in range(1, row_count):
+        target, source = (row + step) % row_count, (row + row_count - step) % row_count
+        row_sends.append(put(small_out.at[row], small_out.at[row], p_send, p_recv, 42 + step - 1, {"row": target}))
+        row_recvs.append(
+            put(small_out.at[source], small_out.at[source], p_send, p_recv, 42 + step - 1, {"row": source})
+        )
+        row_sends[-1].start()
+    for k in range(10, total):
+        middle(k - 2)
         produce(k)
-        middle(k - 2)
         finish(k - 3)
     middle(total - 2)
     finish(total - 3)
@@ -1014,6 +1004,10 @@
     finish(total - 2)
     finish(total - 1)
     finish_outer(total - 1)
+    for copy in row_recvs:
+        copy.wait_recv()
+    for copy in down_sends + stat_sends + dp_sends + row_sends:
+        copy.wait_send()
 
     @pl.when(outer)
     def _():
@@ -1034,12 +1028,14 @@
             put(t.at[0, source], place(k, source), a_send, a_recv, 3 * k + step - 1, {"row": source}).wait_recv()
 
 
-def backward_plane(cid, hid, cot, dup, n2, upw, std, n1, qkvw, downw, attended, outw, mixed, lse, bias, inv2, gain2):
+def backward_plane(
+    cid, hid, cot, slope, n2, upw, std, n1, qkvw, down_nat, resid_own, attended, outw, mixed, lse, bias, inv2, vec_all, std1_own, inv1_own, down_bias
+):
     f32, bf16 = jnp.float32, jnp.bfloat16
     length, full = cot.shape
     rows, width = length // lax.axis_size("col"), full // lax.axis_size("row")
-    row_count = full // width
-    counts = (dup.shape[1] // CHUNK, dup.shape[1] // CHUNK, attended.shape[1] // CHUNK, mixed.shape[1] // CHUNK)
+    row_count, dp_count = full // width, lax.axis_size("dp")
+    counts = (slope.shape[1] // CHUNK, slope.shape[1] // CHUNK, attended.shape[1] // CHUNK, mixed.shape[1] // CHUNK)
     total = sum(counts)
     one = (row_count, width // CHUNK, CHUNK, CHUNK)
     shape = jax.ShapeDtypeStruct
@@ -1056,21 +1052,20 @@
     return pl.pallas_call(
         functools.partial(backward_kernel, counts),
         out_shape=[
-            shape((2, row_count * counts[0] * CHUNK, CHUNK), bf16),
+            shape((row_count * counts[0], CHUNK, width), bf16),
             shape((2, CHUNK, row_count * counts[1] * CHUNK), bf16),
             shape((2, row_count * counts[2] * CHUNK, CHUNK), bf16),
             shape((2, CHUNK, row_count * counts[3] * CHUNK), bf16),
             shape((total,) + one, bf16),
             shape((total,) + one, bf16),
             shape((total,) + one, bf16),
-            shape((rows, width), f32),
-            shape((rows, width), f32),
-            shape((rows, width), f32),
-            shape((8, full), f32),
-            shape((1, mixed.shape[1]), f32),
+            shape((hid.shape[1], full), bf16),
+            shape((rows, width), bf16),
+            shape((rows, width), bf16),
+            shape((row_count, 16, width), f32),
         ],
-        in_specs=[away] * 9 + [near] * 7,
-        out_specs=[away] * 7 + [near] * 5,
+        in_specs=[away] * 10 + [near] * 10,
+        out_specs=[away] * 8 + [near] * 3,
         scratch_shapes=[
             vmem((length, full), bf16),
             vmem((length, full), bf16),
@@ -1079,12 +1074,12 @@
             vmem((length, full), bf16),
             vmem(upw.shape, bf16),
             vmem(hid.shape, bf16),
-            vmem(dup.shape, bf16),
+            vmem(slope.shape, bf16),
             vmem(attended.shape, bf16),
             vmem(mixed.shape, bf16),
             vmem((length, HEAD), f32),
             vmem((length, HEAD), f32),
-            vmem((3,) + one, bf16),
+            vmem((2,) + one, bf16),
             vmem((2,) + one, bf16),
             vmem(one, bf16),
             vmem((2,) + one, bf16),
@@ -1093,48 +1088,423 @@
         + sets
         + [
             vmem((rows, width), f32),
-            dma((9,)),
+            vmem((rows, width), f32),
+            vmem((8, full), f32),
+            vmem((16, width), f32),
+            vmem((8, width), f32),
+            vmem((dp_count, 16, width), f32),
+            vmem((row_count, 8, rows), f32),
+            dma((11,)),
             dma,
-            dma((total,)),
+            dma((total + 1,)),
             dma((3 * total,)),
             dma((3 * total,)),
             dma((3 * total,)),
             dma((3 * total,)),
-            dma((32,)),
-            dma((32,)),
+            dma((45,)),
+            dma((45,)),
         ],
         compiler_params=pltpu.CompilerParams(
             collective_id=cid, has_side_effects=True, vmem_limit_bytes=64 * 1024 * 1024 - 65536
         ),
         cost_estimate=pl.CostEstimate(flops=40_000_000_000, bytes_accessed=100_000_000, transcendentals=4_000_000),
-    )(hid, cot, dup, n2, upw, std, n1, qkvw, downw, attended, outw, mixed, lse, bias, inv2, gain2)
-
-
-def shift_rows(pieces):
-    row, count = lax.axis_index("row"), pieces.shape[0]
-    result = pieces
-    for step in range(1, count):
-        pairs = [(k, (k + step) % count) for k in range(count)]
-        sent = lax.dynamic_index_in_dim(pieces, (row + step) % count, 0, keepdims=True)
-        got = lax.ppermute(sent, "row", pairs)
-        result = lax.dynamic_update_slice_in_dim(result, got, (row + count - step) % count, 0)
-    return result
-
-
-def norm_stats(values):
-    center = jnp.mean(values, axis=1, keepdims=True)
-    spread_of = jnp.mean(values * values, axis=1, keepdims=True) - center * center
-    return center, lax.rsqrt(spread_of + epsilon)
-
-
-def mask_of(span_starts, length):
-    marks = jnp.sum(
-        (span_starts[0][:, None] // SPAN == jnp.arange(length // SPAN, dtype=jnp.int32)[None, :]).astype(jnp.int32),
-        axis=0,
-    )
-    places_of = jnp.arange(length, dtype=jnp.int32)
-    image = jnp.repeat(marks, SPAN)
-    return visible(places_of, image, places_of)
+    )(hid, cot, slope, n2, upw, std, n1, qkvw, down_nat, resid_own, attended, outw, mixed, lse, bias, inv2, vec_all, std1_own, inv1_own, down_bias)
+
+
+class Moves:
+    def __init__(self, source, target, cut, parts, sends, recvs, base):
+        row, plane = lax.axis_index("row"), lax.axis_index("dp")
+        side, core = row // 2, row % 2
+        parity = plane % 2
+        other = {"dp": plane + 1 - 2 * parity}
+        twin = side * 2 + 1 - core
+        far = ((1 - side) * 2 + core, (1 - side) * 2 + 1 - core)
+        self.sibling = put(source(twin), target(row), sends, recvs, base, {"row": twin})
+        self.sibling_in = put(source(twin), target(twin), sends, recvs, base, {"row": twin})
+        self.outs, self.ins, self.passes, self.gets = [], [], [], []
+        at = base + 1
+        for step in range(parts // 2):
+            for k, device in enumerate(far):
+                mine, theirs = 2 * step + parity, 2 * step + 1 - parity
+                there, here = cut(target(row), mine), cut(target(device), mine)
+                self.outs.append(put(cut(source(device), mine), there, sends, recvs, at, {"row": device}))
+                self.ins.append(put(cut(source(device), mine), here, sends, recvs, at, {"row": device}))
+                self.passes.append(put(here, here, sends, recvs, at + 1, other))
+                lands = cut(target(device), theirs)
+                self.gets.append(put(lands, lands, sends, recvs, at + 1, other))
+                at += 2
+
+    @staticmethod
+    def count(parts):
+        return 1 + 2 * parts
+
+    def start(self):
+        self.sibling.start()
+        self.start_far()
+
+    def start_far(self):
+        for copy in self.outs:
+            copy.start()
+
+    def forward(self, begin=0, end=None):
+        for came, passed in list(zip(self.ins, self.passes))[begin:end]:
+            came.wait_recv()
+            passed.start()
+
+    def finish(self):
+        self.sibling_in.wait_recv()
+        for copy in self.gets:
+            copy.wait_recv()
+
+    def drain(self):
+        self.sibling.wait_send()
+        for copy in self.outs + self.passes:
+            copy.wait_send()
+
+
+FAR_PARTS = 4
+
+
+def forward_kernel(
+    tokens,
+    cot_in,
+    vecs,
+    mixed_bias,
+    up_bias,
+    bias,
+    qkv_nat,
+    out_nat,
+    up_nat,
+    cot_all,
+    n1_out,
+    n2_out,
+    std_out,
+    upw_out,
+    qkvw_out,
+    outw_out,
+    mixed_out,
+    attended_out,
+    hid_out,
+    slope_out,
+    lse,
+    inv2,
+    vec_all,
+    resid_own,
+    std1_own,
+    inv1_own,
+    tok,
+    n1,
+    part,
+    tot,
+    qkvw,
+    upw,
+    outw,
+    mixed,
+    attended,
+    hid,
+    slope,
+    own_sum,
+    got,
+    diag,
+    hx,
+    hy,
+    ts,
+    fx,
+    local_sem,
+    w_send,
+    w_recv,
+    p_send,
+    p_recv,
+):
+    f32, bf16 = jnp.float32, jnp.bfloat16
+    plane, row, col = lax.axis_index("dp"), lax.axis_index("row"), lax.axis_index("col")
+    side, core = row // 2, row % 2
+    rows, width = tokens.shape
+    length, full = tok.shape
+    row_count = full // width
+    heads_width = attended.shape[1]
+    units = hid.shape[1]
+
+    barrier = pltpu.get_barrier_semaphore()
+    twins = ({"row": (1 - side) * 2 + 1 - core}, {"dp": plane + 1 - 2 * (plane % 2)})
+    for partner in partners() + twins:
+        pl.semaphore_signal(barrier, inc=1, device_id=partner, device_id_type=MESH)
+    pl.semaphore_wait(barrier, 5)
+
+    def cut_rows(ref, part):
+        count = ref.shape[0] // FAR_PARTS
+        return ref.at[strip(part * count, count)]
+
+    per = qkvw.shape[1]
+    count = Moves.count(FAR_PARTS)
+    qkv_moves = Moves(
+        lambda r: qkv_nat.at[:, strip(r * per, per)],
+        lambda r: qkvw.at[strip(r * width, width), :],
+        cut_rows,
+        FAR_PARTS,
+        w_send,
+        w_recv,
+        0,
+    )
+    out_moves = Moves(
+        lambda r: out_nat.at[strip(r * heads_width, heads_width), :],
+        lambda r: outw.at[:, strip(r * width, width)],
+        cut_rows,
+        FAR_PARTS,
+        w_send,
+        w_recv,
+        count,
+    )
+    up_moves = Moves(
+        lambda r: up_nat.at[:, strip(r * units, units)],
+        lambda r: upw.at[strip(r * width, width), :],
+        cut_rows,
+        FAR_PARTS,
+        w_send,
+        w_recv,
+        2 * count,
+    )
+    locals_ = [
+        (qkv_nat.at[:, strip(row * per, per)], qkvw.at[strip(row * width, width), :]),
+        (out_nat.at[strip(row * heads_width, heads_width), :], outw.at[:, strip(row * width, width)]),
+        (up_nat.at[:, strip(row * units, units)], upw.at[strip(row * width, width), :]),
+        (cot_in, block(cot_all, col, side, core, rows, width)),
+        (n1, n1_out),
+        (part, n2_out),
+        (n1, std_out),
+        (upw, upw_out),
+        (qkvw, qkvw_out),
+        (outw, outw_out),
+        (mixed, mixed_out),
+        (attended, attended_out),
+        (hid, hid_out),
+        (slope, slope_out),
+    ]
+    local = [pltpu.make_async_copy(a, b, local_sem.at[k]) for k, (a, b) in enumerate(locals_)]
+    for k in range(4):
+        local[k].start()
+
+    block(tok, col, side, core, rows, width)[...] = tokens[...]
+    gather = spread_steps(tok, rows, width, p_send, p_recv, 0)
+    next(gather)
+    vec_all[:, strip(row * width, width)] = vecs[...]
+    vec_sends, vec_recvs = [], []
+    for step in range(1, row_count):
+        target, source = (row + step) % row_count, (row + row_count - step) % row_count
+        here, there = vec_all.at[:, strip(row * width, width)], vec_all.at[:, strip(source * width, width)]
+        vec_sends.append(put(here, here, p_send, p_recv, 8 + step - 1, {"row": target}))
+        vec_recvs.append(put(there, there, p_send, p_recv, 8 + step - 1, {"row": source}))
+        vec_sends[-1].start()
+    qkv_moves.sibling.start()
+    out_moves.sibling.start()
+    up_moves.sibling.start()
+    next(gather)
+    qkv_moves.start_far()
+    next(gather)
+    next(gather, None)
+    for copy in vec_recvs:
+        copy.wait_recv()
+
+    tile = 64
+    gain1, shift1 = vec_all[0:1, :], vec_all[1:2, :]
+
+    def norm1_step(k, none):
+        at = strip(k * tile, tile)
+        values = tok[at, :].astype(f32)
+        center = jnp.sum(values, axis=1, keepdims=True) / full
+        inverse = lax.rsqrt(jnp.sum(values * values, axis=1, keepdims=True) / full - center * center + epsilon)
+        n1[at, :] = ((values - center) * inverse * gain1 + shift1).astype(bf16)
+
+        @pl.when(k // (rows // tile) == col)
+        def _():
+            here = strip(k % (rows // tile) * tile, tile)
+            std1_own[here, :] = ((tok[at, strip(row * width, width)].astype(f32) - center) * inverse).astype(bf16)
+            inv1_own[here, :] = inverse
+
+        return none
+
+    half_steps = length // tile // 2
+    lax.fori_loop(0, half_steps, norm1_step, 0)
+    qkv_moves.forward(0, 2)
+    lax.fori_loop(half_steps, 2 * half_steps, norm1_step, 0)
+    local[4].start()
+    qkv_moves.forward(2, 4)
+    out_moves.start_far()
+    up_moves.start_far()
+    qkv_moves.finish()
+    local[0].wait()
+
+    def mixed_step(k, none):
+        down, across = k // (per // CHUNK), k % (per // CHUNK)
+        at, lanes = strip(down * rows, rows), strip(across * CHUNK, CHUNK)
+        value = jnp.dot(n1[at, :], qkvw[:, lanes], preferred_element_type=f32)
+        mixed[at, lanes] = (value + mixed_bias[:, lanes]).astype(bf16)
+        return none
+
+    lax.fori_loop(0, (length // rows) * (per // CHUNK), mixed_step, 0)
+    local[8].start()
+    local[10].start()
+    local[4].wait()
+
+    heads = heads_width // HEAD
+    factor = 1.0 / math.sqrt(HEAD)
+    blocks = length // SPAN
+
+    def head_step(head, none):
+        base = head * 3 * HEAD
+        at_q, at_k, at_v = strip(base, HEAD), strip(base + HEAD, HEAD), strip(base + 2 * HEAD, HEAD)
+        for k in range(blocks):
+            here = pl.ds(k * SPAN, SPAN)
+            seen = (k + 1) * SPAN
+            scores = dot_nt(mixed[here, at_q], mixed[:seen, at_k]) * factor
+            last = scores[:, seen - SPAN :] + bias[k].astype(f32)
+            scores = last if k == 0 else jnp.concatenate([scores[:, : seen - SPAN], last], axis=1)
+            highest = jnp.max(scores, axis=1, keepdims=True)
+            weights = jnp.exp(scores - highest)
+            weight_sum = jnp.sum(weights, axis=1, keepdims=True)
+            lse[head, here] = highest + jnp.log(weight_sum)
+            value = jnp.dot((weights / weight_sum).astype(bf16), mixed[:seen, at_v], preferred_element_type=f32)
+            attended[here, strip(head * HEAD, HEAD)] = value.astype(bf16)
+        return none
+
+    lax.fori_loop(0, heads, head_step, 0)
+    local[11].start()
+    out_moves.forward()
+    up_moves.forward(0, 4)
+    out_moves.finish()
+    local[1].wait()
+    tiled_nn(attended, outw, part, rows, 512)
+    local[9].start()
+    add_up = reduce_steps(part, own_sum, got, diag, hx, hy, ts, fx, p_send, p_recv, 11)
+    next(add_up)
+    next(add_up)
+    up_moves.forward(4, 8)
+    next(add_up)
+    next(add_up, None)
+    block(tot, col, side, core, rows, width)[...] = own_sum[...].astype(bf16)
+    again = spread_steps(tot, rows, width, p_send, p_recv, 19)
+    for k in range(3):
+        next(again)
+    next(again, None)
+    local[3].wait()
+    cot_gather = spread_steps(cot_all, rows, width, p_send, p_recv, 27)
+    next(cot_gather)
+
+    gain2, shift2, out_bias = vec_all[3:4, :], vec_all[4:5, :], vec_all[2:3, :]
+
+    def norm2_step(k, none):
+        at = strip(k * tile, tile)
+        values = tok[at, :].astype(f32) + (tot[at, :].astype(f32) + out_bias)
+        center = jnp.sum(values, axis=1, keepdims=True) / full
+        inverse = lax.rsqrt(jnp.sum(values * values, axis=1, keepdims=True) / full - center * center + epsilon)
+        standard = (values - center) * inverse
+        inv2[at, :] = inverse
+        n1[at, :] = standard.astype(bf16)
+        part[at, :] = (standard * gain2 + shift2).astype(bf16)
+
+        @pl.when(k // (rows // tile) == col)
+        def _():
+            own = strip(row * width, width)
+            here = strip(k % (rows // tile) * tile, tile)
+            resid_own[here, :] = tok[at, own].astype(f32) + (tot[at, own].astype(f32) + vec_all[2:3, own])
+
+        return none
+
+    lax.fori_loop(0, 2 * half_steps, norm2_step, 0)
+    local[5].start()
+    local[6].start()
+    next(cot_gather)
+    up_moves.finish()
+    local[2].wait()
+    local[7].start()
+
+    def up_step(k, none):
+        down, across = k // (units // CHUNK), k % (units // CHUNK)
+        at, lanes = strip(down * rows, rows), strip(across * CHUNK, CHUNK)
+        u = jnp.dot(part[at, :], upw[:, lanes], preferred_element_type=f32) + up_bias[:, lanes]
+        bent = jnp.tanh(0.7978845608028654 * (u + 0.044715 * u * u * u))
+        hid[at, lanes] = (0.5 * u * (1.0 + bent)).astype(bf16)
+        inside = 0.7978845608028654 * (1.0 + 3 * 0.044715 * u * u)
+        slope[at, lanes] = (0.5 * (1.0 + bent) + 0.5 * u * (1.0 - bent * bent) * inside).astype(bf16)
+        return none
+
+    lax.fori_loop(0, (length // rows) * (units // CHUNK), up_step, 0)
+    local[12].start()
+    local[13].start()
+    next(cot_gather)
+    next(cot_gather, None)
+    for k in range(5, 14):
+        local[k].wait()
+    for moves in (qkv_moves, out_moves, up_moves):
+        moves.drain()
+    for copy in vec_sends:
+        copy.wait_send()
+
+
+def forward_plane(cid, tokens, cot, vecs, mixed_bias, up_bias, bias, qkv_nat, out_nat, up_nat):
+    f32, bf16 = jnp.float32, jnp.bfloat16
+    rows, width = tokens.shape
+    row_count = lax.axis_size("row")
+    length, full = rows * lax.axis_size("col"), width * row_count
+    per, heads_width, units = qkv_nat.shape[1] // row_count, out_nat.shape[0] // row_count, up_nat.shape[1] // row_count
+    shape = jax.ShapeDtypeStruct
+    away, near = pl.BlockSpec(memory_space=pl.ANY), pl.BlockSpec(memory_space=pltpu.VMEM)
+    vmem, dma = pltpu.VMEM, pltpu.SemaphoreType.DMA
+    wide = shape((length, full), bf16)
+    moved = 3 * Moves.count(FAR_PARTS)
+    return pl.pallas_call(
+        forward_kernel,
+        out_shape=[
+            wide,
+            wide,
+            wide,
+            wide,
+            shape((full, units), bf16),
+            shape((full, per), bf16),
+            shape((heads_width, full), bf16),
+            shape((length, per), bf16),
+            shape((length, heads_width), bf16),
+            shape((length, units), bf16),
+            shape((length, units), bf16),
+            shape((heads_width // HEAD, length, 1), f32),
+            shape((length, 1), f32),
+            shape((8, full), f32),
+            shape((rows, width), f32),
+            shape((rows, width), bf16),
+            shape((rows, 1), f32),
+        ],
+        in_specs=[near] * 6 + [away] * 3,
+        out_specs=[away] * 11 + [near] * 6,
+        scratch_shapes=[
+            vmem((length, full), bf16),
+            vmem((length, full), bf16),
+            vmem((length, full), bf16),
+            vmem((length, full), bf16),
+            vmem((full, per), bf16),
+            vmem((full, units), bf16),
+            vmem((heads_width, full), bf16),
+            vmem((length, per), bf16),
+            vmem((length, heads_width), bf16),
+            vmem((length, units), bf16),
+            vmem((length, units), bf16),
+            vmem((rows, width), f32),
+            vmem((4, rows, width), bf16),
+            vmem((rows, width), bf16),
+            vmem((rows // 2, width), bf16),
+            vmem((rows // 2, width), bf16),
+            vmem((2, rows, width), bf16),
+            vmem((2, rows, width), bf16),
+            dma((14,)),
+            dma((moved,)),
+            dma((moved,)),
+            dma((35,)),
+            dma((35,)),
+        ],
+        compiler_params=pltpu.CompilerParams(
+            collective_id=cid, has_side_effects=True, vmem_limit_bytes=60 * 1024 * 1024
+        ),
+        cost_estimate=pl.CostEstimate(flops=10_000_000_000, bytes_accessed=60_000_000, transcendentals=4_000_000),
+    )(tokens, cot, vecs, mixed_bias, up_bias, bias, qkv_nat, out_nat, up_nat)
 
 
 def plane_plan(
@@ -1154,137 +1524,61 @@
     span_starts,
     cotangent,
 ):
-    f32, bf16 = jnp.float32, jnp.bfloat16
+    f32 = jnp.float32
     rows, width = tokens.shape
     row_count = lax.axis_size("row")
-    col, row = lax.axis_index("col"), lax.axis_index("row")
-    length, full = rows * lax.axis_size("col"), width * row_count
+    row = lax.axis_index("row")
+    length = rows * lax.axis_size("col")
     heads = qkv_weight.shape[1] // row_count
-    hidden_count = up_weight.shape[1] // row_count
-    factor = 1.0 / math.sqrt(HEAD)
-
-    def own(values):
-        return lax.dynamic_slice(values, (col * rows, row * width), (rows, width))
-
-    def own_width(values):
-        return lax.dynamic_slice_in_dim(values, row * width, width, values.ndim - 1)
-
-    def wide(vector):
-        return lax.all_gather(vector, "row", axis=0, tiled=True)
-
-    qkv_flat = shift_rows(
-        jnp.moveaxis(qkv_weight.reshape(width, row_count, heads * 3 * HEAD), 1, 0)
-    ).reshape(full, heads * 3 * HEAD)
-    out_flat = jnp.moveaxis(
-        shift_rows(out_weight.reshape(row_count, heads * HEAD, width)), 0, 1
-    ).reshape(heads * HEAD, full)
-    up_flat = shift_rows(jnp.moveaxis(up_weight.reshape(width, row_count, hidden_count), 1, 0)).reshape(
-        full, hidden_count
-    )
-    down_flat = jnp.moveaxis(
-        shift_rows(down_weight.reshape(row_count, hidden_count, width)), 0, 1
-    ).reshape(hidden_count, full)
-    vectors = wide(jnp.stack([ln1_gain, ln1_shift, out_bias, ln2_gain, ln2_shift], axis=0).T)
-    gain1, shift1, branch_bias, gain2, shift2 = [vectors[:, k] for k in range(5)]
+    units = up_weight.shape[1] // row_count
+
+    blank = jnp.zeros_like(ln1_gain)
+    vecs = jnp.stack([ln1_gain, ln1_shift, out_bias, ln2_gain, ln2_shift, blank, blank, blank], axis=0)
     own_qv = lax.dynamic_slice_in_dim(qv_bias, row * heads, heads, 0)
-    own_up_bias = lax.dynamic_slice_in_dim(up_bias, row * hidden_count, hidden_count, 0)
-    allowed = mask_of(span_starts, length)
-
-    tokens_all = gather_plane(tokens, 1)
-    cot_all = gather_plane(cotangent, 2)
-    inputs = tokens_all.astype(f32)
-    center1, inverse1 = norm_stats(inputs)
-    normed1 = ((inputs - center1) * inverse1 * gain1 + shift1).astype(bf16)
-    mixed = product(normed1, qkv_flat, False).reshape(length, heads, 3, HEAD)
-    queries = (mixed[:, :, 0] + own_qv[:, 0]).astype(bf16)
-    key_rows = mixed[:, :, 1].astype(bf16)
-    value_rows = (mixed[:, :, 2] + own_qv[:, 1]).astype(bf16)
-    scores = jnp.einsum("qhd,khd->hqk", queries, key_rows, preferred_element_type=f32) * factor
-    scores = jnp.where(allowed[None], scores, masked_score)
-    highest = jnp.max(scores, axis=2, keepdims=True)
-    weights = jnp.exp(scores - highest)
-    weight_sum = jnp.sum(weights, axis=2, keepdims=True)
-    logsum = highest + jnp.log(weight_sum)
-    attended = jnp.einsum("hqk,khd->qhd", (weights / weight_sum).astype(bf16), value_rows, preferred_element_type=f32)
-    attended = attended.astype(bf16).reshape(length, heads * HEAD)
-    branch = total_plane(product(attended, out_flat, False).astype(bf16), 3)
-    residual = inputs + (branch.astype(f32) + branch_bias)
-    center2, inverse2 = norm_stats(residual)
-    standard2 = (residual - center2) * inverse2
-    normed2 = (standard2 * gain2 + shift2).astype(bf16)
-    up_sums = product(normed2, up_flat, False) + own_up_bias
-    hidden = gelu_tanh(up_sums).astype(bf16)
-    d_hidden = product(cot_all, down_flat, True)
-    d_upper = jax.vjp(gelu_tanh, up_sums)[1](d_hidden)[0].astype(bf16)
-
+    mixed_bias = jnp.stack([own_qv[:, 0], jnp.zeros_like(own_qv[:, 0]), own_qv[:, 1]], axis=1).reshape(1, -1)
+    own_up_bias = lax.dynamic_slice_in_dim(up_bias, row * units, units, 0)[None]
     blocks = length // SPAN
-    places_of = jnp.arange(SPAN, dtype=jnp.int32)
+    spots = jnp.arange(SPAN, dtype=jnp.int32)
     marked = jnp.any(span_starts[0][:, None] // SPAN == jnp.arange(blocks, dtype=jnp.int32)[None, :], axis=0)
-    open_pairs = (places_of[None, :] <= places_of[:, None])[None] | marked[:, None, None]
-    bias = jnp.where(open_pairs, 0.0, masked_score).astype(f32)
-    mixed_rows = jnp.stack([queries, key_rows, value_rows], axis=2).reshape(length, heads * 3 * HEAD)
-    down_grad, up_grad, out_grad, qkv_grad, _, _, _, d_residual, d_normed1, sums_out, sums2, mixed_sums = backward_plane(
-        4,
-        hidden,
-        cot_all,
-        d_upper,
-        normed2,
-        up_flat,
-        standard2.astype(bf16),
-        normed1,
-        qkv_flat,
-        down_flat,
-        attended,
-        out_flat,
-        mixed_rows,
-        logsum,
+    open_pairs = (spots[None, :] <= spots[:, None])[None] | marked[:, None, None]
+    bias = jnp.where(open_pairs, 0.0, masked_score).astype(jnp.bfloat16)
+
+    (
+        cot_all, n1, n2, standard2, upw, qkvw, outw, mixed, attended, hidden, slope,
+        lse, inverse2, vec_all, residual_own, standard1_own, inverse1_own,
+    ) = forward_plane(
+        1,
+        tokens,
+        cotangent,
+        vecs,
+        mixed_bias,
+        own_up_bias,
         bias,
-        inverse2,
-        gain2[None],
-    )
-    standard1 = own((inputs - center1) * inverse1)
-    own_inverse1 = lax.dynamic_slice_in_dim(inverse1, col * rows, rows, 0)
-    d_norm1, gain1_grad, shift1_grad = norm_backward(
-        d_normed1, standard1, own_inverse1[:, 0], ln1_gain
-    )
-    tokens_grad = (d_residual + d_norm1).astype(bf16)
-    output = (own(residual) + (sums_out + down_bias)).astype(bf16)
-
-    near = [
-        own_width(sums2[0]),
-        own_width(sums2[1]),
-        own_width(sums2[2]),
-        jnp.sum(own_width(cot_all), axis=0, dtype=f32),
-    ]
-    totals = mixed_sums.reshape(heads, 3, HEAD)
-    spread_sums = [
-        jnp.sum(d_upper, axis=0, dtype=f32),
-        jnp.stack([totals[:, 0], totals[:, 2]], axis=1).reshape(heads * 2 * HEAD),
-    ]
-    slots = [lax.dynamic_update_index_in_dim(jnp.zeros((row_count,) + v.shape, f32), v, row, 0) for v in spread_sums]
-    own_slots = [lax.dynamic_update_index_in_dim(jnp.zeros((row_count,) + v.shape, f32), v, row, 0) for v in near]
-    summed = lax.psum(jnp.concatenate(slots + own_slots, axis=1), ("dp", "row"))
-    up_bias_grad = summed[:, :hidden_count].reshape(-1)
-    begin = hidden_count + heads * 2 * HEAD
-    qv_bias_grad = summed[:, hidden_count:begin].reshape(row_count * heads, 2, HEAD)
-    mine = lax.dynamic_index_in_dim(summed[:, begin:], row, 0, keepdims=False).reshape(4, width)
-    norm1_sums = lax.psum((gain1_grad, shift1_grad), ("dp", "col"))
-
+        qkv_weight.reshape(width, -1),
+        out_weight.reshape(-1, width),
+        up_weight,
+    )
+    down_grad, up_grad, out_grad, qkv_grad, _, _, _, _, output, tokens_grad, small = backward_plane(
+        2, hidden, cot_all, slope, n2, upw, standard2, n1, qkvw, down_weight, residual_own, attended, outw, mixed, lse, bias,
+        inverse2, vec_all, standard1_own, inverse1_own, down_bias[None],
+    )
+    mine = lax.dynamic_index_in_dim(small, row, 0, keepdims=False)
+    spot = 8 + units // width
     return (
         output,
         tokens_grad,
-        norm1_sums[0],
-        norm1_sums[1],
-        qkv_grad.astype(f32).reshape(width, row_count * heads, 3, HEAD),
-        qv_bias_grad,
-        jnp.moveaxis(out_grad, 0, 1).astype(f32).reshape(row_count * heads, HEAD, width),
-        mine[2],
         mine[0],
         mine[1],
-        up_grad.astype(f32).reshape(width, row_count * hidden_count),
-        up_bias_grad,
-        jnp.moveaxis(down_grad, 0, 1).astype(f32).reshape(row_count * hidden_count, width),
+        qkv_grad.astype(f32).reshape(width, row_count * heads, 3, HEAD),
+        small[:, spot, : 2 * heads * HEAD].reshape(row_count * heads, 2, HEAD),
+        jnp.moveaxis(out_grad, 0, 1).astype(f32).reshape(row_count * heads, HEAD, width),
+        mine[4],
+        mine[2],
         mine[3],
+        up_grad.astype(f32).reshape(width, row_count * units),
+        small[:, 8:spot].reshape(-1),
+        down_grad.astype(f32).reshape(row_count * units, width),
+        mine[5],
     )
 
 

time: 862 us -> 580 us (0.67)
  local copies, waits for them, and re-layouts: 141 us -> 38.2 us
  blocking collectives: 89.9 us -> 0 us
  other arithmetic: 48.6 us -> 11.6 us
  matrix products: 32.1 us -> 0 us
  waiting for transfers between devices: 24.2 us -> 0 us
  Pallas kernels: 503 us -> 526 us
  starting transfers between devices: 9.76 us -> 0 us
    psum x3 -> x0, blocking collectives: 84.6 us -> none  [the longest x1 59.5 us: plane_plan(): summed = lax.psum(jnp.concatenate(slots + own_slots, axis=1), ('dp', 'row'))]
    dynamic_update_slice x19 -> x0, local copies, waits for them, and re-layouts: 51.8 us -> none  [the longest x13 50.9 us: shift_rows(): lax.dynamic_update_slice_in_dim(result, got, (row + count - step) % count...]
    dot_general x6 -> x0, matrix products: 32.1 us -> none  [the longest x3 17.6 us: product(): return jnp.dot(left_side, right_side, preferred_element_type=jnp.float32)]
    unnamed x74 -> x28, local copies, waits for them, and re-layouts: 42.6 us -> 18.2 us
    ppermute x12 -> x0, waiting for transfers between devices: 24.2 us -> none  [shift_rows(): got = lax.ppermute(sent, 'row', pairs)]
    pallas_call x1, Pallas kernels: 360 us -> 381 us  [backward_plane(): pl.pallas_call(functools.partial(backward_kernel, counts), out_shape=[sha...]
    reduce_sum x6 -> x0, other arithmetic: 14.8 us -> none  [the longest x2 9.34 us: norm_stats(): center = jnp.mean(values, axis=1, keepdims=True)]
    dynamic_slice x8 -> x1, local copies, waits for them, and re-layouts: 15.8 us -> 1.28 us  [plane_plan(): own_up_bias = lax.dynamic_slice_in_dim(up_bias, row * units, units, 0)[None]]
  transfers between devices with their start and end apart: 12 -> 0, of which waited for: 2 -> 0; matrix products, arithmetic and copies ran while one was open for 16% -> 0% of each run, Pallas kernels for 17% -> 0%
where the time goes in v3:
time: 580 us; the launch traced here: 576 us
  Pallas kernels  526 us (91%)
  local copies, waits for them, and re-layouts  38.2 us (7%)
  other arithmetic  11.6 us (2%)
    pallas_call x1, Pallas kernels, backward_plane(): pl.pallas_call(functools.partial(backward_kernel, counts), out_shape=[sha...  381 us
    pallas_call x1, Pallas kernels, forward_plane(): pl.pallas_call(forward_kernel, out_shape=[wide, wide, wide, wide, shape((...  145 us
    unnamed x28, local copies, waits for them, and re-layouts  18.2 us

profile of v3, /device:TPU:0, one launch (start us, length us, event | category | flops | bytes accessed | tf_op | source)
XLA Modules:
  0.0 576.4 jit_solution(2270284440409220994)
XLA Ops:
  0.7 0.8 constant_dynamic-slice_fusion.5
  1.4 0.1 pad.1.clone
  1.5 0.1 pad_maximum_fusion
  1.6 0.6 reshape.148.mixed_bias
  2.2 1.3 dynamic_slice.11
  3.5 0.7 and_select_fusion
  4.1 0.1 compare_reduce_fusion
  4.2 1.0 select_convert_fusion.bias
  5.2 3.8 copy.37
  9.1 0.0 copy-start.5
  9.1 0.0 copy-start.6
  9.1 0.0 copy-start.7
  9.1 0.0 copy-start.8
  9.1 0.0 copy-start.9
  9.1 3.0 copy.38.qkv_nat
  12.2 0.0 copy-done.5
  12.2 0.0 copy-done.6
  12.2 0.0 copy-done.7
  12.2 0.0 copy-done.8
  12.2 0.0 copy-done.9
  12.2 0.6 stack.30.vecs
  12.8 144.5 %shard_map.254 = (bf16[1024,2048]{1,0:T(8,128)(2,1)}, bf16[1024,2048]{1,0:T(8,128)(2,1)}, bf16[1024,2048]{1,0:T(8,128)(2,1)}, bf16[1024,2048]{1,0:T(8,128)(2,1)}...) custom-call(bf16[512,512]{1,0:T(8,128)(2,1)} %tokens.1, ...), custom_call_target="tpu_custom_call" | custom-call | flops 10000000000 | bytes 60000000 | tf_op jit(solution)/shard_map/pallas_call | solution.py:1455
  157.4 381.3 %shard_map.255 = (bf16[16,256,512]{2,1,0:T(8,128)(2,1)}, bf16[2,256,4096]{2,1,0:T(8,128)(2,1)}, bf16[2,1024,256]{2,1,0:T(8,128)(2,1)}, bf16[2,256,3072]{2,1,0:T(...) custom-call(bf16[1024,1024]{1,0:T(8,128)(2,1)} %get-tuple-element.38, ...), custom_call_target="tpu_custom_call" | custom-call | flops 40000000000 | bytes 100000000 | tf_op jit(solution)/shard_map/pallas_call | solution.py:1052
  538.7 10.6 %reshape.169 = f32[512,8,3,128]{3,2,1,0:T(4,128)} reshape(bf16[2,256,3072]{2,1,0:T(8,128)(2,1)} %get-tuple-element.58) | data formatting | bytes 9437184 | tf_op jit(solution)/shard_map/reshape | solution.py:1572
  549.3 0.0 copy-start.1
  549.3 7.0 %copy.41 = f32[512,8,3,128]{3,1,2,0:T(8,128)} copy(f32[512,8,3,128]{3,2,1,0:T(4,128)} %reshape.169) | data formatting | bytes 12582912
  556.3 0.0 copy-done.1
  556.3 0.0 copy-start
  556.3 4.9 bitcast_convert_fusion
  561.2 0.0 copy-done
  561.2 0.0 copy-start.2
  561.2 4.8 bitcast_convert_fusion.1
  565.9 0.0 copy-done.2
  565.9 0.2 convert_bitcast_fusion
  566.1 0.0 copy-start.4
  566.1 0.0 copy-start.3
  566.1 1.6 copy.45
  567.7 2.7 reshape.170
  570.4 0.8 slice_bitcast_fusion
  571.2 0.6 copy.47
  571.9 1.5 constant_dynamic-slice_fusion.6
  573.4 1.4 slice.40
  574.8 0.0 copy-done.4
  574.9 0.8 copy.50
  575.6 0.0 copy-done.3
  575.6 0.8 copy.51
  (3 shorter events, 0.0 us)
Async XLA Ops:
  9.1 3.1 copy-start.5
  9.1 3.1 copy-start.6
  9.1 3.1 copy-start.7
  9.1 3.1 copy-start.8
  9.1 3.1 copy-start.9
  549.3 7.0 %copy-start.1 = (bf16[16,256,512]{2,1,0:T(8,128)(2,1)S(1)}, bf16[16,256,512]{2,1,0:T(8,128)(2,1)}, u32[]{:S(2)}) copy-start(bf16[16,256,512]{2,1,0:T(8,128)(2,1)} %get-tuple-element.61) | copy-start | bytes 12582916
  556.3 4.9 copy-start
  561.2 4.8 copy-start.2
  566.1 8.8 %copy-start.4 = (bf16[512,512]{1,0:T(8,128)(2,1)S(1)}, bf16[512,512]{1,0:T(8,128)(2,1)}, u32[]{:S(2)}) copy-start(bf16[512,512]{1,0:T(8,128)(2,1)} %get-tuple-element.126) | copy-start | bytes 1572868
  566.1 9.6 %copy-start.3 = (bf16[512,512]{1,0:T(8,128)(2,1)S(1)}, bf16[512,512]{1,0:T(8,128)(2,1)}, u32[]{:S(2)}) copy-start(bf16[512,512]{1,0:T(8,128)(2,1)} %get-tuple-element.127) | copy-start | bytes 1572868

commit v4 on v3

--- a/solution.py
+++ b/solution.py
@@ -545,9 +545,8 @@
     attended,
     outw,
     mixed,
-    lse,
-    bias,
-    inv2,
+    stats,
+    marks,
     vec_all,
     std1_own,
     inv1_own,
@@ -556,8 +555,6 @@
     up_out,
     out_out,
     qkv_out,
-    r_land,
-    m_land,
     b_land,
     downw_land,
     out_block,
@@ -577,8 +574,9 @@
     dv_acc,
     g,
     s,
-    ld,
     t,
+    r_land,
+    m_land,
     got_a,
     diag_a,
     hx_a,
@@ -599,7 +597,7 @@
     dp_land,
     stat_land,
     load_sem,
-    ld_sem,
+    credit,
     own_sem,
     z_send,
     z_recv,
@@ -656,56 +654,62 @@
         down_recvs.append(put(piece, there, p_send, p_recv, 32 + step - 1, {"row": source}))
         down_sends[-1].start()
     down_own = pltpu.make_async_copy(
-        down_nat.at[strip(row * units, units), :], downw_land.at[:, strip(row * width, width)], own_sem.at[total]
+        down_nat.at[strip(row * units, units), :], downw_land.at[:, strip(row * width, width)], own_sem.at[2 * total]
     )
     down_own.start()
 
-    def place(i, source):
+    def place(u, source):
+        i, half = u // 2, u % 2
         if i < n_down:
-            return down_out.at[strip(source * n_down + i // 2 * 2, 2), :, pl.ds(i % 2 * CHUNK, CHUNK)]
+            return down_out.at[source * n_down + i // 2 * 2 + half, :, pl.ds(i % 2 * CHUNK, CHUNK)]
         i -= n_down
         if i < n_up:
-            return up_out.at[:, :, strip(source * n_up * CHUNK + i * CHUNK, CHUNK)]
+            return up_out.at[half, :, strip(source * n_up * CHUNK + i * CHUNK, CHUNK)]
         i -= n_up
         if i < n_out:
-            return out_out.at[:, strip(source * n_out * CHUNK + i * CHUNK, CHUNK), :]
+            return out_out.at[source * n_out + i, :, pl.ds(half * CHUNK, CHUNK)]
         i -= n_out
-        return qkv_out.at[:, :, strip(source * n_qkv * CHUNK + i * CHUNK, CHUNK)]
-
-    g_slots, s_slots = g.shape[0], s.shape[0]
-
-    def inward(i):
-        return put(g.at[i % g_slots], r_land.at[i], z_send, z_recv, i, to_inner)
-
-    def across(i):
-        return put(s.at[i % s_slots], m_land.at[i], z_send, z_recv, total + i, to_middle)
-
-    def outward(i):
-        return put(t.at[i % s_slots], b_land.at[i], z_send, z_recv, 2 * total + i, to_outer)
-
-    def home(i, step, source):
+        return qkv_out.at[half, :, strip(source * n_qkv * CHUNK + i * CHUNK, CHUNK)]
+
+    g_slots, s_slots, t_slots, r_slots, m_slots = g.shape[0], s.shape[0], t.shape[0], r_land.shape[0], m_land.shape[0]
+    pieces = 2 * total
+
+    def made(u):
+        return g.at[u // 2 % g_slots, :, u % 2]
+
+    def inward(u):
+        return put(made(u), r_land.at[u % r_slots], z_send, z_recv, u, to_inner)
+
+    def across(u):
+        return put(s.at[u % s_slots], m_land.at[u % m_slots], z_send, z_recv, pieces + u, to_middle)
+
+    def outward(u):
+        return put(t.at[u % t_slots], b_land.at[u], z_send, z_recv, 2 * pieces + u, to_outer)
+
+    def home(u, step, source):
         target = (row + step) % row_count
-        return put(source.at[target], place(i, row), a_send, a_recv, 3 * i + step - 1, {"row": target})
-
-    def home_own(i, source):
-        return pltpu.make_async_copy(source.at[row], place(i, row), own_sem.at[i])
-
-    def send_home(i, source):
+        return put(source.at[target], place(u, row), a_send, a_recv, 3 * u + step - 1, {"row": target})
+
+    def home_own(u, source):
+        return pltpu.make_async_copy(source.at[row], place(u, row), own_sem.at[u])
+
+    def send_home(u, source):
         for step in range(1, row_count):
-            home(i, step, source).start()
-        home_own(i, source).start()
-
-    def sent_home(i, source):
+            home(u, step, source).start()
+        home_own(u, source).start()
+
+    def sent_home(u, source):
         for step in range(1, row_count):
-            home(i, step, source).wait_send()
-        home_own(i, source).wait()
+            home(u, step, source).wait_send()
+        home_own(u, source).wait()
 
     def produce(i):
         if i >= g_slots:
 
             @pl.when(outer)
             def _():
-                inward(i - g_slots).wait_send()
+                inward(2 * (i - g_slots)).wait_send()
+                inward(2 * (i - g_slots) + 1).wait_send()
 
         slot = g.at[i % g_slots]
         if i < n_down:
@@ -738,54 +742,54 @@
 
         lax.fori_loop(0, row_count, step, 0)
 
+    def launch(u):
         @pl.when(outer)
         def _():
-            inward(i).start()
-
-    def add(first, target):
-        def step(k, none):
-            for half in range(2):
-                target[k, half] = (first[k, half].astype(f32) + ld[k, half].astype(f32)).astype(bf16)
-            return none
-
-        lax.fori_loop(0, row_count, step, 0)
-
-    def fetch(source):
-        copy = pltpu.make_async_copy(source, ld, ld_sem)
-        copy.start()
-        copy.wait()
-
-    def middle(i):
+            if u >= r_slots:
+                pl.semaphore_wait(credit, 1)
+            inward(u).start()
+
+    def add(first, second, target):
+        for k in range(row_count):
+            target[k] = (first[k].astype(f32) + second[k].astype(f32)).astype(bf16)
+
+    def middle(u):
         @pl.when(inner)
         def _():
-            inward(i).wait_recv()
-            fetch(r_land.at[i])
-            add(g.at[i % g_slots], s.at[i % s_slots])
-            across(i).start()
-
-    def finish_inner(i):
+            inward(u).wait_recv()
+            add(made(u), r_land.at[u % r_slots], s.at[u % s_slots])
+            across(u).start()
+            if u + r_slots < pieces:
+                pl.semaphore_signal(credit, inc=1, device_id=to_outer, device_id_type=MESH)
+
+    def finish_inner(u):
         @pl.when(inner)
         def _():
-            if i >= s_slots:
-                outward(i - s_slots).wait_send()
-                sent_home(i - s_slots, t.at[i % s_slots])
-            across(i).wait_recv()
-            fetch(m_land.at[i])
-            add(s.at[i % s_slots], t.at[i % s_slots])
-            outward(i).start()
-            send_home(i, t.at[i % s_slots])
-            across(i).wait_send()
-
-    def finish_outer(i):
+            if u >= t_slots:
+                outward(u - t_slots).wait_send()
+                sent_home(u - t_slots, t.at[u % t_slots])
+            across(u).wait_recv()
+            add(s.at[u % s_slots], m_land.at[u % m_slots], t.at[u % t_slots])
+            outward(u).start()
+            send_home(u, t.at[u % t_slots])
+            across(u).wait_send()
+
+    def finish_outer(u):
         @pl.when(outer)
         def _():
-            outward(i).wait_recv()
-            send_home(i, b_land.at[i])
-
-    def finish(i):
-        finish_inner(i)
-        if i >= 1:
-            finish_outer(i - 1)
+            outward(u).wait_recv()
+            send_home(u, b_land.at[u])
+
+    def turn(u):
+        if u + 2 < pieces:
+            if u % 2 == 0:
+                produce((u + 2) // 2)
+            launch(u + 2)
+        middle(u)
+        if u >= 1:
+            finish_inner(u - 1)
+        if u >= 2:
+            finish_outer(u - 2)
 
     set_a = (got_a, diag_a, hx_a, hy_a, ts_a, fx_a)
     set_b = (got_b, diag_b, hx_b, hy_b, ts_b, fx_b)
@@ -794,18 +798,19 @@
     loads[0].wait()
     loads[1].wait()
     produce(0)
-    produce(1)
+    launch(0)
+    launch(1)
     sums[...] = jnp.zeros_like(sums)
-    middle(0)
-    produce(2)
+    turn(0)
+    turn(1)
+    turn(2)
     down_own.wait()
     for copy in down_recvs:
         copy.wait_recv()
     loads[9].start()
     loads[2].wait()
-    middle(1)
-    produce(3)
-    finish(0)
+    loads[3].wait()
+    turn(3)
     loads[9].wait()
 
     def upper_step(k, none):
@@ -815,33 +820,32 @@
         return none
 
     lax.fori_loop(0, (length // rows) * (units // CHUNK), upper_step, 0)
-    loads[3].wait()
+    turn(4)
     tiled_nt(dup, upw, part, dup.shape[1], 1024, 256)
     loads[6].start()
     first = reduce_steps(part, own_sum, *set_a, p_send, p_recv, 0)
     next(first)
-    next(first)
     loads[4].wait()
     loads[5].wait()
+    turn(5)
     next(first)
-    middle(2)
-    produce(4)
+    next(first)
+    turn(6)
     next(first, None)
     block(tot, col, side, core, rows, width)[...] = own_sum[...].astype(bf16)
     second = spread_steps(tot, rows, width, p_send, p_recv, 8)
     next(second)
-    finish(1)
+    turn(7)
     next(second)
     next(second)
-    middle(3)
-    produce(5)
+    turn(8)
     next(second, None)
 
     tile = 64
 
     def norm_step(k, none):
         at = strip(k * tile, tile)
-        grad, standard, inverse = tot[at, :].astype(f32), std[at, :].astype(f32), inv2[at, :]
+        grad, standard, inverse = tot[at, :].astype(f32), std[at, :].astype(f32), stats[at, 0:1]
         scaled = grad * gain2
         mean_one = jnp.sum(scaled, axis=1, keepdims=True) / full
         mean_two = jnp.sum(scaled * standard, axis=1, keepdims=True) / full
@@ -865,12 +869,14 @@
 
     lax.fori_loop(0, length // tile, norm_step, 0)
     loads[7].start()
-    finish(2)
+    turn(9)
     tiled_nt(part, outw, d_att, full, 512, 256)
 
     heads = mixed.shape[1] // (3 * HEAD)
     factor = 1.0 / math.sqrt(HEAD)
     blocks = length // SPAN
+    spots = (SPAN, SPAN)
+    earlier = lax.broadcasted_iota(jnp.int32, spots, 1) <= lax.broadcasted_iota(jnp.int32, spots, 0)
 
     def head_step(head, none):
         base = head * 3 * HEAD
@@ -884,9 +890,9 @@
             query, dout = mixed[here, at_q], d_att[here, at_o]
             keys, values = mixed[:seen, at_k], mixed[:seen, at_v]
             scores = dot_nt(query, keys) * factor
-            last = scores[:, seen - SPAN :] + bias[k].astype(f32)
+            last = jnp.where(earlier | (marks[k : k + 1, :1] > 0), scores[:, seen - SPAN :], masked_score)
             scores = last if k == 0 else jnp.concatenate([scores[:, : seen - SPAN], last], axis=1)
-            probs = jnp.exp(scores - lse[head, here])
+            probs = jnp.exp(scores - stats[here, 1 + head : 2 + head])
             d_probs = dot_nt(dout, values)
             dots = jnp.sum(probs * d_probs, axis=1, keepdims=True)
             d_scores = (probs * (d_probs - dots)).astype(bf16)
@@ -897,20 +903,18 @@
         d_mix[:, at_v] = dv_acc[...].astype(bf16)
         return none
 
-    lax.fori_loop(0, heads, head_step, 0)
-    middle(4)
-    produce(6)
-    finish(3)
+    for head in range(heads):
+        head_step(head, 0)
+        turn(10 + head)
     loads[6].wait()
     tiled_nt(d_mix, upw, cot, d_mix.shape[1], 1024, 256)
     third = reduce_steps(cot, own_sum, *set_b, p_send, p_recv, 16)
     next(third)
     next(third)
-    middle(5)
-    produce(7)
+    turn(12)
+    next(third)
+    turn(13)
     loads[8].start()
-    finish(4)
-    next(third)
     next(third, None)
 
     grad1, gain1 = own_sum, vec_all[0:1, strip(row * width, width)]
@@ -943,9 +947,7 @@
     to_x = partners()[0]
     x_copy = put(small.at[pl.ds(0, 8)], x_land, p_send, p_recv, 38, to_x)
     x_copy.start()
-    middle(6)
-    produce(8)
-    finish(5)
+    turn(14)
     x_copy.wait_recv()
     x_copy.wait_send()
     small[0:2, :] += x_land[0:2, :]
@@ -972,10 +974,9 @@
     fourth = reduce_steps(tot, own_sum, *set_a, p_send, p_recv, 24)
     next(fourth)
     next(fourth)
-    middle(7)
     loads[7].wait()
-    produce(9)
-    finish(6)
+    turn(15)
+    turn(16)
     next(fourth)
     next(fourth, None)
     loads[10].wait()
@@ -994,16 +995,11 @@
             put(small_out.at[source], small_out.at[source], p_send, p_recv, 42 + step - 1, {"row": source})
         )
         row_sends[-1].start()
-    for k in range(10, total):
-        middle(k - 2)
-        produce(k)
-        finish(k - 3)
-    middle(total - 2)
-    finish(total - 3)
-    middle(total - 1)
-    finish(total - 2)
-    finish(total - 1)
-    finish_outer(total - 1)
+    for u in range(17, pieces):
+        turn(u)
+    finish_inner(pieces - 1)
+    finish_outer(pieces - 2)
+    finish_outer(pieces - 1)
     for copy in row_recvs:
         copy.wait_recv()
     for copy in down_sends + stat_sends + dp_sends + row_sends:
@@ -1011,25 +1007,25 @@
 
     @pl.when(outer)
     def _():
-        for k in range(total - g_slots, total):
-            inward(k).wait_send()
-        for k in range(total):
-            sent_home(k, b_land.at[k])
+        for u in range(pieces - 2 * g_slots, pieces):
+            inward(u).wait_send()
+        for u in range(pieces):
+            sent_home(u, b_land.at[u])
 
     @pl.when(inner)
     def _():
-        for k in range(total - s_slots, total):
-            outward(k).wait_send()
-            sent_home(k, t.at[k % s_slots])
-
-    for k in range(total):
+        for u in range(pieces - t_slots, pieces):
+            outward(u).wait_send()
+            sent_home(u, t.at[u % t_slots])
+
+    for u in range(pieces):
         for step in range(1, row_count):
             source = (row + row_count - step) % row_count
-            put(t.at[0, source], place(k, source), a_send, a_recv, 3 * k + step - 1, {"row": source}).wait_recv()
+            put(t.at[0, source], place(u, source), a_send, a_recv, 3 * u + step - 1, {"row": source}).wait_recv()
 
 
 def backward_plane(
-    cid, hid, cot, slope, n2, upw, std, n1, qkvw, down_nat, resid_own, attended, outw, mixed, lse, bias, inv2, vec_all, std1_own, inv1_own, down_bias
+    cid, hid, cot, slope, n2, upw, std, n1, qkvw, down_nat, resid_own, attended, outw, mixed, stats, marks, vec_all, std1_own, inv1_own, down_bias
 ):
     f32, bf16 = jnp.float32, jnp.bfloat16
     length, full = cot.shape
@@ -1037,7 +1033,7 @@
     row_count, dp_count = full // width, lax.axis_size("dp")
     counts = (slope.shape[1] // CHUNK, slope.shape[1] // CHUNK, attended.shape[1] // CHUNK, mixed.shape[1] // CHUNK)
     total = sum(counts)
-    one = (row_count, width // CHUNK, CHUNK, CHUNK)
+    unit = (row_count, CHUNK, CHUNK)
     shape = jax.ShapeDtypeStruct
     away, near = pl.BlockSpec(memory_space=pl.ANY), pl.BlockSpec(memory_space=pltpu.VMEM)
     vmem, dma = pltpu.VMEM, pltpu.SemaphoreType.DMA
@@ -1054,18 +1050,16 @@
         out_shape=[
             shape((row_count * counts[0], CHUNK, width), bf16),
             shape((2, CHUNK, row_count * counts[1] * CHUNK), bf16),
-            shape((2, row_count * counts[2] * CHUNK, CHUNK), bf16),
+            shape((row_count * counts[2], CHUNK, width), bf16),
             shape((2, CHUNK, row_count * counts[3] * CHUNK), bf16),
-            shape((total,) + one, bf16),
-            shape((total,) + one, bf16),
-            shape((total,) + one, bf16),
+            shape((2 * total,) + unit, bf16),
             shape((hid.shape[1], full), bf16),
             shape((rows, width), bf16),
             shape((rows, width), bf16),
             shape((row_count, 16, width), f32),
         ],
-        in_specs=[away] * 10 + [near] * 10,
-        out_specs=[away] * 8 + [near] * 3,
+        in_specs=[away] * 10 + [near] * 9,
+        out_specs=[away] * 6 + [near] * 3,
         scratch_shapes=[
             vmem((length, full), bf16),
             vmem((length, full), bf16),
@@ -1079,10 +1073,11 @@
             vmem(mixed.shape, bf16),
             vmem((length, HEAD), f32),
             vmem((length, HEAD), f32),
-            vmem((2,) + one, bf16),
-            vmem((2,) + one, bf16),
-            vmem(one, bf16),
-            vmem((2,) + one, bf16),
+            vmem((2, row_count, width // CHUNK, CHUNK, CHUNK), bf16),
+            vmem((2,) + unit, bf16),
+            vmem((2,) + unit, bf16),
+            vmem((3,) + unit, bf16),
+            vmem((4,) + unit, bf16),
         ]
         + sets
         + sets
@@ -1095,12 +1090,12 @@
             vmem((dp_count, 16, width), f32),
             vmem((row_count, 8, rows), f32),
             dma((11,)),
-            dma,
-            dma((total + 1,)),
-            dma((3 * total,)),
-            dma((3 * total,)),
-            dma((3 * total,)),
-            dma((3 * total,)),
+            pltpu.SemaphoreType.REGULAR,
+            dma((2 * total + 1,)),
+            dma((6 * total,)),
+            dma((6 * total,)),
+            dma((6 * total,)),
+            dma((6 * total,)),
             dma((45,)),
             dma((45,)),
         ],
@@ -1108,7 +1103,7 @@
             collective_id=cid, has_side_effects=True, vmem_limit_bytes=64 * 1024 * 1024 - 65536
         ),
         cost_estimate=pl.CostEstimate(flops=40_000_000_000, bytes_accessed=100_000_000, transcendentals=4_000_000),
-    )(hid, cot, slope, n2, upw, std, n1, qkvw, down_nat, resid_own, attended, outw, mixed, lse, bias, inv2, vec_all, std1_own, inv1_own, down_bias)
+    )(hid, cot, slope, n2, upw, std, n1, qkvw, down_nat, resid_own, attended, outw, mixed, stats, marks, vec_all, std1_own, inv1_own, down_bias)
 
 
 class Moves:
@@ -1171,8 +1166,8 @@
     vecs,
     mixed_bias,
     up_bias,
-    bias,
-    qkv_nat,
+    marks,
+    qkv_in,
     out_nat,
     up_nat,
     cot_all,
@@ -1186,8 +1181,7 @@
     attended_out,
     hid_out,
     slope_out,
-    lse,
-    inv2,
+    stats,
     vec_all,
     resid_own,
     std1_own,
@@ -1210,6 +1204,8 @@
     hy,
     ts,
     fx,
+    qkv_raw,
+    qkv_nat,
     local_sem,
     w_send,
     w_recv,
@@ -1279,9 +1275,11 @@
         (attended, attended_out),
         (hid, hid_out),
         (slope, slope_out),
+        (qkv_in, qkv_raw),
     ]
     local = [pltpu.make_async_copy(a, b, local_sem.at[k]) for k, (a, b) in enumerate(locals_)]
-    for k in range(4):
+    local[14].start()
+    for k in range(1, 4):
         local[k].start()
 
     block(tok, col, side, core, rows, width)[...] = tokens[...]
@@ -1295,9 +1293,15 @@
         vec_sends.append(put(here, here, p_send, p_recv, 8 + step - 1, {"row": target}))
         vec_recvs.append(put(there, there, p_send, p_recv, 8 + step - 1, {"row": source}))
         vec_sends[-1].start()
-    qkv_moves.sibling.start()
     out_moves.sibling.start()
     up_moves.sibling.start()
+    local[14].wait()
+    for kind in range(3):
+        flat = qkv_raw[:, kind].reshape(width, qkv_raw.shape[2] * HEAD)
+        for head in range(qkv_raw.shape[2]):
+            qkv_nat[:, pl.ds((head * 3 + kind) * HEAD, HEAD)] = flat[:, head * HEAD : (head + 1) * HEAD]
+    local[0].start()
+    qkv_moves.sibling.start()
     next(gather)
     qkv_moves.start_far()
     next(gather)
@@ -1349,6 +1353,8 @@
     heads = heads_width // HEAD
     factor = 1.0 / math.sqrt(HEAD)
     blocks = length // SPAN
+    spots = (SPAN, SPAN)
+    earlier = lax.broadcasted_iota(jnp.int32, spots, 1) <= lax.broadcasted_iota(jnp.int32, spots, 0)
 
     def head_step(head, none):
         base = head * 3 * HEAD
@@ -1357,17 +1363,18 @@
             here = pl.ds(k * SPAN, SPAN)
             seen = (k + 1) * SPAN
             scores = dot_nt(mixed[here, at_q], mixed[:seen, at_k]) * factor
-            last = scores[:, seen - SPAN :] + bias[k].astype(f32)
+            last = jnp.where(earlier | (marks[k : k + 1, :1] > 0), scores[:, seen - SPAN :], masked_score)
             scores = last if k == 0 else jnp.concatenate([scores[:, : seen - SPAN], last], axis=1)
             highest = jnp.max(scores, axis=1, keepdims=True)
             weights = jnp.exp(scores - highest)
             weight_sum = jnp.sum(weights, axis=1, keepdims=True)
-            lse[head, here] = highest + jnp.log(weight_sum)
+            stats[here, 1 + head : 2 + head] = highest + jnp.log(weight_sum)
             value = jnp.dot((weights / weight_sum).astype(bf16), mixed[:seen, at_v], preferred_element_type=f32)
             attended[here, strip(head * HEAD, HEAD)] = value.astype(bf16)
         return none
 
-    lax.fori_loop(0, heads, head_step, 0)
+    for head in range(heads):
+        head_step(head, 0)
     local[11].start()
     out_moves.forward()
     up_moves.forward(0, 4)
@@ -1398,7 +1405,7 @@
         center = jnp.sum(values, axis=1, keepdims=True) / full
         inverse = lax.rsqrt(jnp.sum(values * values, axis=1, keepdims=True) / full - center * center + epsilon)
         standard = (values - center) * inverse
-        inv2[at, :] = inverse
+        stats[at, 0:1] = inverse
         n1[at, :] = standard.astype(bf16)
         part[at, :] = (standard * gain2 + shift2).astype(bf16)
 
@@ -1441,12 +1448,12 @@
         copy.wait_send()
 
 
-def forward_plane(cid, tokens, cot, vecs, mixed_bias, up_bias, bias, qkv_nat, out_nat, up_nat):
+def forward_plane(cid, tokens, cot, vecs, mixed_bias, up_bias, marks, qkv_in, out_nat, up_nat):
     f32, bf16 = jnp.float32, jnp.bfloat16
     rows, width = tokens.shape
     row_count = lax.axis_size("row")
     length, full = rows * lax.axis_size("col"), width * row_count
-    per, heads_width, units = qkv_nat.shape[1] // row_count, out_nat.shape[0] // row_count, up_nat.shape[1] // row_count
+    per, heads_width, units = qkv_in.shape[1] * qkv_in.shape[2] * HEAD // row_count, out_nat.shape[0] // row_count, up_nat.shape[1] // row_count
     shape = jax.ShapeDtypeStruct
     away, near = pl.BlockSpec(memory_space=pl.ANY), pl.BlockSpec(memory_space=pltpu.VMEM)
     vmem, dma = pltpu.VMEM, pltpu.SemaphoreType.DMA
@@ -1466,15 +1473,14 @@
             shape((length, heads_width), bf16),
             shape((length, units), bf16),
             shape((length, units), bf16),
-            shape((heads_width // HEAD, length, 1), f32),
-            shape((length, 1), f32),
+            shape((length, 8), f32),
             shape((8, full), f32),
             shape((rows, width), f32),
             shape((rows, width), bf16),
             shape((rows, 1), f32),
         ],
         in_specs=[near] * 6 + [away] * 3,
-        out_specs=[away] * 11 + [near] * 6,
+        out_specs=[away] * 11 + [near] * 5,
         scratch_shapes=[
             vmem((length, full), bf16),
             vmem((length, full), bf16),
@@ -1494,7 +1500,9 @@
             vmem((rows // 2, width), bf16),
             vmem((2, rows, width), bf16),
             vmem((2, rows, width), bf16),
-            dma((14,)),
+            vmem(qkv_in.shape, bf16),
+            vmem((width, row_count * per), bf16),
+            dma((15,)),
             dma((moved,)),
             dma((moved,)),
             dma((35,)),
@@ -1504,7 +1512,27 @@
             collective_id=cid, has_side_effects=True, vmem_limit_bytes=60 * 1024 * 1024
         ),
         cost_estimate=pl.CostEstimate(flops=10_000_000_000, bytes_accessed=60_000_000, transcendentals=4_000_000),
-    )(tokens, cot, vecs, mixed_bias, up_bias, bias, qkv_nat, out_nat, up_nat)
+    )(tokens, cot, vecs, mixed_bias, up_bias, marks, qkv_in, out_nat, up_nat)
+
+
+def head_order_kernel(flat, result):
+    for head in range(result.shape[2]):
+        for kind in range(3):
+            begin = (head * 3 + kind) * HEAD
+            result[:, kind, head, :] = flat[:, begin : begin + HEAD].astype(jnp.float32)
+
+
+def head_order(flat):
+    rows, heads = flat.shape[0], flat.shape[1] // (3 * HEAD)
+    tile = 128
+    result = pl.pallas_call(
+        head_order_kernel,
+        grid=(rows // tile,),
+        out_shape=jax.ShapeDtypeStruct((rows, 3, heads, HEAD), jnp.float32),
+        in_specs=[pl.BlockSpec((tile, flat.shape[1]), lambda k: (k, 0))],
+        out_specs=pl.BlockSpec((tile, 3, heads, HEAD), lambda k: (k, 0, 0, 0)),
+    )(flat)
+    return jnp.swapaxes(result, 1, 2)
 
 
 def plane_plan(
@@ -1538,14 +1566,12 @@
     mixed_bias = jnp.stack([own_qv[:, 0], jnp.zeros_like(own_qv[:, 0]), own_qv[:, 1]], axis=1).reshape(1, -1)
     own_up_bias = lax.dynamic_slice_in_dim(up_bias, row * units, units, 0)[None]
     blocks = length // SPAN
-    spots = jnp.arange(SPAN, dtype=jnp.int32)
     marked = jnp.any(span_starts[0][:, None] // SPAN == jnp.arange(blocks, dtype=jnp.int32)[None, :], axis=0)
-    open_pairs = (spots[None, :] <= spots[:, None])[None] | marked[:, None, None]
-    bias = jnp.where(open_pairs, 0.0, masked_score).astype(jnp.bfloat16)
+    marks = jnp.broadcast_to(jnp.pad(marked.astype(f32), (0, -blocks % 8))[:, None], (blocks + -blocks % 8, 128))
 
     (
         cot_all, n1, n2, standard2, upw, qkvw, outw, mixed, attended, hidden, slope,
-        lse, inverse2, vec_all, residual_own, standard1_own, inverse1_own,
+        stats, vec_all, residual_own, standard1_own, inverse1_own,
     ) = forward_plane(
         1,
         tokens,
@@ -1553,14 +1579,14 @@
         vecs,
         mixed_bias,
         own_up_bias,
-        bias,
-        qkv_weight.reshape(width, -1),
+        marks,
+        jnp.swapaxes(qkv_weight, 1, 2),
         out_weight.reshape(-1, width),
         up_weight,
     )
-    down_grad, up_grad, out_grad, qkv_grad, _, _, _, _, output, tokens_grad, small = backward_plane(
-        2, hidden, cot_all, slope, n2, upw, standard2, n1, qkvw, down_weight, residual_own, attended, outw, mixed, lse, bias,
-        inverse2, vec_all, standard1_own, inverse1_own, down_bias[None],
+    down_grad, up_grad, out_grad, qkv_grad, _, _, output, tokens_grad, small = backward_plane(
+        2, hidden, cot_all, slope, n2, upw, standard2, n1, qkvw, down_weight, residual_own, attended, outw, mixed, stats, marks,
+        vec_all, standard1_own, inverse1_own, down_bias[None],
     )
     mine = lax.dynamic_index_in_dim(small, row, 0, keepdims=False)
     spot = 8 + units // width
@@ -1569,9 +1595,9 @@
         tokens_grad,
         mine[0],
         mine[1],
-        qkv_grad.astype(f32).reshape(width, row_count * heads, 3, HEAD),
+        head_order(qkv_grad.reshape(width, -1)),
         small[:, spot, : 2 * heads * HEAD].reshape(row_count * heads, 2, HEAD),
-        jnp.moveaxis(out_grad, 0, 1).astype(f32).reshape(row_count * heads, HEAD, width),
+        out_grad.astype(f32).reshape(row_count * heads, HEAD, width),
         mine[4],
         mine[2],
         mine[3],

time: 580 us -> 536 us (0.924)
  local copies, waits for them, and re-layouts: 38.2 us -> 10.9 us
  Pallas kernels: 526 us -> 501 us
    pallas_call x1, Pallas kernels: 381 us -> 350 us  [backward_plane(): pl.pallas_call(functools.partial(backward_kernel, counts), out_shape=[sha...]
    unnamed x28 -> x12, local copies, waits for them, and re-layouts: 18.2 us -> 3.06 us
    reshape x2 -> x0, local copies, waits for them, and re-layouts: 13.6 us -> none  [the longest x1 10.6 us: plane_plan(): qkv_grad.astype(f32).reshape(width, row_count * heads, 3, HEAD)]
    pallas_call x0 -> x1, Pallas kernels: none -> 6.75 us  [head_order(): pl.pallas_call(head_order_kernel, grid=(rows // tile,), out_shape=jax.Sha...]
where the time goes in v4:
time: 536 us; the launch traced here: 527 us
  Pallas kernels  501 us (93%)
  other arithmetic  14.1 us (3%)
  local copies, waits for them, and re-layouts  10.9 us (2%)
    pallas_call x1, Pallas kernels, backward_plane(): pl.pallas_call(functools.partial(backward_kernel, counts), out_shape=[sha...  350 us
    pallas_call x1, Pallas kernels, forward_plane(): pl.pallas_call(forward_kernel, out_shape=[wide, wide, wide, wide, shape((...  144 us

profile of v4, /device:TPU:0, one launch (start us, length us, event | category | flops | bytes accessed | tf_op | source)
XLA Modules:
  0.0 526.9 jit_solution(13276042207706161173)
XLA Ops:
  0.7 0.8 constant_dynamic-slice_fusion.5
  1.4 0.1 pad.10.clone
  1.5 0.1 pad_maximum_fusion
  1.6 0.6 reshape.130.mixed_bias
  2.2 1.3 dynamic_slice.11
  3.4 0.7 and_select_fusion
  4.1 0.1 compare_reduce_fusion
  4.2 0.7 broadcast_in_dim.14.marks
  4.9 1.4 stack.30.vecs
  6.2 143.9 %shard_map.254 = (bf16[1024,2048]{1,0:T(8,128)(2,1)}, bf16[1024,2048]{1,0:T(8,128)(2,1)}, bf16[1024,2048]{1,0:T(8,128)(2,1)}, bf16[1024,2048]{1,0:T(8,128)(2,1)}...) custom-call(bf16[512,512]{1,0:T(8,128)(2,1)} %tokens.1, ...), custom_call_target="tpu_custom_call" | custom-call | flops 10000000000 | bytes 60000000 | tf_op jit(solution)/shard_map/pallas_call | solution.py:1462
  150.2 350.1 %shard_map.255 = (bf16[16,256,512]{2,1,0:T(8,128)(2,1)}, bf16[2,256,4096]{2,1,0:T(8,128)(2,1)}, bf16[4,256,512]{2,1,0:T(8,128)(2,1)}, bf16[2,256,3072]{2,1,0:T(8...) custom-call(bf16[1024,1024]{1,0:T(8,128)(2,1)} %get-tuple-element.37, ...), custom_call_target="tpu_custom_call" | custom-call | flops 40000000000 | bytes 100000000 | tf_op jit(solution)/shard_map/pallas_call | solution.py:1048
  500.3 0.0 copy-start
  500.3 6.9 %bitcast_convert_fusion = f32[4096,512]{1,0:T(8,128)} fusion(bf16[16,256,512]{2,1,0:T(8,128)(2,1)} %get-tuple-element.59), kind=kLoop, calls=%fused_computation | loop fusion | flops 2097152 | bytes 12582912 | tf_op jit(solution)/shard_map/reshape | solution.py:1606
  507.2 0.0 copy-done
  507.2 4.8 bitcast_convert_fusion.1
  512.0 0.0 copy-start.1
  512.0 0.0 copy-start.3
  512.0 6.7 %shard_map.256 = f32[512,3,8,128]{3,2,1,0:T(8,128)} custom-call(bf16[512,3072]{1,0:T(8,128)(2,1)} %bitcast.39), custom_call_target="tpu_custom_call" | custom-call | tf_op jit(solution)/shard_map/pallas_call | solution.py:1528
  518.7 0.0 copy-start.2
  518.8 0.0 copy-done.1
  518.8 1.6 convert.5
  520.4 0.8 slice_bitcast_fusion
  521.2 0.6 copy.29
  521.8 1.6 constant_dynamic-slice_fusion.6
  523.4 1.4 slice.40
  524.9 0.0 copy-done.3
  524.9 0.8 copy.32
  525.7 0.0 copy-done.2
  525.7 0.8 copy.33
  (3 shorter events, 0.0 us)
Async XLA Ops:
  500.3 6.9 %copy-start = (bf16[2,256,4096]{2,1,0:T(8,128)(2,1)S(1)}, bf16[2,256,4096]{2,1,0:T(8,128)(2,1)}, u32[]{:S(2)}) copy-start(bf16[2,256,4096]{2,1,0:T(8,128)(2,1)} %get-tuple-element.58) | copy-start | bytes 12582916
  512.0 6.8 %copy-start.1 = (bf16[4,256,512]{2,1,0:T(8,128)(2,1)S(1)}, bf16[4,256,512]{2,1,0:T(8,128)(2,1)}, u32[]{:S(2)}) copy-start(bf16[4,256,512]{2,1,0:T(8,128)(2,1)} %get-tuple-element.57) | copy-start | bytes 3145732
  512.0 12.9 %copy-start.3 = (bf16[512,512]{1,0:T(8,128)(2,1)S(1)}, bf16[512,512]{1,0:T(8,128)(2,1)}, u32[]{:S(2)}) copy-start(bf16[512,512]{1,0:T(8,128)(2,1)} %get-tuple-element.82) | copy-start | bytes 1572868
  518.7 6.9 %copy-start.2 = (bf16[512,512]{1,0:T(8,128)(2,1)S(1)}, bf16[512,512]{1,0:T(8,128)(2,1)}, u32[]{:S(2)}) copy-start(bf16[512,512]{1,0:T(8,128)(2,1)} %get-tuple-element.83) | copy-start | bytes 1572868

commit v5 on v4

--- a/solution.py
+++ b/solution.py
@@ -488,7 +488,7 @@
         copy.wait_send()
 
 
-def spread_steps(out, rows, width, sends, recvs, base):
+def spread_steps(out, rows, width, sends, recvs, base, mostly_x=False):
     col, side, core = places()
     to_x, to_y, to_core = partners()
 
@@ -501,8 +501,8 @@
         copy_of(0, own, to_x),
         copy_of(1, own, to_y),
         copy_of(2, own, to_core),
-        copy_of(3, ox, to_y, 0),
-        copy_of(4, oy, to_x, 1),
+        None if mostly_x else copy_of(3, ox, to_y, 0),
+        copy_of(4, oy, to_x, None if mostly_x else 1),
         copy_of(5, ox, to_core),
         copy_of(6, oy, to_core),
         copy_of(7, od, to_core),
@@ -510,21 +510,24 @@
     for at in (0, 1, 2):
         plan[at].start()
     yield
+    used = [at for at in range(8) if at != 3 or not mostly_x]
     plan[0].wait_recv()
-    plan[3].start()
+    if not mostly_x:
+        plan[3].start()
     plan[1].wait_recv()
     plan[4].start()
     plan[5].start()
     plan[6].start()
     yield
-    plan[3].wait_recv()
+    if not mostly_x:
+        plan[3].wait_recv()
     plan[4].wait_recv()
     plan[7].start()
     yield
     for at in (2, 5, 6, 7):
         plan[at].wait_recv()
-    for copy in plan:
-        copy.wait_send()
+    for at in used:
+        plan[at].wait_send()
 
 
 CHUNK = 256
@@ -542,13 +545,13 @@
     qkvw_h,
     down_nat,
     resid_h,
-    attended,
-    outw,
-    mixed,
+    attended_h,
+    outw_h,
+    mixed_h,
+    std1_h,
     stats,
     marks,
     vec_all,
-    std1_own,
     inv1_own,
     down_bias,
     down_out,
@@ -568,6 +571,10 @@
     upw,
     hid,
     dup,
+    attended,
+    outw,
+    mixed,
+    std1_own,
     d_att,
     d_mix,
     dk_acc,
@@ -632,9 +639,13 @@
         (downw_land, n2),
         (downw_land, tot),
         (resid_h, dres_own),
+        (attended_h, attended),
+        (outw_h, outw),
+        (mixed_h, mixed),
+        (std1_h, std1_own),
     ]
     loads = [pltpu.make_async_copy(a, b, load_sem.at[k]) for k, (a, b) in enumerate(loads)]
-    for k in range(6):
+    for k in (0, 1, 2, 3, 4, 5, 11, 12, 13, 14):
         loads[k].start()
 
     dp_count = dp_land.shape[0]
@@ -781,13 +792,13 @@
             send_home(u, b_land.at[u])
 
     def turn(u):
+        middle(u)
+        if u >= 1:
+            finish_inner(u - 1)
         if u + 2 < pieces:
             if u % 2 == 0:
                 produce((u + 2) // 2)
             launch(u + 2)
-        middle(u)
-        if u >= 1:
-            finish_inner(u - 1)
         if u >= 2:
             finish_outer(u - 2)
 
@@ -810,6 +821,7 @@
     loads[9].start()
     loads[2].wait()
     loads[3].wait()
+    loads[4].wait()
     turn(3)
     loads[9].wait()
 
@@ -825,20 +837,22 @@
     loads[6].start()
     first = reduce_steps(part, own_sum, *set_a, p_send, p_recv, 0)
     next(first)
-    loads[4].wait()
-    loads[5].wait()
     turn(5)
     next(first)
+    turn(6)
     next(first)
-    turn(6)
+    turn(7)
+    for k in (5, 11, 12, 13, 14):
+        loads[k].wait()
     next(first, None)
     block(tot, col, side, core, rows, width)[...] = own_sum[...].astype(bf16)
     second = spread_steps(tot, rows, width, p_send, p_recv, 8)
     next(second)
-    turn(7)
+    turn(8)
     next(second)
+    turn(9)
     next(second)
-    turn(8)
+    turn(10)
     next(second, None)
 
     tile = 64
@@ -869,7 +883,6 @@
 
     lax.fori_loop(0, length // tile, norm_step, 0)
     loads[7].start()
-    turn(9)
     tiled_nt(part, outw, d_att, full, 512, 256)
 
     heads = mixed.shape[1] // (3 * HEAD)
@@ -905,16 +918,18 @@
 
     for head in range(heads):
         head_step(head, 0)
-        turn(10 + head)
+        turn(11 + head)
     loads[6].wait()
     tiled_nt(d_mix, upw, cot, d_mix.shape[1], 1024, 256)
     third = reduce_steps(cot, own_sum, *set_b, p_send, p_recv, 16)
     next(third)
+    turn(11 + heads)
     next(third)
-    turn(12)
+    loads[8].start()
+    turn(12 + heads)
     next(third)
-    turn(13)
-    loads[8].start()
+    loads[7].wait()
+    turn(13 + heads)
     next(third, None)
 
     grad1, gain1 = own_sum, vec_all[0:1, strip(row * width, width)]
@@ -947,7 +962,7 @@
     to_x = partners()[0]
     x_copy = put(small.at[pl.ds(0, 8)], x_land, p_send, p_recv, 38, to_x)
     x_copy.start()
-    turn(14)
+    turn(14 + heads)
     x_copy.wait_recv()
     x_copy.wait_send()
     small[0:2, :] += x_land[0:2, :]
@@ -973,11 +988,11 @@
     tiled_nn(hid, n2, tot, 1024, 256)
     fourth = reduce_steps(tot, own_sum, *set_a, p_send, p_recv, 24)
     next(fourth)
+    turn(15 + heads)
     next(fourth)
-    loads[7].wait()
-    turn(15)
-    turn(16)
+    turn(16 + heads)
     next(fourth)
+    turn(17 + heads)
     next(fourth, None)
     loads[10].wait()
     out_block[...] = (dres_own[...] + (own_sum[...] + down_bias[...])).astype(bf16)
@@ -995,7 +1010,7 @@
             put(small_out.at[source], small_out.at[source], p_send, p_recv, 42 + step - 1, {"row": source})
         )
         row_sends[-1].start()
-    for u in range(17, pieces):
+    for u in range(18 + heads, pieces):
         turn(u)
     finish_inner(pieces - 1)
     finish_outer(pieces - 2)
@@ -1025,7 +1040,7 @@
 
 
 def backward_plane(
-    cid, hid, cot, slope, n2, upw, std, n1, qkvw, down_nat, resid_own, attended, outw, mixed, stats, marks, vec_all, std1_own, inv1_own, down_bias
+    cid, hid, cot, slope, n2, upw, std, n1, qkvw, down_nat, resid_own, attended, outw, mixed, std1_own, stats, marks, vec_all, inv1_own, down_bias
 ):
     f32, bf16 = jnp.float32, jnp.bfloat16
     length, full = cot.shape
@@ -1058,7 +1073,7 @@
             shape((rows, width), bf16),
             shape((row_count, 16, width), f32),
         ],
-        in_specs=[away] * 10 + [near] * 9,
+        in_specs=[away] * 14 + [near] * 5,
         out_specs=[away] * 6 + [near] * 3,
         scratch_shapes=[
             vmem((length, full), bf16),
@@ -1069,6 +1084,10 @@
             vmem(upw.shape, bf16),
             vmem(hid.shape, bf16),
             vmem(slope.shape, bf16),
+            vmem(attended.shape, bf16),
+            vmem(outw.shape, bf16),
+            vmem(mixed.shape, bf16),
+            vmem(std1_own.shape, bf16),
             vmem(attended.shape, bf16),
             vmem(mixed.shape, bf16),
             vmem((length, HEAD), f32),
@@ -1089,7 +1108,7 @@
             vmem((8, width), f32),
             vmem((dp_count, 16, width), f32),
             vmem((row_count, 8, rows), f32),
-            dma((11,)),
+            dma((15,)),
             pltpu.SemaphoreType.REGULAR,
             dma((2 * total + 1,)),
             dma((6 * total,)),
@@ -1103,7 +1122,7 @@
             collective_id=cid, has_side_effects=True, vmem_limit_bytes=64 * 1024 * 1024 - 65536
         ),
         cost_estimate=pl.CostEstimate(flops=40_000_000_000, bytes_accessed=100_000_000, transcendentals=4_000_000),
-    )(hid, cot, slope, n2, upw, std, n1, qkvw, down_nat, resid_own, attended, outw, mixed, stats, marks, vec_all, std1_own, inv1_own, down_bias)
+    )(hid, cot, slope, n2, upw, std, n1, qkvw, down_nat, resid_own, attended, outw, mixed, std1_own, stats, marks, vec_all, inv1_own, down_bias)
 
 
 class Moves:
@@ -1585,8 +1604,8 @@
         up_weight,
     )
     down_grad, up_grad, out_grad, qkv_grad, _, _, output, tokens_grad, small = backward_plane(
-        2, hidden, cot_all, slope, n2, upw, standard2, n1, qkvw, down_weight, residual_own, attended, outw, mixed, stats, marks,
-        vec_all, standard1_own, inverse1_own, down_bias[None],
+        2, hidden, cot_all, slope, n2, upw, standard2, n1, qkvw, down_weight, residual_own, attended, outw, mixed, standard1_own,
+        stats, marks, vec_all, inverse1_own, down_bias[None],
     )
     mine = lax.dynamic_index_in_dim(small, row, 0, keepdims=False)
     spot = 8 + units // width

time: 536 us -> 511 us (0.953)
  Pallas kernels: 501 us -> 476 us
    pallas_call x1, Pallas kernels: 350 us -> 326 us  [backward_plane(): pl.pallas_call(functools.partial(backward_kernel, counts), out_shape=[sha...]
where the time goes in v5:
time: 511 us; the launch traced here: 503 us
  Pallas kernels  476 us (93%)
  other arithmetic  14.1 us (3%)
  local copies, waits for them, and re-layouts  10.9 us (2%)
    pallas_call x1, Pallas kernels, backward_plane(): pl.pallas_call(functools.partial(backward_kernel, counts), out_shape=[sha...  326 us
    pallas_call x1, Pallas kernels, forward_plane(): pl.pallas_call(forward_kernel, out_shape=[wide, wide, wide, wide, shape((...  144 us

profile of v5, /device:TPU:0, one launch (start us, length us, event | category | flops | bytes accessed | tf_op | source)
XLA Modules:
  0.0 502.6 jit_solution(4952317391742459546)
XLA Ops:
  0.7 0.8 constant_dynamic-slice_fusion.5
  1.4 0.1 pad.10.clone
  1.5 0.1 pad_maximum_fusion
  1.6 0.6 reshape.130.mixed_bias
  2.2 1.3 dynamic_slice.11
  3.4 0.7 and_select_fusion
  4.1 0.1 compare_reduce_fusion
  4.2 0.7 broadcast_in_dim.14.marks
  4.9 1.4 stack.30.vecs
  6.2 143.9 %shard_map.254 = (bf16[1024,2048]{1,0:T(8,128)(2,1)}, bf16[1024,2048]{1,0:T(8,128)(2,1)}, bf16[1024,2048]{1,0:T(8,128)(2,1)}, bf16[1024,2048]{1,0:T(8,128)(2,1)}...) custom-call(bf16[512,512]{1,0:T(8,128)(2,1)} %tokens.1, ...), custom_call_target="tpu_custom_call" | custom-call | flops 10000000000 | bytes 60000000 | tf_op jit(solution)/shard_map/pallas_call | solution.py:1481
  150.2 325.8 %shard_map.255 = (bf16[16,256,512]{2,1,0:T(8,128)(2,1)}, bf16[2,256,4096]{2,1,0:T(8,128)(2,1)}, bf16[4,256,512]{2,1,0:T(8,128)(2,1)}, bf16[2,256,3072]{2,1,0:T(8...) custom-call(bf16[1024,1024]{1,0:T(8,128)(2,1)} %get-tuple-element.37, ...), custom_call_target="tpu_custom_call" | custom-call | flops 40000000000 | bytes 100000000 | tf_op jit(solution)/shard_map/pallas_call | solution.py:1063
  476.0 0.0 copy-start
  476.0 6.9 %bitcast_convert_fusion = f32[4096,512]{1,0:T(8,128)} fusion(bf16[16,256,512]{2,1,0:T(8,128)(2,1)} %get-tuple-element.59), kind=kLoop, calls=%fused_computation | loop fusion | flops 2097152 | bytes 12582912 | tf_op jit(solution)/shard_map/reshape | solution.py:1625
  482.9 0.0 copy-done
  482.9 4.8 bitcast_convert_fusion.1
  487.7 0.0 copy-start.1
  487.7 0.0 copy-start.3
  487.7 6.7 %shard_map.256 = f32[512,3,8,128]{3,2,1,0:T(8,128)} custom-call(bf16[512,3072]{1,0:T(8,128)(2,1)} %bitcast.39), custom_call_target="tpu_custom_call" | custom-call | tf_op jit(solution)/shard_map/pallas_call | solution.py:1547
  494.5 0.0 copy-start.2
  494.5 0.0 copy-done.1
  494.5 1.6 convert.5
  496.1 0.8 slice_bitcast_fusion
  496.9 0.6 copy.29
  497.5 1.6 constant_dynamic-slice_fusion.6
  499.1 1.4 slice.40
  500.6 0.0 copy-done.3
  500.6 0.8 copy.32
  501.4 0.0 copy-done.2
  501.4 0.8 copy.33
  (3 shorter events, 0.0 us)
Async XLA Ops:
  476.0 6.9 %copy-start = (bf16[2,256,4096]{2,1,0:T(8,128)(2,1)S(1)}, bf16[2,256,4096]{2,1,0:T(8,128)(2,1)}, u32[]{:S(2)}) copy-start(bf16[2,256,4096]{2,1,0:T(8,128)(2,1)} %get-tuple-element.58) | copy-start | bytes 12582916
  487.7 6.8 %copy-start.1 = (bf16[4,256,512]{2,1,0:T(8,128)(2,1)S(1)}, bf16[4,256,512]{2,1,0:T(8,128)(2,1)}, u32[]{:S(2)}) copy-start(bf16[4,256,512]{2,1,0:T(8,128)(2,1)} %get-tuple-element.57) | copy-start | bytes 3145732
  487.7 12.9 %copy-start.3 = (bf16[512,512]{1,0:T(8,128)(2,1)S(1)}, bf16[512,512]{1,0:T(8,128)(2,1)}, u32[]{:S(2)}) copy-start(bf16[512,512]{1,0:T(8,128)(2,1)} %get-tuple-element.82) | copy-start | bytes 1572868
  494.5 6.9 %copy-start.2 = (bf16[512,512]{1,0:T(8,128)(2,1)S(1)}, bf16[512,512]{1,0:T(8,128)(2,1)}, u32[]{:S(2)}) copy-start(bf16[512,512]{1,0:T(8,128)(2,1)} %get-tuple-element.83) | copy-start | bytes 1572868

commit v6 on v5

--- a/solution.py
+++ b/solution.py
@@ -1182,10 +1182,14 @@
 def forward_kernel(
     tokens,
     cot_in,
-    vecs,
-    mixed_bias,
-    up_bias,
-    marks,
+    ln1_gain,
+    ln1_shift,
+    out_bias_in,
+    ln2_gain,
+    ln2_shift,
+    qv_bias,
+    up_bias_in,
+    spans,
     qkv_in,
     out_nat,
     up_nat,
@@ -1201,6 +1205,7 @@
     hid_out,
     slope_out,
     stats,
+    marks,
     vec_all,
     resid_own,
     std1_own,
@@ -1225,6 +1230,7 @@
     fx,
     qkv_raw,
     qkv_nat,
+    mixed_bias,
     local_sem,
     w_send,
     w_recv,
@@ -1304,7 +1310,10 @@
     block(tok, col, side, core, rows, width)[...] = tokens[...]
     gather = spread_steps(tok, rows, width, p_send, p_recv, 0)
     next(gather)
-    vec_all[:, strip(row * width, width)] = vecs[...]
+    here = strip(row * width, width)
+    vec_all[:, here] = jnp.zeros((vec_all.shape[0], width), f32)
+    for k, vector in enumerate((ln1_gain, ln1_shift, out_bias_in, ln2_gain, ln2_shift)):
+        vec_all[k : k + 1, here] = vector[...]
     vec_sends, vec_recvs = [], []
     for step in range(1, row_count):
         target, source = (row + step) % row_count, (row + row_count - step) % row_count
@@ -1327,6 +1336,11 @@
     next(gather, None)
     for copy in vec_recvs:
         copy.wait_recv()
+    lines = lax.broadcasted_iota(jnp.int32, marks.shape, 0) * SPAN
+    found = jnp.zeros(marks.shape, f32)
+    for k in range(spans.shape[1]):
+        found = jnp.where(lines == spans[0:1, k : k + 1] // SPAN * SPAN, 1.0, found)
+    marks[...] = found
 
     tile = 64
     gain1, shift1 = vec_all[0:1, :], vec_all[1:2, :]
@@ -1356,6 +1370,13 @@
     up_moves.start_far()
     qkv_moves.finish()
     local[0].wait()
+
+    mixed_bias[...] = jnp.zeros_like(mixed_bias)
+    for head in range(heads_width // HEAD):
+        for k in range(2):
+            lanes = pl.ds((head * 3 + 2 * k) * HEAD, HEAD)
+            mixed_bias[:, lanes] = qv_bias[row * (heads_width // HEAD) + head, k : k + 1, :]
+    up_bias = up_bias_in.at[:, strip(row * units, units)]
 
     def mixed_step(k, none):
         down, across = k // (per // CHUNK), k % (per // CHUNK)
@@ -1467,7 +1488,7 @@
         copy.wait_send()
 
 
-def forward_plane(cid, tokens, cot, vecs, mixed_bias, up_bias, marks, qkv_in, out_nat, up_nat):
+def forward_plane(cid, tokens, cot, vectors, qv_bias, up_bias, spans, qkv_in, out_nat, up_nat):
     f32, bf16 = jnp.float32, jnp.bfloat16
     rows, width = tokens.shape
     row_count = lax.axis_size("row")
@@ -1493,13 +1514,14 @@
             shape((length, units), bf16),
             shape((length, units), bf16),
             shape((length, 8), f32),
+            shape((8, 128), f32),
             shape((8, full), f32),
             shape((rows, width), f32),
             shape((rows, width), bf16),
             shape((rows, 1), f32),
         ],
-        in_specs=[near] * 6 + [away] * 3,
-        out_specs=[away] * 11 + [near] * 5,
+        in_specs=[near] * (5 + len(vectors)) + [away] * 3,
+        out_specs=[away] * 11 + [near] * 6,
         scratch_shapes=[
             vmem((length, full), bf16),
             vmem((length, full), bf16),
@@ -1521,6 +1543,7 @@
             vmem((2, rows, width), bf16),
             vmem(qkv_in.shape, bf16),
             vmem((width, row_count * per), bf16),
+            vmem((1, per), f32),
             dma((15,)),
             dma((moved,)),
             dma((moved,)),
@@ -1531,27 +1554,74 @@
             collective_id=cid, has_side_effects=True, vmem_limit_bytes=60 * 1024 * 1024
         ),
         cost_estimate=pl.CostEstimate(flops=10_000_000_000, bytes_accessed=60_000_000, transcendentals=4_000_000),
-    )(tokens, cot, vecs, mixed_bias, up_bias, marks, qkv_in, out_nat, up_nat)
-
-
-def head_order_kernel(flat, result):
-    for head in range(result.shape[2]):
+    )(tokens, cot, *[vector[None] for vector in vectors], qv_bias, up_bias[None], spans, qkv_in, out_nat, up_nat)
+
+
+def results_kernel(
+    down, up, out, output, tokens, qkv, small, down_result, up_result, out_result, output_result, tokens_result, qkv_result, *vectors
+):
+    *sums, up_bias, qv_bias = vectors
+    f32 = jnp.float32
+    down_result[...] = down[...].astype(f32)
+    up_result[...] = up[...].astype(f32)
+    out_result[...] = out[...].astype(f32)
+    output_result[...] = output[...]
+    tokens_result[...] = tokens[...]
+    for head in range(qkv_result.shape[2]):
         for kind in range(3):
             begin = (head * 3 + kind) * HEAD
-            result[:, kind, head, :] = flat[:, begin : begin + HEAD].astype(jnp.float32)
-
-
-def head_order(flat):
-    rows, heads = flat.shape[0], flat.shape[1] // (3 * HEAD)
-    tile = 128
-    result = pl.pallas_call(
-        head_order_kernel,
-        grid=(rows // tile,),
-        out_shape=jax.ShapeDtypeStruct((rows, 3, heads, HEAD), jnp.float32),
-        in_specs=[pl.BlockSpec((tile, flat.shape[1]), lambda k: (k, 0))],
-        out_specs=pl.BlockSpec((tile, 3, heads, HEAD), lambda k: (k, 0, 0, 0)),
-    )(flat)
-    return jnp.swapaxes(result, 1, 2)
+            qkv_result[:, kind, head, :] = qkv[:, begin : begin + HEAD].astype(f32)
+
+    @pl.when(pl.program_id(0) == 0)
+    def _():
+        row = lax.axis_index("row")
+        for k, result in enumerate(sums):
+            result[...] = small[row, k : k + 1, :]
+        count, _, width = small.shape
+        lines = up_bias.shape[1] // (count * width)
+        heads = qv_bias.shape[0] // count
+        for source in range(count):
+            for k in range(lines):
+                begin = (source * lines + k) * width
+                up_bias[:, begin : begin + width] = small[source, 8 + k : 9 + k, :]
+            for head in range(heads):
+                for k in range(2):
+                    begin = (head * 2 + k) * HEAD
+                    line = small[source, 8 + lines : 9 + lines, begin : begin + HEAD]
+                    qv_bias[source * heads + head, k : k + 1, :] = line
+
+
+def results(down, up, out, output, tokens, qkv, small):
+    f32 = jnp.float32
+    shape = jax.ShapeDtypeStruct
+    rows, heads = qkv.shape[0], qkv.shape[1] // (3 * HEAD)
+    width, units = small.shape[2], up.shape[1]
+    steps = 8
+
+    def cut(array):
+        return pl.BlockSpec((array.shape[0] // steps, array.shape[1]), lambda k: (k, 0))
+
+    def whole(*dims):
+        return pl.BlockSpec(dims, lambda k: (0,) * len(dims))
+
+    line = whole(1, width)
+    *made, up_bias, qv_bias = pl.pallas_call(
+        results_kernel,
+        grid=(steps,),
+        out_shape=[shape(a.shape, f32) for a in (down, up, out)]
+        + [shape(a.shape, a.dtype) for a in (output, tokens)]
+        + [shape((rows, 3, heads, HEAD), f32)]
+        + [shape((1, width), f32)] * 6
+        + [shape((1, units), f32), shape((heads, 2, HEAD), f32)],
+        in_specs=[cut(a) for a in (down, up, out, output, tokens, qkv)] + [whole(*small.shape)],
+        out_specs=[cut(a) for a in (down, up, out, output, tokens)]
+        + [pl.BlockSpec((rows // steps, 3, heads, HEAD), lambda k: (k, 0, 0, 0))]
+        + [line] * 6
+        + [whole(1, units), whole(heads, 2, HEAD)],
+        compiler_params=pltpu.CompilerParams(vmem_limit_bytes=63 * 1024 * 1024),
+    )(down, up, out, output, tokens, qkv, small)
+    made[5] = jnp.swapaxes(made[5], 1, 2)
+    return made[:6], [sums[0] for sums in made[6:]], up_bias[0], qv_bias
 
 
 def plane_plan(
@@ -1571,34 +1641,18 @@
     span_starts,
     cotangent,
 ):
-    f32 = jnp.float32
-    rows, width = tokens.shape
-    row_count = lax.axis_size("row")
-    row = lax.axis_index("row")
-    length = rows * lax.axis_size("col")
-    heads = qkv_weight.shape[1] // row_count
-    units = up_weight.shape[1] // row_count
-
-    blank = jnp.zeros_like(ln1_gain)
-    vecs = jnp.stack([ln1_gain, ln1_shift, out_bias, ln2_gain, ln2_shift, blank, blank, blank], axis=0)
-    own_qv = lax.dynamic_slice_in_dim(qv_bias, row * heads, heads, 0)
-    mixed_bias = jnp.stack([own_qv[:, 0], jnp.zeros_like(own_qv[:, 0]), own_qv[:, 1]], axis=1).reshape(1, -1)
-    own_up_bias = lax.dynamic_slice_in_dim(up_bias, row * units, units, 0)[None]
-    blocks = length // SPAN
-    marked = jnp.any(span_starts[0][:, None] // SPAN == jnp.arange(blocks, dtype=jnp.int32)[None, :], axis=0)
-    marks = jnp.broadcast_to(jnp.pad(marked.astype(f32), (0, -blocks % 8))[:, None], (blocks + -blocks % 8, 128))
-
+    width = tokens.shape[1]
     (
         cot_all, n1, n2, standard2, upw, qkvw, outw, mixed, attended, hidden, slope,
-        stats, vec_all, residual_own, standard1_own, inverse1_own,
+        stats, marks, vec_all, residual_own, standard1_own, inverse1_own,
     ) = forward_plane(
         1,
         tokens,
         cotangent,
-        vecs,
-        mixed_bias,
-        own_up_bias,
-        marks,
+        (ln1_gain, ln1_shift, out_bias, ln2_gain, ln2_shift),
+        qv_bias,
+        up_bias,
+        span_starts,
         jnp.swapaxes(qkv_weight, 1, 2),
         out_weight.reshape(-1, width),
         up_weight,
@@ -1607,23 +1661,25 @@
         2, hidden, cot_all, slope, n2, upw, standard2, n1, qkvw, down_weight, residual_own, attended, outw, mixed, standard1_own,
         stats, marks, vec_all, inverse1_own, down_bias[None],
     )
-    mine = lax.dynamic_index_in_dim(small, row, 0, keepdims=False)
-    spot = 8 + units // width
+    grads, sums, up_bias_grad, qv_bias_grad = results(
+        down_grad.reshape(-1, width), up_grad.reshape(width, -1), out_grad.reshape(-1, width), output, tokens_grad,
+        qkv_grad.reshape(width, -1), small
+    )
     return (
-        output,
-        tokens_grad,
-        mine[0],
-        mine[1],
-        head_order(qkv_grad.reshape(width, -1)),
-        small[:, spot, : 2 * heads * HEAD].reshape(row_count * heads, 2, HEAD),
-        out_grad.astype(f32).reshape(row_count * heads, HEAD, width),
-        mine[4],
-        mine[2],
-        mine[3],
-        up_grad.astype(f32).reshape(width, row_count * units),
-        small[:, 8:spot].reshape(-1),
-        down_grad.astype(f32).reshape(row_count * units, width),
-        mine[5],
+        grads[3],
+        grads[4],
+        sums[0],
+        sums[1],
+        grads[5],
+        qv_bias_grad,
+        grads[2].reshape(out_weight.shape),
+        sums[4],
+        sums[2],
+        sums[3],
+        grads[1],
+        up_bias_grad,
+        grads[0],
+        sums[5],
     )
 
 

time: 511 us -> 495 us (0.969)
  other arithmetic: 14.1 us -> 0 us
  local copies, waits for them, and re-layouts: 10.9 us -> 0 us
  Pallas kernels: 476 us -> 485 us
    reshape x3 -> x0, other arithmetic: 13.3 us -> none  [the longest x1 6.94 us: plane_plan(): down_grad.astype(f32).reshape(row_count * units, width)]
    pallas_call x1, Pallas kernels: 6.75 us -> 15.5 us  [results(): pl.pallas_call(results_kernel, grid=(steps,), out_shape=[shape(a.shape, f...]
where the time goes in v6:
time: 495 us; the launch traced here: 486 us
  Pallas kernels  485 us (98%)
    pallas_call x1, Pallas kernels, backward_plane(): pl.pallas_call(functools.partial(backward_kernel, counts), out_shape=[sha...  326 us
    pallas_call x1, Pallas kernels, forward_plane(): pl.pallas_call(forward_kernel, out_shape=[wide, wide, wide, wide, shape((...  144 us
    pallas_call x1, Pallas kernels, results(): pl.pallas_call(results_kernel, grid=(steps,), out_shape=[shape(a.shape, f...  15.5 us

profile of v6, /device:TPU:0, one launch (start us, length us, event | category | flops | bytes accessed | tf_op | source)
XLA Modules:
  0.0 486.4 jit_solution(17592906612384786229)
XLA Ops:
  0.7 144.1 %shard_map.254 = (bf16[1024,2048]{1,0:T(8,128)(2,1)}, bf16[1024,2048]{1,0:T(8,128)(2,1)}, bf16[1024,2048]{1,0:T(8,128)(2,1)}, bf16[1024,2048]{1,0:T(8,128)(2,1)}...) custom-call(bf16[512,512]{1,0:T(8,128)(2,1)} %tokens.1, ...), custom_call_target="tpu_custom_call" | custom-call | flops 10000000000 | bytes 60000000 | tf_op jit(solution)/shard_map/pallas_call | solution.py:1502
  144.8 325.7 %shard_map.255 = (bf16[16,256,512]{2,1,0:T(8,128)(2,1)}, bf16[2,256,4096]{2,1,0:T(8,128)(2,1)}, bf16[4,256,512]{2,1,0:T(8,128)(2,1)}, bf16[2,256,3072]{2,1,0:T(8...) custom-call(bf16[1024,1024]{1,0:T(8,128)(2,1)} %get-tuple-element.52, ...), custom_call_target="tpu_custom_call" | custom-call | flops 40000000000 | bytes 100000000 | tf_op jit(solution)/shard_map/pallas_call | solution.py:1063
  470.4 15.5 %shard_map.256 = (f32[4096,512]{1,0:T(8,128)}, f32[512,4096]{1,0:T(8,128)}, f32[1024,512]{1,0:T(8,128)}, bf16[512,512]{1,0:T(8,128)(2,1)}, bf16[512,512]{1,0:T(8...) custom-call(bf16[4096,512]{1,0:T(8,128)(2,1)} %bitcast.22, ...), custom_call_target="tpu_custom_call" | custom-call | tf_op jit(solution)/shard_map/pallas_call | solution.py:1608

commit v7 on v6

--- a/solution.py
+++ b/solution.py
@@ -411,7 +411,7 @@
     return lax.dot_general(left, right, (((0,), (0,)), ((), ())), preferred_element_type=jnp.float32)
 
 
-def tiled_nt(left, right, target, inner, tile_rows, tile_cols):
+def tiled_nt(left, right, target, inner, tile_rows, tile_cols, span=(0, 1, 1)):
     rows, cols = target.shape
     across = cols // tile_cols
 
@@ -421,10 +421,11 @@
         target[strip(down * tile_rows, tile_rows), strip(side * tile_cols, tile_cols)] = value.astype(target.dtype)
         return none
 
-    lax.fori_loop(0, (rows // tile_rows) * across, step, 0)
-
-
-def tiled_nn(left, right, target, tile_rows, tile_cols):
+    count = (rows // tile_rows) * across
+    lax.fori_loop(span[0] * count // span[2], span[1] * count // span[2], step, 0)
+
+
+def tiled_nn(left, right, target, tile_rows, tile_cols, span=(0, 1, 1)):
     rows, cols = target.shape
     across = cols // tile_cols
 
@@ -438,10 +439,11 @@
         target[strip(down * tile_rows, tile_rows), strip(side * tile_cols, tile_cols)] = value.astype(target.dtype)
         return none
 
-    lax.fori_loop(0, (rows // tile_rows) * across, step, 0)
-
-
-def reduce_steps(part, result, got, diag, half_x, half_y, to_send, from_xy, sends, recvs, base):
+    count = (rows // tile_rows) * across
+    lax.fori_loop(span[0] * count // span[2], span[1] * count // span[2], step, 0)
+
+
+def reduce_steps(part, result, got, diag, half_x, half_y, to_send, from_xy, sends, recvs, base, mostly_x=False):
     f32 = jnp.float32
     rows, width = result.shape
     half = rows // 2
@@ -457,34 +459,50 @@
         copy.start()
     mine = [block(part, a, b, core, rows, width) for a, b in spots]
     dx = put(diag.at[low], half_x, sends, recvs, base + 4, to_x)
-    dy = put(diag.at[high], half_y, sends, recvs, base + 5, to_y)
-    cy = put(to_send.at[0], from_xy.at[0], sends, recvs, base + 6, to_y)
-    cx = put(to_send.at[1], from_xy.at[1], sends, recvs, base + 7, to_x)
+    dy = put(diag.at[high], half_y, sends, recvs, base + 5, to_x if mostly_x else to_y)
+
+    def onward(k, span, at, partner):
+        return put(to_send.at[k, span], from_xy.at[k, span], sends, recvs, base + at, partner)
+
+    y_high, x_low = onward(0, high, 6, to_y), onward(1, low, 7, to_x)
+    y_low, x_high = onward(0, low, 8, to_y), onward(1, high, 9, to_x)
+
+    def pair(k, span):
+        return mine[k][span].astype(f32) + got[k, span].astype(f32)
+
     yield
     copies[0].wait_recv()
     diag[...] = (mine[0][...].astype(f32) + got[0].astype(f32)).astype(diag.dtype)
     dx.start()
     dy.start()
     copies[1].wait_recv()
+    if not mostly_x:
+        to_send[0, high] = pair(1, high).astype(diag.dtype)
+        y_high.start()
     copies[2].wait_recv()
-    to_send[0, high] = (mine[1][high].astype(f32) + got[1, high].astype(f32)).astype(diag.dtype)
-    to_send[1, low] = (mine[2][low].astype(f32) + got[2, low].astype(f32)).astype(diag.dtype)
+    to_send[1, low] = pair(2, low).astype(diag.dtype)
+    x_low.start()
+    if mostly_x:
+        to_send[1, high] = pair(2, high).astype(diag.dtype)
+        x_high.start()
     copies[3].wait_recv()
-    result[...] = mine[3][...].astype(f32) + got[3].astype(f32)
     yield
     dx.wait_recv()
-    to_send[0, low] = (mine[1][low].astype(f32) + got[1, low].astype(f32) + half_x[...].astype(f32)).astype(diag.dtype)
-    cy.start()
+    to_send[0, low] = (pair(1, low) + half_x[...].astype(f32)).astype(diag.dtype)
+    y_low.start()
     dy.wait_recv()
-    to_send[1, high] = (mine[2][high].astype(f32) + got[2, high].astype(f32) + half_y[...].astype(f32)).astype(
-        diag.dtype
-    )
-    cx.start()
+    if mostly_x:
+        to_send[0, high] = (pair(1, high) + half_y[...].astype(f32)).astype(diag.dtype)
+        y_high.start()
+    else:
+        to_send[1, high] = (pair(2, high) + half_y[...].astype(f32)).astype(diag.dtype)
+        x_high.start()
     yield
-    cy.wait_recv()
-    cx.wait_recv()
-    result[...] = result[...] + from_xy[0].astype(f32) + from_xy[1].astype(f32)
-    for copy in copies + [dx, dy, cy, cx]:
+    for copy in (y_high, x_low, y_low, x_high):
+        copy.wait_recv()
+    near = mine[3][...].astype(f32) + got[3].astype(f32)
+    result[...] = near + from_xy[0].astype(f32) + from_xy[1].astype(f32)
+    for copy in copies + [dx, dy, y_high, x_low, y_low, x_high]:
         copy.wait_send()
 
 
@@ -498,39 +516,44 @@
 
     own, ox, oy, od = (col, side, core), (1 - col, side, core), (col, 1 - side, core), (1 - col, 1 - side, core)
     plan = [
-        copy_of(0, own, to_x),
-        copy_of(1, own, to_y),
-        copy_of(2, own, to_core),
-        None if mostly_x else copy_of(3, ox, to_y, 0),
-        copy_of(4, oy, to_x, None if mostly_x else 1),
-        copy_of(5, ox, to_core),
-        copy_of(6, oy, to_core),
-        copy_of(7, od, to_core),
+        copy_of(0, own, to_x, 0),
+        copy_of(1, own, to_y, 1),
+        copy_of(2, own, to_x, 1),
+        copy_of(3, own, to_y, 0),
+        copy_of(4, own, to_core),
+        copy_of(5, oy, to_x, 0) if mostly_x else copy_of(5, ox, to_y, 0),
+        copy_of(6, oy, to_x, 1),
+        copy_of(7, ox, to_core),
+        copy_of(8, oy, to_core),
+        copy_of(9, od, to_core),
     ]
-    for at in (0, 1, 2):
+    for at in range(5):
         plan[at].start()
     yield
-    used = [at for at in range(8) if at != 3 or not mostly_x]
     plan[0].wait_recv()
     if not mostly_x:
-        plan[3].start()
+        plan[5].start()
     plan[1].wait_recv()
-    plan[4].start()
-    plan[5].start()
     plan[6].start()
+    plan[2].wait_recv()
+    plan[7].start()
+    plan[3].wait_recv()
+    plan[8].start()
+    if mostly_x:
+        plan[5].start()
     yield
-    if not mostly_x:
-        plan[3].wait_recv()
-    plan[4].wait_recv()
-    plan[7].start()
+    plan[5].wait_recv()
+    plan[6].wait_recv()
+    plan[9].start()
     yield
-    for at in (2, 5, 6, 7):
+    for at in (4, 7, 8, 9):
         plan[at].wait_recv()
-    for at in used:
-        plan[at].wait_send()
+    for copy in plan:
+        copy.wait_send()
 
 
 CHUNK = 256
+LINES = CHUNK // 2
 
 
 def backward_kernel(
@@ -661,32 +684,32 @@
         target, source = (row + step) % row_count, (row + row_count - step) % row_count
         here, there = downw_land.at[:, strip(row * width, width)], downw_land.at[:, strip(source * width, width)]
         piece = down_nat.at[strip(target * units, units), :]
-        down_sends.append(put(piece, here, p_send, p_recv, 32 + step - 1, {"row": target}))
-        down_recvs.append(put(piece, there, p_send, p_recv, 32 + step - 1, {"row": source}))
+        down_sends.append(put(piece, here, p_send, p_recv, 40 + step - 1, {"row": target}))
+        down_recvs.append(put(piece, there, p_send, p_recv, 40 + step - 1, {"row": source}))
         down_sends[-1].start()
     down_own = pltpu.make_async_copy(
-        down_nat.at[strip(row * units, units), :], downw_land.at[:, strip(row * width, width)], own_sem.at[2 * total]
+        down_nat.at[strip(row * units, units), :], downw_land.at[:, strip(row * width, width)], own_sem.at[4 * total]
     )
     down_own.start()
 
     def place(u, source):
-        i, half = u // 2, u % 2
+        i, half, quarter = u // 4, u // 2 % 2, pl.ds(u % 2 * LINES, LINES)
         if i < n_down:
-            return down_out.at[source * n_down + i // 2 * 2 + half, :, pl.ds(i % 2 * CHUNK, CHUNK)]
+            return down_out.at[source * n_down + i // 2 * 2 + half, quarter, pl.ds(i % 2 * CHUNK, CHUNK)]
         i -= n_down
         if i < n_up:
-            return up_out.at[half, :, strip(source * n_up * CHUNK + i * CHUNK, CHUNK)]
+            return up_out.at[half, quarter, strip(source * n_up * CHUNK + i * CHUNK, CHUNK)]
         i -= n_up
         if i < n_out:
-            return out_out.at[source * n_out + i, :, pl.ds(half * CHUNK, CHUNK)]
+            return out_out.at[source * n_out + i, quarter, pl.ds(half * CHUNK, CHUNK)]
         i -= n_out
-        return qkv_out.at[half, :, strip(source * n_qkv * CHUNK + i * CHUNK, CHUNK)]
+        return qkv_out.at[half, quarter, strip(source * n_qkv * CHUNK + i * CHUNK, CHUNK)]
 
     g_slots, s_slots, t_slots, r_slots, m_slots = g.shape[0], s.shape[0], t.shape[0], r_land.shape[0], m_land.shape[0]
-    pieces = 2 * total
+    pieces = 4 * total
 
     def made(u):
-        return g.at[u // 2 % g_slots, :, u % 2]
+        return g.at[u // 4 % g_slots, :, u // 2 % 2, pl.ds(u % 2 * LINES, LINES)]
 
     def inward(u):
         return put(made(u), r_land.at[u % r_slots], z_send, z_recv, u, to_inner)
@@ -719,8 +742,8 @@
 
             @pl.when(outer)
             def _():
-                inward(2 * (i - g_slots)).wait_send()
-                inward(2 * (i - g_slots) + 1).wait_send()
+                for k in range(4):
+                    inward(4 * (i - g_slots) + k).wait_send()
 
         slot = g.at[i % g_slots]
         if i < n_down:
@@ -791,39 +814,35 @@
             outward(u).wait_recv()
             send_home(u, b_land.at[u])
 
-    def turn(u):
+    ahead = 4
+
+    def pass_on(u):
         middle(u)
-        if u >= 1:
-            finish_inner(u - 1)
-        if u + 2 < pieces:
-            if u % 2 == 0:
-                produce((u + 2) // 2)
-            launch(u + 2)
         if u >= 2:
-            finish_outer(u - 2)
+            finish_inner(u - 2)
+        if u + ahead < pieces:
+            if u % 4 == 0:
+                produce((u + ahead) // 4)
+            launch(u + ahead)
+        if u >= 3:
+            finish_outer(u - 3)
 
     set_a = (got_a, diag_a, hx_a, hy_a, ts_a, fx_a)
     set_b = (got_b, diag_b, hx_b, hy_b, ts_b, fx_b)
     gain2 = vec_all[3:4, :]
-
-    loads[0].wait()
-    loads[1].wait()
-    produce(0)
-    launch(0)
-    launch(1)
-    sums[...] = jnp.zeros_like(sums)
-    turn(0)
-    turn(1)
-    turn(2)
-    down_own.wait()
-    for copy in down_recvs:
-        copy.wait_recv()
-    loads[9].start()
-    loads[2].wait()
-    loads[3].wait()
-    loads[4].wait()
-    turn(3)
-    loads[9].wait()
+    heads = mixed.shape[1] // (3 * HEAD)
+    here = strip(row * width, width)
+    tile = 64
+    first = reduce_steps(part, own_sum, *set_a, p_send, p_recv, 0, mostly_x=True)
+    second = spread_steps(tot, rows, width, p_send, p_recv, 10, mostly_x=True)
+    third = reduce_steps(cot, own_sum, *set_b, p_send, p_recv, 20, mostly_x=True)
+    fourth = reduce_steps(tot, own_sum, *set_a, p_send, p_recv, 30, mostly_x=True)
+
+    def down_here():
+        down_own.wait()
+        for copy in down_recvs:
+            copy.wait_recv()
+        loads[9].start()
 
     def upper_step(k, none):
         down, across_ = k // (units // CHUNK), k % (units // CHUNK)
@@ -831,31 +850,23 @@
         dup[at, lanes] = (dot_nt(cot[at, :], tot[lanes, :]) * dup[at, lanes].astype(f32)).astype(bf16)
         return none
 
-    lax.fori_loop(0, (length // rows) * (units // CHUNK), upper_step, 0)
-    turn(4)
-    tiled_nt(dup, upw, part, dup.shape[1], 1024, 256)
-    loads[6].start()
-    first = reduce_steps(part, own_sum, *set_a, p_send, p_recv, 0)
-    next(first)
-    turn(5)
-    next(first)
-    turn(6)
-    next(first)
-    turn(7)
-    for k in (5, 11, 12, 13, 14):
-        loads[k].wait()
-    next(first, None)
-    block(tot, col, side, core, rows, width)[...] = own_sum[...].astype(bf16)
-    second = spread_steps(tot, rows, width, p_send, p_recv, 8)
-    next(second)
-    turn(8)
-    next(second)
-    turn(9)
-    next(second)
-    turn(10)
-    next(second, None)
-
-    tile = 64
+    def uppers(part_of):
+        if part_of == 0:
+            for k in (2, 3, 4, 9):
+                loads[k].wait()
+        count = (length // rows) * (units // CHUNK) // 2
+        lax.fori_loop(part_of * count, (part_of + 1) * count, upper_step, 0)
+
+    def d_normed2(part_of):
+        tiled_nt(dup, upw, part, units, 1024, 256, (part_of, part_of + 1, 2))
+        if part_of == 1:
+            loads[6].start()
+            next(first)
+
+    def gather_start():
+        next(first, None)
+        block(tot, col, side, core, rows, width)[...] = own_sum[...].astype(bf16)
+        next(second)
 
     def norm_step(k, none):
         at = strip(k * tile, tile)
@@ -873,7 +884,6 @@
 
         @pl.when(k // (rows // tile) == col)
         def _():
-            here = strip(row * width, width)
             own = tot[at, here].astype(f32) * vec_all[3:4, here]
             dres_own[strip(k % (rows // tile) * tile, tile), :] = cot[at, here].astype(f32) + inverse * (
                 own - mean_one - std[at, here].astype(f32) * mean_two
@@ -881,138 +891,187 @@
 
         return none
 
-    lax.fori_loop(0, length // tile, norm_step, 0)
-    loads[7].start()
-    tiled_nt(part, outw, d_att, full, 512, 256)
-
-    heads = mixed.shape[1] // (3 * HEAD)
+    def norm_back(part_of):
+        if part_of == 0:
+            for k in (5, 11, 12, 13, 14):
+                loads[k].wait()
+        count = length // tile // 2
+        lax.fori_loop(part_of * count, (part_of + 1) * count, norm_step, 0)
+        if part_of == 1:
+            loads[7].start()
+
+    def d_attended():
+        tiled_nt(part, outw, d_att, full, 512, 256)
+
     factor = 1.0 / math.sqrt(HEAD)
     blocks = length // SPAN
     spots = (SPAN, SPAN)
     earlier = lax.broadcasted_iota(jnp.int32, spots, 1) <= lax.broadcasted_iota(jnp.int32, spots, 0)
 
-    def head_step(head, none):
+    def attention_back(head, begin, end):
         base = head * 3 * HEAD
-        at_q, at_k, at_v = strip(base, HEAD), strip(base + HEAD, HEAD), strip(base + 2 * HEAD, HEAD)
-        at_o = strip(head * HEAD, HEAD)
-        dk_acc[...] = jnp.zeros_like(dk_acc)
-        dv_acc[...] = jnp.zeros_like(dv_acc)
-        for k in range(blocks):
-            here = pl.ds(k * SPAN, SPAN)
+        at_q, at_k, at_v = pl.ds(base, HEAD), pl.ds(base + HEAD, HEAD), pl.ds(base + 2 * HEAD, HEAD)
+        at_o = pl.ds(head * HEAD, HEAD)
+        if begin == 0:
+            dk_acc[...] = jnp.zeros_like(dk_acc)
+            dv_acc[...] = jnp.zeros_like(dv_acc)
+        for k in range(begin, end):
+            now = pl.ds(k * SPAN, SPAN)
             seen = (k + 1) * SPAN
-            query, dout = mixed[here, at_q], d_att[here, at_o]
+            query, dout = mixed[now, at_q], d_att[now, at_o]
             keys, values = mixed[:seen, at_k], mixed[:seen, at_v]
             scores = dot_nt(query, keys) * factor
             last = jnp.where(earlier | (marks[k : k + 1, :1] > 0), scores[:, seen - SPAN :], masked_score)
             scores = last if k == 0 else jnp.concatenate([scores[:, : seen - SPAN], last], axis=1)
-            probs = jnp.exp(scores - stats[here, 1 + head : 2 + head])
+            probs = jnp.exp(scores - stats[now, 1 + head : 2 + head])
             d_probs = dot_nt(dout, values)
             dots = jnp.sum(probs * d_probs, axis=1, keepdims=True)
             d_scores = (probs * (d_probs - dots)).astype(bf16)
-            d_mix[here, at_q] = (jnp.dot(d_scores, keys, preferred_element_type=f32) * factor).astype(bf16)
+            d_mix[now, at_q] = (jnp.dot(d_scores, keys, preferred_element_type=f32) * factor).astype(bf16)
             dk_acc[:seen] += dot_tn(d_scores, query)
             dv_acc[:seen] += dot_tn(probs.astype(bf16), dout)
-        d_mix[:, at_k] = (dk_acc[...] * factor).astype(bf16)
-        d_mix[:, at_v] = dv_acc[...].astype(bf16)
-        return none
-
-    for head in range(heads):
-        head_step(head, 0)
-        turn(11 + head)
-    loads[6].wait()
-    tiled_nt(d_mix, upw, cot, d_mix.shape[1], 1024, 256)
-    third = reduce_steps(cot, own_sum, *set_b, p_send, p_recv, 16)
-    next(third)
-    turn(11 + heads)
-    next(third)
-    loads[8].start()
-    turn(12 + heads)
-    next(third)
-    loads[7].wait()
-    turn(13 + heads)
-    next(third, None)
-
-    grad1, gain1 = own_sum, vec_all[0:1, strip(row * width, width)]
-    scaled1 = grad1[...] * gain1
-    first_sum = jnp.sum(scaled1, axis=1, keepdims=True)
-    second_sum = jnp.sum(scaled1 * std1_own[...].astype(f32), axis=1, keepdims=True)
-    lane = lax.broadcasted_iota(jnp.int32, (rows, 128), 1)
-    pair = jnp.where(lane == 0, first_sum, jnp.where(lane == 1, second_sum, 0.0))
-    stat_land[row] = pair.T[:8]
-    stat_sends, stat_recvs = [], []
+        if end == blocks:
+            d_mix[:, at_k] = (dk_acc[...] * factor).astype(bf16)
+            d_mix[:, at_v] = dv_acc[...].astype(bf16)
+
+    def d_normed1(part_of):
+        if part_of == 0:
+            loads[6].wait()
+        tiled_nt(d_mix, upw, cot, d_mix.shape[1], 1024, 256, (part_of, part_of + 1, 2))
+        if part_of == 1:
+            next(third)
+
+    def output_sums(part_of):
+        if part_of == 0:
+            loads[8].wait()
+        tiled_nn(hid, n2, tot, 1024, 256, (part_of, part_of + 1, 2))
+        if part_of == 1:
+            next(fourth)
+
+    grad1 = own_sum
+    stat_sends, stat_recvs, dp_sends, dp_recvs, row_sends, row_recvs = [], [], [], [], [], []
     for step in range(1, row_count):
         target, source = (row + step) % row_count, (row + row_count - step) % row_count
-        stat_sends.append(put(stat_land.at[row], stat_land.at[row], p_send, p_recv, 35 + step - 1, {"row": target}))
-        stat_recvs.append(
-            put(stat_land.at[source], stat_land.at[source], p_send, p_recv, 35 + step - 1, {"row": source})
-        )
-        stat_sends[-1].start()
-    small[...] = jnp.zeros_like(small)
-    here = strip(row * width, width)
-    small[0:1, :] = jnp.sum(grad1[...] * std1_own[...].astype(f32), axis=0, keepdims=True)
-    small[1:2, :] = jnp.sum(grad1[...], axis=0, keepdims=True)
-    small[2:6, :] = sums[0:4, here]
-    uppers = jnp.sum(dup[...].astype(f32), axis=0, keepdims=True)
-    for k in range(units // width):
-        small[8 + k : 9 + k, :] = uppers[:, k * width : (k + 1) * width]
-    mixes = jnp.sum(d_mix[...].astype(f32), axis=0, keepdims=True)
-    spot = 8 + units // width
-    picked = [mixes[:, (head * 3 + kind) * HEAD : (head * 3 + kind + 1) * HEAD] for head in range(heads) for kind in (0, 2)]
-    small[spot : spot + 1, : 2 * heads * HEAD] = jnp.concatenate(picked, axis=1)
-    to_x = partners()[0]
-    x_copy = put(small.at[pl.ds(0, 8)], x_land, p_send, p_recv, 38, to_x)
-    x_copy.start()
-    turn(14 + heads)
-    x_copy.wait_recv()
-    x_copy.wait_send()
-    small[0:2, :] += x_land[0:2, :]
-    dp_sends, dp_recvs = [], []
-    dp_land[plane] = small[...]
+        to, since = {"row": target}, {"row": source}
+        stat_sends.append(put(stat_land.at[row], stat_land.at[row], p_send, p_recv, 43 + step - 1, to))
+        stat_recvs.append(put(stat_land.at[source], stat_land.at[source], p_send, p_recv, 43 + step - 1, since))
+        row_sends.append(put(small_out.at[row], small_out.at[row], p_send, p_recv, 50 + step - 1, to))
+        row_recvs.append(put(small_out.at[source], small_out.at[source], p_send, p_recv, 50 + step - 1, since))
     for step in range(1, dp_count):
         target, source = (plane + step) % dp_count, (plane + dp_count - step) % dp_count
-        dp_sends.append(put(dp_land.at[plane], dp_land.at[plane], p_send, p_recv, 39 + step - 1, {"dp": target}))
-        dp_recvs.append(put(dp_land.at[source], dp_land.at[source], p_send, p_recv, 39 + step - 1, {"dp": source}))
-        dp_sends[-1].start()
-    for copy in stat_recvs:
-        copy.wait_recv()
-    both = stat_land[0]
-    for k in range(1, row_count):
-        both = both + stat_land[k]
-    both = jnp.concatenate([both, jnp.zeros((120, rows), f32)], axis=0).T
-    d_norm1 = inv1_own[...] * (
-        scaled1 - both[:, 0:1] / full - std1_own[...].astype(f32) * (both[:, 1:2] / full)
-    )
-    tokens_block[...] = (dres_own[...] + d_norm1).astype(bf16)
-    loads[10].start()
-    loads[8].wait()
-    tiled_nn(hid, n2, tot, 1024, 256)
-    fourth = reduce_steps(tot, own_sum, *set_a, p_send, p_recv, 24)
-    next(fourth)
-    turn(15 + heads)
-    next(fourth)
-    turn(16 + heads)
-    next(fourth)
-    turn(17 + heads)
-    next(fourth, None)
-    loads[10].wait()
-    out_block[...] = (dres_own[...] + (own_sum[...] + down_bias[...])).astype(bf16)
-    for copy in dp_recvs:
-        copy.wait_recv()
-    together = dp_land[0]
-    for k in range(1, dp_count):
-        together = together + dp_land[k]
-    small_out[row] = together
-    row_sends, row_recvs = [], []
-    for step in range(1, row_count):
-        target, source = (row + step) % row_count, (row + row_count - step) % row_count
-        row_sends.append(put(small_out.at[row], small_out.at[row], p_send, p_recv, 42 + step - 1, {"row": target}))
-        row_recvs.append(
-            put(small_out.at[source], small_out.at[source], p_send, p_recv, 42 + step - 1, {"row": source})
+        dp_sends.append(put(dp_land.at[plane], dp_land.at[plane], p_send, p_recv, 47 + step - 1, {"dp": target}))
+        dp_recvs.append(put(dp_land.at[source], dp_land.at[source], p_send, p_recv, 47 + step - 1, {"dp": source}))
+    x_copy = put(small.at[pl.ds(0, 8)], x_land, p_send, p_recv, 46, partners()[0])
+
+    def row_stats():
+        next(third, None)
+        scaled = grad1[...] * vec_all[0:1, here]
+        first_sum = jnp.sum(scaled, axis=1, keepdims=True)
+        second_sum = jnp.sum(scaled * std1_own[...].astype(f32), axis=1, keepdims=True)
+        lane = lax.broadcasted_iota(jnp.int32, (rows, 128), 1)
+        pair = jnp.where(lane == 0, first_sum, jnp.where(lane == 1, second_sum, 0.0))
+        stat_land[row] = pair.T[:8]
+        for copy in stat_sends:
+            copy.start()
+
+    def small_sums():
+        small[...] = jnp.zeros_like(small)
+        small[0:1, :] = jnp.sum(grad1[...] * std1_own[...].astype(f32), axis=0, keepdims=True)
+        small[1:2, :] = jnp.sum(grad1[...], axis=0, keepdims=True)
+        small[2:6, :] = sums[0:4, here]
+        totals = jnp.sum(dup[...].astype(f32), axis=0, keepdims=True)
+        for k in range(units // width):
+            small[8 + k : 9 + k, :] = totals[:, k * width : (k + 1) * width]
+        mixes = jnp.sum(d_mix[...].astype(f32), axis=0, keepdims=True)
+        spot = 8 + units // width
+        picked = [
+            mixes[:, (head * 3 + kind) * HEAD : (head * 3 + kind + 1) * HEAD] for head in range(heads) for kind in (0, 2)
+        ]
+        small[spot : spot + 1, : 2 * heads * HEAD] = jnp.concatenate(picked, axis=1)
+        x_copy.start()
+
+    def tokens_out():
+        for copy in stat_recvs:
+            copy.wait_recv()
+        both = stat_land[0]
+        for k in range(1, row_count):
+            both = both + stat_land[k]
+        both = jnp.concatenate([both, jnp.zeros((120, rows), f32)], axis=0).T
+        scaled = grad1[...] * vec_all[0:1, here]
+        d_norm1 = inv1_own[...] * (
+            scaled - both[:, 0:1] / full - std1_own[...].astype(f32) * (both[:, 1:2] / full)
         )
-        row_sends[-1].start()
-    for u in range(18 + heads, pieces):
-        turn(u)
+        tokens_block[...] = (dres_own[...] + d_norm1).astype(bf16)
+        loads[10].start()
+
+    def dp_start():
+        x_copy.wait_recv()
+        x_copy.wait_send()
+        small[0:2, :] += x_land[0:2, :]
+        dp_land[plane] = small[...]
+        for copy in dp_sends:
+            copy.start()
+
+    def output_out():
+        next(fourth, None)
+        loads[10].wait()
+        out_block[...] = (dres_own[...] + (own_sum[...] + down_bias[...])).astype(bf16)
+
+    def rows_start():
+        for copy in dp_recvs:
+            copy.wait_recv()
+        together = dp_land[0]
+        for k in range(1, dp_count):
+            together = together + dp_land[k]
+        small_out[row] = together
+        for copy in row_sends:
+            copy.start()
+
+    tasks = {
+        6: [down_here],
+        8: [lambda: uppers(0)],
+        9: [lambda: uppers(1)],
+        10: [lambda: d_normed2(0)],
+        11: [lambda: d_normed2(1)],
+        13: [lambda: next(first)],
+        16: [lambda: next(first)],
+        19: [gather_start],
+        22: [lambda: next(second)],
+        24: [lambda: next(second)],
+        25: [lambda: next(second, None), loads[8].start],
+        26: [lambda: norm_back(0)],
+        27: [lambda: norm_back(1)],
+        28: [d_attended],
+        29: [lambda: attention_back(0, 0, blocks)],
+        30: [lambda: attention_back(1, 0, blocks)],
+        31: [lambda: output_sums(0), loads[7].wait],
+        32: [lambda: d_normed1(0)],
+        33: [lambda: d_normed1(1)],
+        34: [lambda: next(third)],
+        35: [lambda: output_sums(1)],
+        36: [lambda: next(fourth)],
+        37: [lambda: next(third)],
+        39: [lambda: next(fourth)],
+        40: [row_stats],
+        41: [small_sums],
+        42: [tokens_out],
+        43: [dp_start],
+        44: [output_out],
+        45: [rows_start],
+    }
+    sums[...] = jnp.zeros_like(sums)
+    loads[0].wait()
+    loads[1].wait()
+    produce(0)
+    for k in range(ahead):
+        launch(k)
+    for u in range(pieces):
+        pass_on(u)
+        for task in tasks.get(u, ()):
+            task()
+    finish_inner(pieces - 2)
     finish_inner(pieces - 1)
+    finish_outer(pieces - 3)
     finish_outer(pieces - 2)
     finish_outer(pieces - 1)
     for copy in row_recvs:
@@ -1022,7 +1081,7 @@
 
     @pl.when(outer)
     def _():
-        for u in range(pieces - 2 * g_slots, pieces):
+        for u in range(pieces - 4 * g_slots, pieces):
             inward(u).wait_send()
         for u in range(pieces):
             sent_home(u, b_land.at[u])
@@ -1048,7 +1107,7 @@
     row_count, dp_count = full // width, lax.axis_size("dp")
     counts = (slope.shape[1] // CHUNK, slope.shape[1] // CHUNK, attended.shape[1] // CHUNK, mixed.shape[1] // CHUNK)
     total = sum(counts)
-    unit = (row_count, CHUNK, CHUNK)
+    unit = (row_count, LINES, CHUNK)
     shape = jax.ShapeDtypeStruct
     away, near = pl.BlockSpec(memory_space=pl.ANY), pl.BlockSpec(memory_space=pltpu.VMEM)
     vmem, dma = pltpu.VMEM, pltpu.SemaphoreType.DMA
@@ -1067,7 +1126,7 @@
             shape((2, CHUNK, row_count * counts[1] * CHUNK), bf16),
             shape((row_count * counts[2], CHUNK, width), bf16),
             shape((2, CHUNK, row_count * counts[3] * CHUNK), bf16),
-            shape((2 * total,) + unit, bf16),
+            shape((4 * total,) + unit, bf16),
             shape((hid.shape[1], full), bf16),
             shape((rows, width), bf16),
             shape((rows, width), bf16),
@@ -1093,10 +1152,10 @@
             vmem((length, HEAD), f32),
             vmem((length, HEAD), f32),
             vmem((2, row_count, width // CHUNK, CHUNK, CHUNK), bf16),
-            vmem((2,) + unit, bf16),
-            vmem((2,) + unit, bf16),
             vmem((3,) + unit, bf16),
             vmem((4,) + unit, bf16),
+            vmem((6,) + unit, bf16),
+            vmem((6,) + unit, bf16),
         ]
         + sets
         + sets
@@ -1110,13 +1169,13 @@
             vmem((row_count, 8, rows), f32),
             dma((15,)),
             pltpu.SemaphoreType.REGULAR,
-            dma((2 * total + 1,)),
-            dma((6 * total,)),
-            dma((6 * total,)),
-            dma((6 * total,)),
-            dma((6 * total,)),
-            dma((45,)),
-            dma((45,)),
+            dma((4 * total + 1,)),
+            dma((12 * total,)),
+            dma((12 * total,)),
+            dma((12 * total,)),
+            dma((12 * total,)),
+            dma((53,)),
+            dma((53,)),
         ],
         compiler_params=pltpu.CompilerParams(
             collective_id=cid, has_side_effects=True, vmem_limit_bytes=64 * 1024 * 1024 - 65536
@@ -1318,8 +1377,8 @@
     for step in range(1, row_count):
         target, source = (row + step) % row_count, (row + row_count - step) % row_count
         here, there = vec_all.at[:, strip(row * width, width)], vec_all.at[:, strip(source * width, width)]
-        vec_sends.append(put(here, here, p_send, p_recv, 8 + step - 1, {"row": target}))
-        vec_recvs.append(put(there, there, p_send, p_recv, 8 + step - 1, {"row": source}))
+        vec_sends.append(put(here, here, p_send, p_recv, 10 + step - 1, {"row": target}))
+        vec_recvs.append(put(there, there, p_send, p_recv, 10 + step - 1, {"row": source}))
         vec_sends[-1].start()
     out_moves.sibling.start()
     up_moves.sibling.start()
@@ -1422,19 +1481,19 @@
     local[1].wait()
     tiled_nn(attended, outw, part, rows, 512)
     local[9].start()
-    add_up = reduce_steps(part, own_sum, got, diag, hx, hy, ts, fx, p_send, p_recv, 11)
+    add_up = reduce_steps(part, own_sum, got, diag, hx, hy, ts, fx, p_send, p_recv, 13)
     next(add_up)
     next(add_up)
     up_moves.forward(4, 8)
     next(add_up)
     next(add_up, None)
     block(tot, col, side, core, rows, width)[...] = own_sum[...].astype(bf16)
-    again = spread_steps(tot, rows, width, p_send, p_recv, 19)
+    again = spread_steps(tot, rows, width, p_send, p_recv, 23)
     for k in range(3):
         next(again)
     next(again, None)
     local[3].wait()
-    cot_gather = spread_steps(cot_all, rows, width, p_send, p_recv, 27)
+    cot_gather = spread_steps(cot_all, rows, width, p_send, p_recv, 33)
     next(cot_gather)
 
     gain2, shift2, out_bias = vec_all[3:4, :], vec_all[4:5, :], vec_all[2:3, :]
@@ -1547,8 +1606,8 @@
             dma((15,)),
             dma((moved,)),
             dma((moved,)),
-            dma((35,)),
-            dma((35,)),
+            dma((43,)),
+            dma((43,)),
         ],
         compiler_params=pltpu.CompilerParams(
             collective_id=cid, has_side_effects=True, vmem_limit_bytes=60 * 1024 * 1024

time: 495 us -> 484 us (0.978)
  Pallas kernels: 485 us -> 475 us
    pallas_call x1, Pallas kernels: 326 us -> 317 us  [backward_plane(): pl.pallas_call(functools.partial(backward_kernel, counts), out_shape=[sha...]
where the time goes in v7:
time: 484 us; the launch traced here: 476 us
  Pallas kernels  475 us (98%)
    pallas_call x1, Pallas kernels, backward_plane(): pl.pallas_call(functools.partial(backward_kernel, counts), out_shape=[sha...  317 us
    pallas_call x1, Pallas kernels, forward_plane(): pl.pallas_call(forward_kernel, out_shape=[wide, wide, wide, wide, shape((...  142 us
    pallas_call x1, Pallas kernels, results(): pl.pallas_call(results_kernel, grid=(steps,), out_shape=[shape(a.shape, f...  15.5 us

profile of v7, /device:TPU:0, one launch (start us, length us, event | category | flops | bytes accessed | tf_op | source)
XLA Modules:
  0.0 475.6 jit_solution(11233578001981707645)
XLA Ops:
  0.7 142.1 %shard_map.254 = (bf16[1024,2048]{1,0:T(8,128)(2,1)}, bf16[1024,2048]{1,0:T(8,128)(2,1)}, bf16[1024,2048]{1,0:T(8,128)(2,1)}, bf16[1024,2048]{1,0:T(8,128)(2,1)}...) custom-call(bf16[512,512]{1,0:T(8,128)(2,1)} %tokens.1, ...), custom_call_target="tpu_custom_call" | custom-call | flops 10000000000 | bytes 60000000 | tf_op jit(solution)/shard_map/pallas_call | solution.py:1561
  142.8 316.9 %shard_map.255 = (bf16[16,256,512]{2,1,0:T(8,128)(2,1)}, bf16[2,256,4096]{2,1,0:T(8,128)(2,1)}, bf16[4,256,512]{2,1,0:T(8,128)(2,1)}, bf16[2,256,3072]{2,1,0:T(8...) custom-call(bf16[1024,1024]{1,0:T(8,128)(2,1)} %get-tuple-element.52, ...), custom_call_target="tpu_custom_call" | custom-call | flops 40000000000 | bytes 100000000 | tf_op jit(solution)/shard_map/pallas_call | solution.py:1122
  459.7 15.5 %shard_map.256 = (f32[4096,512]{1,0:T(8,128)}, f32[512,4096]{1,0:T(8,128)}, f32[1024,512]{1,0:T(8,128)}, bf16[512,512]{1,0:T(8,128)(2,1)}, bf16[512,512]{1,0:T(8...) custom-call(bf16[4096,512]{1,0:T(8,128)(2,1)} %bitcast.22, ...), custom_call_target="tpu_custom_call" | custom-call | tf_op jit(solution)/shard_map/pallas_call | solution.py:1667

commit v8 on v7

--- a/solution.py
+++ b/solution.py
@@ -1235,7 +1235,7 @@
             copy.wait_send()
 
 
-FAR_PARTS = 4
+FAR_PARTS = 8
 
 
 def forward_kernel(
@@ -1367,7 +1367,7 @@
         local[k].start()
 
     block(tok, col, side, core, rows, width)[...] = tokens[...]
-    gather = spread_steps(tok, rows, width, p_send, p_recv, 0)
+    gather = spread_steps(tok, rows, width, p_send, p_recv, 0, mostly_x=True)
     next(gather)
     here = strip(row * width, width)
     vec_all[:, here] = jnp.zeros((vec_all.shape[0], width), f32)
@@ -1389,8 +1389,8 @@
             qkv_nat[:, pl.ds((head * 3 + kind) * HEAD, HEAD)] = flat[:, head * HEAD : (head + 1) * HEAD]
     local[0].start()
     qkv_moves.sibling.start()
+    qkv_moves.start_far()
     next(gather)
-    qkv_moves.start_far()
     next(gather)
     next(gather, None)
     for copy in vec_recvs:
@@ -1420,11 +1420,12 @@
         return none
 
     half_steps = length // tile // 2
-    lax.fori_loop(0, half_steps, norm1_step, 0)
-    qkv_moves.forward(0, 2)
-    lax.fori_loop(half_steps, 2 * half_steps, norm1_step, 0)
+    quarter = half_steps // 2
+    for k in range(4):
+        qkv_moves.forward(2 * k, 2 * k + 1)
+        lax.fori_loop(k * quarter, (k + 1) * quarter, norm1_step, 0)
+        qkv_moves.forward(2 * k + 1, 2 * k + 2)
     local[4].start()
-    qkv_moves.forward(2, 4)
     out_moves.start_far()
     up_moves.start_far()
     qkv_moves.finish()
@@ -1489,12 +1490,13 @@
     next(add_up, None)
     block(tot, col, side, core, rows, width)[...] = own_sum[...].astype(bf16)
     again = spread_steps(tot, rows, width, p_send, p_recv, 23)
-    for k in range(3):
-        next(again)
-    next(again, None)
+    next(again)
+    next(again)
     local[3].wait()
     cot_gather = spread_steps(cot_all, rows, width, p_send, p_recv, 33)
     next(cot_gather)
+    next(again)
+    next(again, None)
 
     gain2, shift2, out_bias = vec_all[3:4, :], vec_all[4:5, :], vec_all[2:3, :]
 

time: 484 us -> 474 us (0.979)
  Pallas kernels: 475 us -> 464 us
    pallas_call x1, Pallas kernels: 142 us -> 132 us  [forward_plane(): pl.pallas_call(forward_kernel, out_shape=[wide, wide, wide, wide, shape((...]
where the time goes in v8:
time: 474 us; the launch traced here: 466 us
  Pallas kernels  464 us (98%)
    pallas_call x1, Pallas kernels, backward_plane(): pl.pallas_call(functools.partial(backward_kernel, counts), out_shape=[sha...  317 us
    pallas_call x1, Pallas kernels, forward_plane(): pl.pallas_call(forward_kernel, out_shape=[wide, wide, wide, wide, shape((...  132 us
    pallas_call x1, Pallas kernels, results(): pl.pallas_call(results_kernel, grid=(steps,), out_shape=[shape(a.shape, f...  15.5 us

profile of v8, /device:TPU:0, one launch (start us, length us, event | category | flops | bytes accessed | tf_op | source)
XLA Modules:
  0.0 465.5 jit_solution(10546041921153358390)
XLA Ops:
  0.7 132.4 %shard_map.254 = (bf16[1024,2048]{1,0:T(8,128)(2,1)}, bf16[1024,2048]{1,0:T(8,128)(2,1)}, bf16[1024,2048]{1,0:T(8,128)(2,1)}, bf16[1024,2048]{1,0:T(8,128)(2,1)}...) custom-call(bf16[512,512]{1,0:T(8,128)(2,1)} %tokens.1, ...), custom_call_target="tpu_custom_call" | custom-call | flops 10000000000 | bytes 60000000 | tf_op jit(solution)/shard_map/pallas_call | solution.py:1563
  133.0 316.5 %shard_map.255 = (bf16[16,256,512]{2,1,0:T(8,128)(2,1)}, bf16[2,256,4096]{2,1,0:T(8,128)(2,1)}, bf16[4,256,512]{2,1,0:T(8,128)(2,1)}, bf16[2,256,3072]{2,1,0:T(8...) custom-call(bf16[1024,1024]{1,0:T(8,128)(2,1)} %get-tuple-element.52, ...), custom_call_target="tpu_custom_call" | custom-call | flops 40000000000 | bytes 100000000 | tf_op jit(solution)/shard_map/pallas_call | solution.py:1122
  449.6 15.5 %shard_map.256 = (f32[4096,512]{1,0:T(8,128)}, f32[512,4096]{1,0:T(8,128)}, f32[1024,512]{1,0:T(8,128)}, bf16[512,512]{1,0:T(8,128)(2,1)}, bf16[512,512]{1,0:T(8...) custom-call(bf16[4096,512]{1,0:T(8,128)(2,1)} %bitcast.22, ...), custom_call_target="tpu_custom_call" | custom-call | tf_op jit(solution)/shard_map/pallas_call | solution.py:1669

commit v9 on v8

--- a/solution.py
+++ b/solution.py
@@ -1475,8 +1475,9 @@
 
     for head in range(heads):
         head_step(head, 0)
+        if head == 0:
+            out_moves.forward()
     local[11].start()
-    out_moves.forward()
     up_moves.forward(0, 4)
     out_moves.finish()
     local[1].wait()
@@ -1485,8 +1486,8 @@
     add_up = reduce_steps(part, own_sum, got, diag, hx, hy, ts, fx, p_send, p_recv, 13)
     next(add_up)
     next(add_up)
+    next(add_up)
     up_moves.forward(4, 8)
-    next(add_up)
     next(add_up, None)
     block(tot, col, side, core, rows, width)[...] = own_sum[...].astype(bf16)
     again = spread_steps(tot, rows, width, p_send, p_recv, 23)

time: 474 us -> 472 us (level)
  no operation moved by 1% of the time
where the time goes in v9:
time: 472 us; the launch traced here: 463 us
  Pallas kernels  462 us (98%)
    pallas_call x1, Pallas kernels, backward_plane(): pl.pallas_call(functools.partial(backward_kernel, counts), out_shape=[sha...  316 us
    pallas_call x1, Pallas kernels, forward_plane(): pl.pallas_call(forward_kernel, out_shape=[wide, wide, wide, wide, shape((...  131 us
    pallas_call x1, Pallas kernels, results(): pl.pallas_call(results_kernel, grid=(steps,), out_shape=[shape(a.shape, f...  15.5 us

profile of v9, /device:TPU:0, one launch (start us, length us, event | category | flops | bytes accessed | tf_op | source)
XLA Modules:
  0.0 463.3 jit_solution(17284389937349442720)
XLA Ops:
  0.7 130.6 %shard_map.254 = (bf16[1024,2048]{1,0:T(8,128)(2,1)}, bf16[1024,2048]{1,0:T(8,128)(2,1)}, bf16[1024,2048]{1,0:T(8,128)(2,1)}, bf16[1024,2048]{1,0:T(8,128)(2,1)}...) custom-call(bf16[512,512]{1,0:T(8,128)(2,1)} %tokens.1, ...), custom_call_target="tpu_custom_call" | custom-call | flops 10000000000 | bytes 60000000 | tf_op jit(solution)/shard_map/pallas_call | solution.py:1564
  131.2 316.1 %shard_map.255 = (bf16[16,256,512]{2,1,0:T(8,128)(2,1)}, bf16[2,256,4096]{2,1,0:T(8,128)(2,1)}, bf16[4,256,512]{2,1,0:T(8,128)(2,1)}, bf16[2,256,3072]{2,1,0:T(8...) custom-call(bf16[1024,1024]{1,0:T(8,128)(2,1)} %get-tuple-element.52, ...), custom_call_target="tpu_custom_call" | custom-call | flops 40000000000 | bytes 100000000 | tf_op jit(solution)/shard_map/pallas_call | solution.py:1122
  447.4 15.5 %shard_map.256 = (f32[4096,512]{1,0:T(8,128)}, f32[512,4096]{1,0:T(8,128)}, f32[1024,512]{1,0:T(8,128)}, bf16[512,512]{1,0:T(8,128)(2,1)}, bf16[512,512]{1,0:T(8...) custom-call(bf16[4096,512]{1,0:T(8,128)(2,1)} %bitcast.22, ...), custom_call_target="tpu_custom_call" | custom-call | tf_op jit(solution)/shard_map/pallas_call | solution.py:1670

commit v10 on v9

--- a/solution.py
+++ b/solution.py
@@ -1042,12 +1042,12 @@
         26: [lambda: norm_back(0)],
         27: [lambda: norm_back(1)],
         28: [d_attended],
-        29: [lambda: attention_back(0, 0, blocks)],
-        30: [lambda: attention_back(1, 0, blocks)],
-        31: [lambda: output_sums(0), loads[7].wait],
+        29: [lambda: attention_back(0, 0, blocks - 1)],
+        30: [lambda: attention_back(0, blocks - 1, blocks), lambda: attention_back(1, 0, blocks // 2)],
+        31: [lambda: attention_back(1, blocks // 2, blocks), loads[7].wait],
         32: [lambda: d_normed1(0)],
         33: [lambda: d_normed1(1)],
-        34: [lambda: next(third)],
+        34: [lambda: next(third), lambda: output_sums(0)],
         35: [lambda: output_sums(1)],
         36: [lambda: next(fourth)],
         37: [lambda: next(third)],

time: 472 us -> 472 us (level)
  no operation moved by 1% of the time
where the time goes in v10:
time: 472 us; the launch traced here: 463 us
  Pallas kernels  462 us (98%)
    pallas_call x1, Pallas kernels, backward_plane(): pl.pallas_call(functools.partial(backward_kernel, counts), out_shape=[sha...  316 us
    pallas_call x1, Pallas kernels, forward_plane(): pl.pallas_call(forward_kernel, out_shape=[wide, wide, wide, wide, shape((...  131 us
    pallas_call x1, Pallas kernels, results(): pl.pallas_call(results_kernel, grid=(steps,), out_shape=[shape(a.shape, f...  15.5 us

profile of v10, /device:TPU:0, one launch (start us, length us, event | category | flops | bytes accessed | tf_op | source)
XLA Modules:
  0.0 463.3 jit_solution(7271433388860338226)
XLA Ops:
  0.7 130.6 %shard_map.254 = (bf16[1024,2048]{1,0:T(8,128)(2,1)}, bf16[1024,2048]{1,0:T(8,128)(2,1)}, bf16[1024,2048]{1,0:T(8,128)(2,1)}, bf16[1024,2048]{1,0:T(8,128)(2,1)}...) custom-call(bf16[512,512]{1,0:T(8,128)(2,1)} %tokens.1, ...), custom_call_target="tpu_custom_call" | custom-call | flops 10000000000 | bytes 60000000 | tf_op jit(solution)/shard_map/pallas_call | solution.py:1564
  131.2 316.1 %shard_map.255 = (bf16[16,256,512]{2,1,0:T(8,128)(2,1)}, bf16[2,256,4096]{2,1,0:T(8,128)(2,1)}, bf16[4,256,512]{2,1,0:T(8,128)(2,1)}, bf16[2,256,3072]{2,1,0:T(8...) custom-call(bf16[1024,1024]{1,0:T(8,128)(2,1)} %get-tuple-element.52, ...), custom_call_target="tpu_custom_call" | custom-call | flops 40000000000 | bytes 100000000 | tf_op jit(solution)/shard_map/pallas_call | solution.py:1122
  447.3 15.5 %shard_map.256 = (f32[4096,512]{1,0:T(8,128)}, f32[512,4096]{1,0:T(8,128)}, f32[1024,512]{1,0:T(8,128)}, bf16[512,512]{1,0:T(8,128)(2,1)}, bf16[512,512]{1,0:T(8...) custom-call(bf16[4096,512]{1,0:T(8,128)(2,1)} %bitcast.22, ...), custom_call_target="tpu_custom_call" | custom-call | tf_op jit(solution)/shard_map/pallas_call | solution.py:1670

commit v11 on v9

--- a/solution.py
+++ b/solution.py
@@ -1477,8 +1477,9 @@
         head_step(head, 0)
         if head == 0:
             out_moves.forward()
+            up_moves.forward(0, 2)
     local[11].start()
-    up_moves.forward(0, 4)
+    up_moves.forward(2, 4)
     out_moves.finish()
     local[1].wait()
     tiled_nn(attended, outw, part, rows, 512)

time: 472 us -> 472 us (level)
  no operation moved by 1% of the time
where the time goes in v11:
time: 472 us; the launch traced here: 463 us
  Pallas kernels  462 us (98%)
    pallas_call x1, Pallas kernels, backward_plane(): pl.pallas_call(functools.partial(backward_kernel, counts), out_shape=[sha...  316 us
    pallas_call x1, Pallas kernels, forward_plane(): pl.pallas_call(forward_kernel, out_shape=[wide, wide, wide, wide, shape((...  131 us
    pallas_call x1, Pallas kernels, results(): pl.pallas_call(results_kernel, grid=(steps,), out_shape=[shape(a.shape, f...  15.5 us

profile of v11, /device:TPU:0, one launch (start us, length us, event | category | flops | bytes accessed | tf_op | source)
XLA Modules:
  0.0 463.3 jit_solution(2037151924616963825)
XLA Ops:
  0.7 130.6 %shard_map.254 = (bf16[1024,2048]{1,0:T(8,128)(2,1)}, bf16[1024,2048]{1,0:T(8,128)(2,1)}, bf16[1024,2048]{1,0:T(8,128)(2,1)}, bf16[1024,2048]{1,0:T(8,128)(2,1)}...) custom-call(bf16[512,512]{1,0:T(8,128)(2,1)} %tokens.1, ...), custom_call_target="tpu_custom_call" | custom-call | flops 10000000000 | bytes 60000000 | tf_op jit(solution)/shard_map/pallas_call | solution.py:1565
  131.2 316.1 %shard_map.255 = (bf16[16,256,512]{2,1,0:T(8,128)(2,1)}, bf16[2,256,4096]{2,1,0:T(8,128)(2,1)}, bf16[4,256,512]{2,1,0:T(8,128)(2,1)}, bf16[2,256,3072]{2,1,0:T(8...) custom-call(bf16[1024,1024]{1,0:T(8,128)(2,1)} %get-tuple-element.52, ...), custom_call_target="tpu_custom_call" | custom-call | flops 40000000000 | bytes 100000000 | tf_op jit(solution)/shard_map/pallas_call | solution.py:1122
  447.4 15.5 %shard_map.256 = (f32[4096,512]{1,0:T(8,128)}, f32[512,4096]{1,0:T(8,128)}, f32[1024,512]{1,0:T(8,128)}, bf16[512,512]{1,0:T(8,128)(2,1)}, bf16[512,512]{1,0:T(8...) custom-call(bf16[4096,512]{1,0:T(8,128)(2,1)} %bitcast.22, ...), custom_call_target="tpu_custom_call" | custom-call | tf_op jit(solution)/shard_map/pallas_call | solution.py:1671
